TPU v7x, 32 devices: a whole 2x2x4 slice. The times are simulated.
32 devices in a mesh: dp: 16 (over z, y, core), mp: 2 (over x).
Axes of the slice: x: 2, y: 2, z: 4, core: 2. Of those that a mesh axis runs over, the one named last changes fastest.
Arguments:
- activations: bfloat16 [2, 16384, 512], P(None, 'dp'), may hold values from -6 to 6
- cotangent: bfloat16 [2, 16384, 512], P(None, 'dp'), may hold values from -6 to 6
- w_qkv: bfloat16 [3, 512, 512], P(None, 'dp', 'mp'), may hold values from -0.25 to 0.25
- w_o: bfloat16 [512, 512], P('mp', 'dp'), may hold values from -0.75 to 0.75
- w_up: bfloat16 [512, 2048], P('dp', 'mp'), may hold values from -0.25 to 0.25
- w_down: bfloat16 [2048, 512], P('mp', 'dp'), may hold values from -0.125 to 0.125
- b_qv: bfloat16 [2, 8, 64], P(None, 'mp', 'dp'), may hold values from -3 to 3
- b_up: bfloat16 [32, 64], P('mp', 'dp'), may hold values from -3 to 3
- out_bias: bfloat16 [2, 512], P(None, 'dp'), may hold values from -3 to 3
- norm_gain: bfloat16 [2, 512], P(None, 'dp'), may hold values from 0.25 to 1.75
- norm_bias: bfloat16 [2, 512], P(None, 'dp'), may hold values from -2 to 2
- chain_ids: int32 [2, 16384], P(None, 'dp'), may hold values from -1 to 1023, as said below
- key_keep: int32 [2, 16384], P(None, 'dp'), may hold values 0 or 1
Outputs:
- output: float32 [2, 16384, 512], P(None, 'dp')
- grad_x: float32 [2, 16384, 512], P(None, 'dp')
- grad_w_qkv: float32 [3, 512, 512], P(None, 'dp', 'mp')
- grad_w_o: float32 [512, 512], P('mp', 'dp')
- grad_w_up: float32 [512, 2048], P('dp', 'mp')
- grad_w_down: float32 [2048, 512], P('mp', 'dp')
- grad_b_qv: float32 [2, 8, 64], P(None, 'mp', 'dp')
- grad_b_up: float32 [32, 64], P('mp', 'dp')
- grad_out_bias: float32 [2, 512], P(None, 'dp')
- grad_norm_gain: float32 [2, 512], P(None, 'dp')
- grad_norm_bias: float32 [2, 512], P(None, 'dp')
Inputs may be any that keep to these rules, and one draw needn't show every extreme that they name: `chain_ids`: in each aligned block of 1024 slots along the last dimension, a live slot carries the index within the block of the first slot of its chain, chains are contiguous runs of live slots, the first slot of every block is live, and padding slots (-1) come after all live slots of their block; how many slots are live differs from block to block.
All inputs are finite; a program needn't handle non-finite values. No bound on the sum of `key_keep` on one device may be relied on, other than what follows from the above.
Results may differ from a plain program's by a relative error of at most 0.018.
Values may be sent and summed in bfloat16 or wider, within the bound.
A program may use at most 192 MiB of HBM per device.

v0:
```python
import math

import jax
import jax.numpy as jnp
from jax import lax
from jax.sharding import PartitionSpec as P

epsilon = 1e-05
masked_value = -1e30


def product(left, right):
    return jnp.dot(left, right, preferred_element_type=jnp.float32)


def normalize(values, scale_row, shift_row):
    row_mean = jnp.mean(values, axis=-1, keepdims=True)
    centred = values - row_mean
    inverse = lax.rsqrt(jnp.mean(centred * centred, axis=-1, keepdims=True) + epsilon)
    scaled = centred * inverse
    return (scaled * scale_row + shift_row, scaled, inverse)


def normalize_back(grad_rows, scaled, inverse, scale_row):
    inner = grad_rows * scale_row
    return inverse * (
        inner
        - jnp.mean(inner, axis=-1, keepdims=True)
        - scaled * jnp.mean(inner * scaled, axis=-1, keepdims=True)
    )


def gelu_slope(values):
    normal_cdf = 0.5 * (1.0 + lax.erf(values * 0.7071067811865476))
    density = jnp.exp(-0.5 * values * values) * 0.3989422804014327
    return normal_cdf + values * density


def permitted(chain_rows, keep_rows):
    slot_count = chain_rows.shape[0]
    same_chain = chain_rows[:, None] == chain_rows[None, :]
    diagonal = lax.broadcasted_iota(jnp.int32, (slot_count, slot_count), 0) == lax.broadcasted_iota(
        jnp.int32, (slot_count, slot_count), 1
    )
    return same_chain & ((keep_rows[None, :] == 1) | diagonal)


def head_scores(query, key_rows, allowed, head_count, head_width):
    query_heads = query.reshape(-1, head_count, head_width)
    key_heads = key_rows.reshape(-1, head_count, head_width)
    scores = jnp.einsum(
        "qhd,khd->hqk", query_heads, key_heads, preferred_element_type=jnp.float32
    ) * (1.0 / math.sqrt(head_width))
    return jnp.where(allowed[None], scores, masked_value)


def forward(rows_in, chain_rows, keep_rows, weights):
    qkv_full, out_full, up_full, down_full, bias_qv, bias_up, bias_out, gain_full, shift_full = (
        weights
    )
    head_count = bias_qv.shape[1]
    head_width = bias_qv.shape[2]
    row_count = rows_in.shape[0]
    bias_qv = bias_qv.astype(jnp.float32)
    bias_out = bias_out.astype(jnp.float32)
    gain_full = gain_full.astype(jnp.float32)
    shift_full = shift_full.astype(jnp.float32)
    allowed = permitted(chain_rows, keep_rows)
    normed_one, scaled_one, inverse_one = normalize(rows_in, gain_full[0], shift_full[0])
    hidden_one = normed_one.astype(jnp.bfloat16)
    query = (product(hidden_one, qkv_full[0]) + bias_qv[0].reshape(-1)).astype(jnp.bfloat16)
    key_rows = product(hidden_one, qkv_full[1]).astype(jnp.bfloat16)
    value_rows = (product(hidden_one, qkv_full[2]) + bias_qv[1].reshape(-1)).astype(jnp.bfloat16)
    scores = head_scores(query, key_rows, allowed, head_count, head_width)
    row_top = jnp.max(scores, axis=-1, keepdims=True)
    log_total = jnp.log(jnp.sum(jnp.exp(scores - row_top), axis=-1, keepdims=True)) + row_top
    probs_low = jnp.exp(scores - log_total).astype(jnp.bfloat16)
    mixed = jnp.einsum(
        "hqk,khd->qhd",
        probs_low,
        value_rows.reshape(row_count, head_count, head_width),
        preferred_element_type=jnp.float32,
    )
    mixed = mixed.reshape(row_count, -1).astype(jnp.bfloat16)
    partial_attn = product(mixed, out_full)
    resid = rows_in + lax.psum(partial_attn, "mp") + bias_out[0]
    normed_two, scaled_two, inverse_two = normalize(resid, gain_full[1], shift_full[1])
    hidden_two = normed_two.astype(jnp.bfloat16)
    pre = product(hidden_two, up_full) + bias_up.astype(jnp.float32).reshape(-1)
    act = jax.nn.gelu(pre, approximate=False).astype(jnp.bfloat16)
    partial_ffn = product(act, down_full)
    result = (
        resid + lax.psum(partial_ffn.astype(jnp.bfloat16), "mp").astype(jnp.float32) + bias_out[1]
    )
    kept = (
        allowed,
        scaled_one,
        inverse_one,
        hidden_one,
        query,
        key_rows,
        value_rows,
        log_total,
        mixed,
        scaled_two,
        inverse_two,
        hidden_two,
        pre,
        act,
    )
    return (result, kept)


def backward(grad_out, result, kept, weights):
    qkv_full, out_full, up_full, down_full, bias_qv, bias_up, bias_out, gain_full, shift_full = (
        weights
    )
    (
        allowed,
        scaled_one,
        inverse_one,
        hidden_one,
        query,
        key_rows,
        value_rows,
        log_total,
        mixed,
        scaled_two,
        inverse_two,
        hidden_two,
        pre,
        act,
    ) = kept
    head_count = bias_qv.shape[1]
    head_width = bias_qv.shape[2]
    row_count = grad_out.shape[0]
    gain_full = gain_full.astype(jnp.float32)
    grad_low = grad_out.astype(jnp.bfloat16)
    grad_down = product(act.T, grad_low)
    grad_pre = (product(grad_low, down_full.T) * gelu_slope(pre)).astype(jnp.bfloat16)
    grad_bup = jnp.sum(grad_pre, axis=0, dtype=jnp.float32).reshape(bias_up.shape)
    grad_up = product(hidden_two.T, grad_pre)
    partial_two = product(grad_pre, up_full.T)
    grad_two = lax.psum(partial_two.astype(jnp.bfloat16), "mp").astype(jnp.float32)
    gain_two = jnp.sum(grad_two * scaled_two, axis=0)
    shift_two = jnp.sum(grad_two, axis=0)
    grad_resid = grad_out + normalize_back(grad_two, scaled_two, inverse_two, gain_full[1])
    resid_low = grad_resid.astype(jnp.bfloat16)
    grad_out_proj = product(mixed.T, resid_low)
    grad_mixed = (
        product(resid_low, out_full.T)
        .astype(jnp.bfloat16)
        .reshape(row_count, head_count, head_width)
    )
    scores = head_scores(query, key_rows, allowed, head_count, head_width)
    probs = jnp.exp(scores - log_total)
    probs_low = probs.astype(jnp.bfloat16)
    value_heads = value_rows.reshape(row_count, head_count, head_width)
    grad_value = jnp.einsum(
        "hqk,qhd->khd", probs_low, grad_mixed, preferred_element_type=jnp.float32
    ).astype(jnp.bfloat16)
    grad_probs = jnp.einsum(
        "qhd,khd->hqk", grad_mixed, value_heads, preferred_element_type=jnp.float32
    )
    grad_scores = (
        probs * (grad_probs - jnp.sum(grad_probs * probs, axis=-1, keepdims=True))
    ).astype(jnp.bfloat16)
    score_scale = 1.0 / math.sqrt(head_width)
    key_heads = key_rows.reshape(row_count, head_count, head_width)
    query_heads = query.reshape(row_count, head_count, head_width)
    grad_query = (
        jnp.einsum("hqk,khd->qhd", grad_scores, key_heads, preferred_element_type=jnp.float32)
        * score_scale
    ).astype(jnp.bfloat16)
    grad_key = (
        jnp.einsum("hqk,qhd->khd", grad_scores, query_heads, preferred_element_type=jnp.float32)
        * score_scale
    ).astype(jnp.bfloat16)
    stacked = jnp.stack(
        [
            grad_query.reshape(row_count, -1),
            grad_key.reshape(row_count, -1),
            grad_value.reshape(row_count, -1),
        ]
    )
    grad_qkv = jnp.einsum("rd,crk->cdk", hidden_one, stacked, preferred_element_type=jnp.float32)
    partial_one = jnp.einsum("crk,cdk->rd", stacked, qkv_full, preferred_element_type=jnp.float32)
    grad_one = lax.psum(partial_one.astype(jnp.bfloat16), "mp").astype(jnp.float32)
    grad_bqv = jnp.stack(
        [
            jnp.sum(stacked[0], axis=0, dtype=jnp.float32),
            jnp.sum(stacked[2], axis=0, dtype=jnp.float32),
        ]
    ).reshape(2, head_count, head_width)
    gain_one = jnp.sum(grad_one * scaled_one, axis=0)
    shift_one = jnp.sum(grad_one, axis=0)
    grad_in = grad_resid + normalize_back(grad_one, scaled_one, inverse_one, gain_full[0])
    small_sums = jnp.stack(
        [
            jnp.sum(grad_resid, axis=0),
            jnp.sum(grad_out, axis=0),
            gain_one,
            gain_two,
            shift_one,
            shift_two,
        ]
    )
    local_grads = (
        grad_qkv,
        grad_out_proj,
        grad_up,
        grad_down,
        grad_bqv,
        grad_bup,
        small_sums[0:2],
        small_sums[2:4],
        small_sums[4:6],
    )
    return (result, grad_in, local_grads)


def body(
    activations,
    cotangent,
    w_qkv,
    w_o,
    w_up,
    w_down,
    b_qv,
    b_up,
    out_bias,
    norm_gain,
    norm_bias,
    chain_ids,
    key_keep,
):
    batch_count = activations.shape[0]
    outputs = []
    input_grads = []
    running = None
    for batch_index in range(batch_count):
        weights = (
            lax.all_gather(w_qkv, "dp", axis=1, tiled=True),
            lax.all_gather(w_o, "dp", axis=1, tiled=True),
            lax.all_gather(w_up, "dp", axis=0, tiled=True),
            lax.all_gather(w_down, "dp", axis=1, tiled=True),
            lax.all_gather(b_qv, "dp", axis=2, tiled=True),
            lax.all_gather(b_up, "dp", axis=1, tiled=True),
            lax.all_gather(out_bias, "dp", axis=1, tiled=True),
            lax.all_gather(norm_gain, "dp", axis=1, tiled=True),
            lax.all_gather(norm_bias, "dp", axis=1, tiled=True),
        )
        result, kept = forward(
            activations[batch_index].astype(jnp.float32),
            chain_ids[batch_index],
            key_keep[batch_index],
            weights,
        )
        live_rows = (chain_ids[batch_index] >= 0).astype(jnp.float32)[:, None]
        output_rows, grad_in, local_grads = backward(
            cotangent[batch_index].astype(jnp.float32) * live_rows, result, kept, weights
        )
        outputs.append(output_rows)
        input_grads.append(grad_in)
        shares = (
            lax.psum_scatter(
                local_grads[0].astype(jnp.bfloat16), "dp", scatter_dimension=1, tiled=True
            ).astype(jnp.float32),
            lax.psum_scatter(
                local_grads[1].astype(jnp.bfloat16), "dp", scatter_dimension=1, tiled=True
            ).astype(jnp.float32),
            lax.psum_scatter(
                local_grads[2].astype(jnp.bfloat16), "dp", scatter_dimension=0, tiled=True
            ).astype(jnp.float32),
            lax.psum_scatter(
                local_grads[3].astype(jnp.bfloat16), "dp", scatter_dimension=1, tiled=True
            ).astype(jnp.float32),
            lax.psum_scatter(
                local_grads[4].astype(jnp.bfloat16), "dp", scatter_dimension=2, tiled=True
            ).astype(jnp.float32),
            lax.psum_scatter(
                local_grads[5].astype(jnp.bfloat16), "dp", scatter_dimension=1, tiled=True
            ).astype(jnp.float32),
            lax.psum_scatter(
                local_grads[6].astype(jnp.bfloat16), "dp", scatter_dimension=1, tiled=True
            ).astype(jnp.float32),
            lax.psum_scatter(
                local_grads[7].astype(jnp.bfloat16), "dp", scatter_dimension=1, tiled=True
            ).astype(jnp.float32),
            lax.psum_scatter(
                local_grads[8].astype(jnp.bfloat16), "dp", scatter_dimension=1, tiled=True
            ).astype(jnp.float32),
        )
        if running is None:
            running = tuple(shares)
        else:
            running = tuple(jax.tree.map(jnp.add, tuple(running), tuple(shares)))
    return (
        jnp.stack(outputs),
        jnp.stack(input_grads),
        running[0],
        running[1],
        running[2],
        running[3],
        running[4],
        running[5],
        running[6],
        running[7],
        running[8],
    )


def solution(mesh):
    placed = (
        P(None, "dp", None),
        P(None, "dp", None),
        P(None, "dp", "mp"),
        P("mp", "dp"),
        P("dp", "mp"),
        P("mp", "dp"),
        P(None, "mp", "dp"),
        P("mp", "dp"),
        P(None, "dp"),
        P(None, "dp"),
        P(None, "dp"),
        P(None, "dp"),
        P(None, "dp"),
    )
    return jax.shard_map(
        body,
        mesh=mesh,
        in_specs=placed,
        out_specs=(
            P(None, "dp", None),
            P(None, "dp", None),
            P(None, "dp", "mp"),
            P("mp", "dp"),
            P("dp", "mp"),
            P("mp", "dp"),
            P(None, "mp", "dp"),
            P("mp", "dp"),
            P(None, "dp"),
            P(None, "dp"),
            P(None, "dp"),
        ),
        check_vma=False,
    )
```

profile of v0, /device:TPU:0, one launch (start us, length us, event | category | flops | bytes accessed | tf_op | source)
XLA Modules:
  0.0 1243.1 jit_solution(9962415222344937010)
XLA Ops:
  9.0 23.3 %all-gather = bf16[16,32,2]{1,2,0:T(2,128)(2,1)S(1)} all-gather(bf16[1,32,2]{1,2,0:T(2,128)(2,1)} %bitcast.362), channel_id=1, replica_groups=mesh['dp'=16,'mp'=2] {'dp'}, dimensions={0}, use_global_device_ids=true | all-gather | bytes 2176 | tf_op jit(solution)/shard_map/all_gather | solution.py:250
  32.4 17.6 %all-gather.1 = bf16[16,32,2]{1,2,0:T(2,128)(2,1)S(1)} all-gather(bf16[1,32,2]{1,2,0:T(2,128)(2,1)} %bitcast.363), channel_id=1, replica_groups=mesh['dp'=16,'mp'=2] {'dp'}, dimensions={0}, use_global_device_ids=true | all-gather | bytes 2176 | tf_op jit(solution)/shard_map/all_gather | solution.py:251
  54.5 18.8 %all_gather.39 = bf16[2,4,64]{1,0,2:T(2,128)(2,1)S(1)} all-gather(bf16[2,4,4]{1,0,2:T(2,128)(2,1)S(1)} %copy.117), channel_id=1, replica_groups=mesh['dp'=16,'mp'=2] {'dp'}, dimensions={2}, use_global_device_ids=true | all-gather | bytes 1088 | tf_op jit(solution)/shard_map/all_gather | solution.py:247
  73.7 19.6 %all_gather.38 = bf16[3,512,256]{2,1,0:T(8,128)(2,1)S(1)} all-gather(bf16[3,32,256]{2,1,0:T(8,128)(2,1)S(1)} %copy-done.61), channel_id=1, replica_groups=mesh['dp'=16,'mp'=2] {'dp'}, dimensions={1}, use_global_device_ids=true | all-gather | bytes 835584 | tf_op jit(solution)/shard_map/all_gather | solution.py:243
  99.8 19.8 %all_gather.40 = bf16[256,512]{0,1:T(8,128)(2,1)S(1)} all-gather(bf16[256,32]{0,1:T(8,128)(2,1)S(1)} %copy-done.64), channel_id=1, replica_groups=mesh['dp'=16,'mp'=2] {'dp'}, dimensions={1}, use_global_device_ids=true | all-gather | bytes 278528 | tf_op jit(solution)/shard_map/all_gather | solution.py:244
  138.2 10.3 convolution_convert_fusion.14
  158.8 17.4 %all-gather.2 = bf16[16,32,2]{1,2,0:T(2,128)(2,1)S(1)} all-gather(bf16[1,32,2]{1,2,0:T(2,128)(2,1)S(1)} %bitcast.364), channel_id=1, replica_groups=mesh['dp'=16,'mp'=2] {'dp'}, dimensions={0}, use_global_device_ids=true | all-gather | bytes 2176 | tf_op jit(solution)/shard_map/all_gather | solution.py:249
  176.9 19.3 %all-gather.3 = bf16[16,4,16]{2,1,0:T(4,128)(2,1)S(1)} all-gather(bf16[1,4,16]{2,1,0:T(4,128)(2,1)S(1)} %bitcast.359), channel_id=1, replica_groups=mesh['dp'=16,'mp'=2] {'dp'}, dimensions={0}, use_global_device_ids=true | all-gather | bytes 2176 | tf_op jit(solution)/shard_map/all_gather | solution.py:248
  196.3 66.6 %all-reduce.16.cloned.1.call-done = (f32[1024,512]{1,0:T(8,128)}, f32[1024,512]{1,0:T(8,128)}) async-done(((f32[1024,512]{1,0:T(8,128)}, f32[1024,512]{1,0:T(8,128)}), (f32[1024,512]{1,0:T(8,128)}, f32[1024,512]{1,0:T(8,128)})) %all-reduce.16.cloned.1.call-update) | async-done | bytes 4194320 | tf_op jit(solution)/shard_map/psum | solution.py:86
  267.8 5.3 fusion.149
  273.2 5.7 fusion.163
  283.5 21.0 %fusion.6 = (bf16[1024,1024]{1,0:T(8,128)(2,1)}, bf16[1024,1024]{1,0:T(8,128)(2,1)}, f32[1024,1024]{1,0:T(8,128)S(1)}) fusion(f32[1024]{0:T(1024)S(1)} %reshape.484, f32[1024,1024]{1,0:T(8,128)S(1)} %copy-done.85, bf16[512,1024]{1,0:T(8,128)(2,1)S(1)} %copy-done.83, f32[1024,512]{1,0:T(8,128)S(1)} %copy-done.5, f32[512]{0:T(512)S(1)} %bitcast.356, ...), kind=kOutput, calls=%fused_computation.20 | convolution fusion | flops 1214775296 | bytes 15745024 | tf_op jit(solution)/shard_map/dot_general | solution.py:13
  312.0 4.7 convolution_convert_fusion.2
  334.3 40.7 %all-reduce.22.cloned.1.call-done = (bf16[1024,512]{1,0:T(8,128)(2,1)}, bf16[1024,512]{1,0:T(8,128)(2,1)}) async-done(((bf16[1024,512]{1,0:T(8,128)(2,1)}, bf16[1024,512]{1,0:T(8,128)(2,1)}), (bf16[1024,512]{1,0:T(8,128)(2,1)}, bf16[1024,512]{1,0:T(8,128)(2,1)})) %all-reduce.22.cloned.1.call-update) | async-done | bytes 2097168 | tf_op jit(solution)/shard_map/psum | solution.py:144
  378.3 6.3 fusion.104
  389.1 16.5 %multiply_reduce_fusion.1 = (f32[4,1024]{1,0:T(4,128)}, f32[4,1024,1024]{1,2,0:T(8,128)}) fusion(f32[4,1024,1024]{1,2,0:T(8,128)} %copy-done, f32[4,1024]{1,0:T(4,128)} %copy-done.49, pred[1024,1024]{0,1:T(8,128)(4,1)S(1)} %get-tuple-element.158, bf16[1024,4,64]{0,2,1:T(8,128)(2,1)} %bitcast.297, bf16[1024,4,64]{0,2,1:T(8,128)(2,1)} %bitcast.311), kind=kOutput, calls=%fused_computation.3 | convolution fusion | flops 557838336 | bytes 35684352 | tf_op jit(solution)/shard_map/qhd,khd->hqk/dot_general | solution.py:162
  405.6 8.3 multiply_convert_fusion.1
  421.0 9.7 bitcast_reduce_fusion
  430.8 12.4 multiply_reduce_fusion
  444.0 12.7 %multiply_convert_fusion = bf16[4,1024,1024]{1,2,0:T(8,128)(2,1)S(1)} fusion(f32[4,1024,1024]{1,2,0:T(8,128)} %get-tuple-element.141, f32[4,1024,1024]{1,2,0:T(8,128)} %copy-done.1, f32[4,1024]{1,0:T(4,128)S(1)} %get-tuple-element.140, f32[4,1024]{1,0:T(4,128)S(1)} %copy-done.52, pred[1024,1024]{0,1:T(8,128)(4,1)S(1)} %copy-done.9), kind=kLoop, calls=%fused_computation | loop fusion | flops 25165824 | bytes 43024384 | tf_op jit(solution)/shard_map/convert_element_type | solution.py:167
  463.2 9.7 bitcast_reduce_fusion.2
  510.7 44.8 %reduce-scatter.37.cloned.1.call-done = bf16[1024,32]{0,1:T(8,128)(2,1)} async-done(((bf16[1024,512]{0,1:T(8,128)(2,1)}), bf16[1024,32]{0,1:T(8,128)(2,1)}) %reduce-scatter.37.cloned.1.call-update) | async-done | bytes 65552 | tf_op jit(solution)/shard_map/reduce_scatter | solution.py:275
  558.8 57.7 %all-reduce.7 = (bf16[2,4,64]{2,1,0:T(4,128)(2,1)S(1)}, bf16[2,4,64]{2,1,0:T(4,128)(2,1)S(1)}, bf16[16,64]{1,0:T(8,128)(2,1)S(1)}, bf16[16,64]{1,0:T(8,128)(2,1)S(1)}) all-reduce(bf16[2,4,64]{2,1,0:T(4,128)(2,1)S(1)} %pad_maximum_fusion.9, ...), channel_id=11, replica_groups=mesh['dp'=16,'mp'=2] {'dp'}, use_global_device_ids=true, to_apply=%region_43.44.clone | all-reduce | flops 3072 | bytes 12288
  618.6 52.8 %reduce-scatter.41.cloned.1.call-done = bf16[32,2]{1,0:T(8,128)(2,1)} async-done(((bf16[512,2]{1,0:T(8,128)(2,1)}), bf16[32,2]{1,0:T(8,128)(2,1)}) %reduce-scatter.41.cloned.1.call-update) | async-done | bytes 144
  672.8 56.9 %reduce-scatter.31.cloned.1.call-done = bf16[256,32]{0,1:T(8,128)(2,1)} async-done(((bf16[256,512]{0,1:T(8,128)(2,1)}), bf16[256,32]{0,1:T(8,128)(2,1)}) %reduce-scatter.31.cloned.1.call-update) | async-done | bytes 16400 | tf_op jit(solution)/shard_map/reduce_scatter | solution.py:269
  729.7 58.4 %reduce-scatter.29.cloned.1.call-done = bf16[256,32]{0,1:T(8,128)(2,1)} async-done(((bf16[256,512]{0,1:T(8,128)(2,1)}), bf16[256,32]{0,1:T(8,128)(2,1)}) %reduce-scatter.29.cloned.1.call-update) | async-done | bytes 16400 | tf_op jit(solution)/shard_map/reduce_scatter | solution.py:269
  789.4 99.1 %all-reduce.18.cloned.1.call-done = (bf16[3,512,256]{2,0,1:T(4,128)(2,1)}, bf16[3,512,256]{2,0,1:T(4,128)(2,1)}) async-done(((bf16[3,512,256]{2,0,1:T(4,128)(2,1)}, bf16[3,512,256]{2,0,1:T(4,128)(2,1)}), (bf16[3,512,256]{2,0,1:T(4,128)(2,1)}, bf16[3,512,256]{2,0,1:T(4,128)(2,1)})) %all-reduce.18.cloned.1.call-update) | async-done | bytes 1572880
  890.1 108.0 %all-reduce.20.cloned.1.call-done = (bf16[1024,512]{1,0:T(8,128)(2,1)}, bf16[1024,512]{1,0:T(8,128)(2,1)}, bf16[1024,512]{1,0:T(8,128)(2,1)}, bf16[1024,512]{1,0:T(8,128)(2,1)}) async-done(((bf16[1024,512]{1,0:T(8,128)(2,1)}, bf16[1024,512]{1,0:T(8,128)(2,1)}, bf16[1024,512]{1,0:T(8,128)(2,1)}, bf16[1024,512]{1,0:T(8,128)(2,1)}), (bf16[1024,512]{1,0:T(8,128)(2,1)}, bf16[1024,512]{1,0:T(8,128)(2,1)}, ...) | async-done | bytes 4194320 | tf_op jit(solution)/shard_map/psum | solution.py:93
  1019.6 39.0 %reduce-scatter.45.cloned.1.call-done = bf16[32,2]{1,0:T(8,128)(2,1)} async-done(((bf16[512,2]{1,0:T(8,128)(2,1)}), bf16[32,2]{1,0:T(8,128)(2,1)}) %reduce-scatter.45.cloned.1.call-update) | async-done | bytes 144
  1059.4 57.4 %reduce-scatter.47.cloned.1.call-done = bf16[32,2]{1,0:T(8,128)(2,1)} async-done(((bf16[512,2]{1,0:T(8,128)(2,1)}), bf16[32,2]{1,0:T(8,128)(2,1)}) %reduce-scatter.47.cloned.1.call-update) | async-done | bytes 144
  1117.6 57.4 %reduce-scatter.49.cloned.1.call-done = bf16[32,2]{1,0:T(8,128)(2,1)} async-done(((bf16[512,2]{1,0:T(8,128)(2,1)}), bf16[32,2]{1,0:T(8,128)(2,1)}) %reduce-scatter.49.cloned.1.call-update) | async-done | bytes 144
  1175.7 57.4 %reduce-scatter.51.cloned.1.call-done = bf16[32,2]{1,0:T(8,128)(2,1)} async-done(((bf16[512,2]{1,0:T(8,128)(2,1)}), bf16[32,2]{1,0:T(8,128)(2,1)}) %reduce-scatter.51.cloned.1.call-update) | async-done | bytes 144
  (369 shorter events, 169.6 us)
Async XLA Ops:
  8.0 85.3 %copy-start.2 = (bf16[2,1024,512]{2,1,0:T(8,128)(2,1)S(1)}, bf16[2,1024,512]{2,1,0:T(8,128)(2,1)}, u32[]{:S(2)}) copy-start(bf16[2,1024,512]{2,1,0:T(8,128)(2,1)} %param.13) | copy-start | bytes 6291460
  8.0 65.6 %copy-start.61 = (bf16[3,32,256]{2,1,0:T(8,128)(2,1)S(1)}, bf16[3,32,256]{2,1,0:T(8,128)(2,1)}, u32[]{:S(2)}) copy-start(bf16[3,32,256]{2,1,0:T(8,128)(2,1)} %param.15) | copy-start | bytes 147460
  8.0 254.9 %all-reduce.16.cloned.1.call-start = ((), (), s32[]{:S(2)}) async-start(), calls=%async_computation.26 | async-start | bytes 8388608 | tf_op jit(solution)/shard_map/psum | solution.py:86
  32.4 61.9 %copy-start.62 = (f32[1,512]{1,0:T(1,128)}, f32[1,512]{1,0:T(1,128)S(1)}, u32[]{:S(2)}) copy-start(f32[1,512]{1,0:T(1,128)S(1)} %get-tuple-element.127) | copy-start | bytes 6148
  50.1 44.2 %copy-start.65 = (f32[1,512]{1,0:T(1,128)}, f32[1,512]{1,0:T(1,128)S(1)}, u32[]{:S(2)}) copy-start(f32[1,512]{1,0:T(1,128)S(1)} %get-tuple-element.129) | copy-start | bytes 6148
  52.0 42.8 %copy-start.53 = (f32[1024]{0:T(1024)}, f32[1024]{0:T(1024)S(1)}, u32[]{:S(2)}) copy-start(f32[1024]{0:T(1024)S(1)} %get-tuple-element.156) | copy-start | bytes 12292
  52.0 42.7 %copy-start.55 = (f32[1024]{0:T(1024)}, f32[1024]{0:T(1024)S(1)}, u32[]{:S(2)}) copy-start(f32[1024]{0:T(1024)S(1)} %get-tuple-element.157) | copy-start | bytes 12292
  119.6 266.8 %copy-start.15 = (bf16[256,512]{0,1:T(8,128)(2,1)}, bf16[256,512]{0,1:T(8,128)(2,1)S(1)}, u32[]{:S(2)}) copy-start(bf16[256,512]{0,1:T(8,128)(2,1)S(1)} %all_gather.40) | copy-start | bytes 786436
  157.6 110.2 %all-gather.7.cloned.1.call-start = ((), (), s32[]{:S(2)}) async-start(), calls=%async_computation.12 | async-start | bytes 1114112 | tf_op jit(solution)/shard_map/all_gather | solution.py:245
  158.1 115.0 %all-gather.9.cloned.1.call-start = ((), (), s32[]{:S(2)}) async-start(), calls=%async_computation.13 | async-start | bytes 1114112 | tf_op jit(solution)/shard_map/all_gather | solution.py:246
  158.7 216.3 %all-reduce.22.cloned.1.call-start = ((), (), s32[]{:S(2)}) async-start(), calls=%async_computation.29 | async-start | bytes 4194304 | tf_op jit(solution)/shard_map/psum | solution.py:144
  311.9 197.2 %reduce-scatter.35.cloned.1.call-start = ((), (), s32[]{:S(2)}) async-start(), calls=%async_computation.17 | async-start | bytes 1114112 | tf_op jit(solution)/shard_map/reduce_scatter | solution.py:272
  316.7 192.5 %reduce-scatter.33.cloned.1.call-start = ((), (), s32[]{:S(2)}) async-start(), calls=%async_computation.16 | async-start | bytes 1114112 | tf_op jit(solution)/shard_map/reduce_scatter | solution.py:272
  321.2 189.5 %reduce-scatter.39.cloned.1.call-start = ((), (), s32[]{:S(2)}) async-start(), calls=%async_computation.19 | async-start | bytes 1114112 | tf_op jit(solution)/shard_map/reduce_scatter | solution.py:275
  325.6 229.9 %reduce-scatter.37.cloned.1.call-start = ((), (), s32[]{:S(2)}) async-start(), calls=%async_computation.18 | async-start | bytes 1114112 | tf_op jit(solution)/shard_map/reduce_scatter | solution.py:275
  330.0 287.8 %reduce-scatter.43.cloned.1.call-start = ((), (), s32[]{:S(2)}) async-start(), calls=%async_computation.21 | async-start | bytes 139264
  473.0 198.5 %reduce-scatter.41.cloned.1.call-start = ((), (), s32[]{:S(2)}) async-start(), calls=%async_computation.20 | async-start | bytes 139264
  473.9 255.8 %reduce-scatter.31.cloned.1.call-start = ((), (), s32[]{:S(2)}) async-start(), calls=%async_computation.15 | async-start | bytes 278528 | tf_op jit(solution)/shard_map/reduce_scatter | solution.py:269
  481.1 306.9 %reduce-scatter.29.cloned.1.call-start = ((), (), s32[]{:S(2)}) async-start(), calls=%async_computation.14 | async-start | bytes 278528 | tf_op jit(solution)/shard_map/reduce_scatter | solution.py:269
  494.5 394.0 %all-reduce.18.cloned.1.call-start = ((), (), s32[]{:S(2)}) async-start(), calls=%async_computation.27 | async-start | bytes 4194304
  498.4 499.7 %all-reduce.20.cloned.1.call-start = ((), (), s32[]{:S(2)}) async-start(), calls=%async_computation.28 | async-start | bytes 8388608 | tf_op jit(solution)/shard_map/psum | solution.py:93
  504.9 52.1 %copy-start.12 = (bf16[1024,512]{1,0:T(8,128)(2,1)S(1)}, bf16[1024,512]{1,0:T(8,128)(2,1)}, u32[]{:S(2)}) copy-start(bf16[1024,512]{1,0:T(8,128)(2,1)} %get-tuple-element.100) | copy-start | bytes 3145732
  507.0 51.7 %copy-start.70 = (bf16[512]{0:T(512)(128)(2,1)S(1)}, bf16[512]{0:T(512)(128)(2,1)}, u32[]{:S(2)}) copy-start(bf16[512]{0:T(512)(128)(2,1)} %get-tuple-element.132) | copy-start | bytes 3076
  507.0 51.7 %copy-start.73 = (bf16[4,64]{1,0:T(4,128)(2,1)S(1)}, bf16[4,64]{1,0:T(4,128)(2,1)}, u32[]{:S(2)}) copy-start(bf16[4,64]{1,0:T(4,128)(2,1)} %get-tuple-element.150) | copy-start | bytes 1540
  507.0 51.7 %copy-start.80 = (bf16[4,64]{1,0:T(4,128)(2,1)S(1)}, bf16[4,64]{1,0:T(4,128)(2,1)}, u32[]{:S(2)}) copy-start(bf16[4,64]{1,0:T(4,128)(2,1)} %get-tuple-element.148) | copy-start | bytes 1540
  507.0 51.8 %copy-start.74 = (bf16[4,64]{1,0:T(4,128)(2,1)S(1)}, bf16[4,64]{1,0:T(4,128)(2,1)}, u32[]{:S(2)}) copy-start(bf16[4,64]{1,0:T(4,128)(2,1)} %get-tuple-element.146) | copy-start | bytes 1540
  507.0 51.8 %copy-start.79 = (bf16[4,64]{1,0:T(4,128)(2,1)S(1)}, bf16[4,64]{1,0:T(4,128)(2,1)}, u32[]{:S(2)}) copy-start(bf16[4,64]{1,0:T(4,128)(2,1)} %get-tuple-element.144) | copy-start | bytes 1540
  507.0 495.9 %copy-start.69 = (f32[1,512]{1,0:T(1,128)S(1)}, f32[1,512]{1,0:T(1,128)}, u32[]{:S(2)}) copy-start(f32[1,512]{1,0:T(1,128)} %get-tuple-element.122) | copy-start | bytes 6148
  507.0 551.6 %reduce-scatter.45.cloned.1.call-start = ((), (), s32[]{:S(2)}) async-start(), calls=%async_computation.22 | async-start | bytes 139264
  1002.9 113.9 %reduce-scatter.47.cloned.1.call-start = ((), (), s32[]{:S(2)}) async-start(), calls=%async_computation.23 | async-start | bytes 139264
  1011.0 163.9 %reduce-scatter.49.cloned.1.call-start = ((), (), s32[]{:S(2)}) async-start(), calls=%async_computation.24 | async-start | bytes 139264
  1012.1 221.0 %reduce-scatter.51.cloned.1.call-start = ((), (), s32[]{:S(2)}) async-start(), calls=%async_computation.25 | async-start | bytes 139264
  (78 other events, 682.3 us)
Sparse Core Ops, SparseCore 0:
  157.7 105.1 all-reduce.15
  312.0 62.9 all-reduce.21
Sparse Core Ops, SparseCore 1:
  160.2 35.0 all-gather.6
  197.3 36.8 all-gather.8
  316.8 57.6 reduce-scatter.34
  378.1 56.6 reduce-scatter.32
  438.4 56.7 reduce-scatter.38
  498.8 56.6 reduce-scatter.36
  558.8 54.6 reduce-scatter.42
  616.8 54.6 reduce-scatter.40
  674.8 54.8 reduce-scatter.30
  733.2 54.8 reduce-scatter.28
  791.5 96.9 all-reduce.17
  891.1 107.0 all-reduce.19
  1003.0 55.6 reduce-scatter.44
  1062.1 54.6 reduce-scatter.46
  1120.3 54.6 reduce-scatter.48
  1178.4 54.7 reduce-scatter.50
where the time goes:
time: 1250 us; the launch traced here: 1240 us
  waiting for transfers between devices  740 us (59%)
  blocking collectives  193 us (15%)
  matrix products  176 us (14%)
  other arithmetic  78.4 us (6%)
  local copies, waits for them, and re-layouts  35.5 us (3%)
  between operations  18.9 us (2%)
    unnamed x25, waiting for transfers between devices  364 us
    reduce_scatter x2, waiting for transfers between devices, body(): lax.psum_scatter(local_grads[1].astype(jnp.bfloat16), 'dp', scatter_dimen...  115 us
    psum x1, waiting for transfers between devices, forward(): lax.psum(partial_ffn.astype(jnp.bfloat16), 'mp').astype(jnp.float32)  108 us
    dot_general x24, matrix products, product(): return jnp.dot(left, right, preferred_element_type=jnp.float32)  83.6 us
    psum x1, waiting for transfers between devices, forward(): resid = rows_in + lax.psum(partial_attn, 'mp') + bias_out[0]  66.6 us
    unnamed x1, blocking collectives  57.7 us
    reduce_scatter x2, waiting for transfers between devices, body(): lax.psum_scatter(local_grads[3].astype(jnp.bfloat16), 'dp', scatter_dimen...  44.8 us
    psum x1, waiting for transfers between devices, backward(): lax.psum(partial_two.astype(jnp.bfloat16), 'mp').astype(jnp.float32)  40.7 us
  transfers between devices with their start and end apart: 18, of which 12 were waited for; matrix products, arithmetic and copies ran while one was open for 15% of the time, Pallas kernels for 0%

commit v1 on v0

--- a/solution.py
+++ b/solution.py
@@ -54,7 +54,7 @@
     return jnp.where(allowed[None], scores, masked_value)
 
 
-def forward(rows_in, chain_rows, keep_rows, weights):
+def forward(rows_in, chain_rows, keep_rows, weights, join=lambda a: a):
     qkv_full, out_full, up_full, down_full, bias_qv, bias_up, bias_out, gain_full, shift_full = (
         weights
     )
@@ -83,14 +83,14 @@
     )
     mixed = mixed.reshape(row_count, -1).astype(jnp.bfloat16)
     partial_attn = product(mixed, out_full)
-    resid = rows_in + lax.psum(partial_attn, "mp") + bias_out[0]
+    resid = rows_in + join(partial_attn) + bias_out[0]
     normed_two, scaled_two, inverse_two = normalize(resid, gain_full[1], shift_full[1])
     hidden_two = normed_two.astype(jnp.bfloat16)
     pre = product(hidden_two, up_full) + bias_up.astype(jnp.float32).reshape(-1)
     act = jax.nn.gelu(pre, approximate=False).astype(jnp.bfloat16)
     partial_ffn = product(act, down_full)
     result = (
-        resid + lax.psum(partial_ffn.astype(jnp.bfloat16), "mp").astype(jnp.float32) + bias_out[1]
+        resid + join(partial_ffn.astype(jnp.bfloat16)).astype(jnp.float32) + bias_out[1]
     )
     kept = (
         allowed,
@@ -111,7 +111,7 @@
     return (result, kept)
 
 
-def backward(grad_out, result, kept, weights):
+def backward(grad_out, result, kept, weights, join=lambda a: a):
     qkv_full, out_full, up_full, down_full, bias_qv, bias_up, bias_out, gain_full, shift_full = (
         weights
     )
@@ -141,7 +141,7 @@
     grad_bup = jnp.sum(grad_pre, axis=0, dtype=jnp.float32).reshape(bias_up.shape)
     grad_up = product(hidden_two.T, grad_pre)
     partial_two = product(grad_pre, up_full.T)
-    grad_two = lax.psum(partial_two.astype(jnp.bfloat16), "mp").astype(jnp.float32)
+    grad_two = join(partial_two.astype(jnp.bfloat16)).astype(jnp.float32)
     gain_two = jnp.sum(grad_two * scaled_two, axis=0)
     shift_two = jnp.sum(grad_two, axis=0)
     grad_resid = grad_out + normalize_back(grad_two, scaled_two, inverse_two, gain_full[1])
@@ -185,7 +185,7 @@
     )
     grad_qkv = jnp.einsum("rd,crk->cdk", hidden_one, stacked, preferred_element_type=jnp.float32)
     partial_one = jnp.einsum("crk,cdk->rd", stacked, qkv_full, preferred_element_type=jnp.float32)
-    grad_one = lax.psum(partial_one.astype(jnp.bfloat16), "mp").astype(jnp.float32)
+    grad_one = join(partial_one.astype(jnp.bfloat16)).astype(jnp.float32)
     grad_bqv = jnp.stack(
         [
             jnp.sum(stacked[0], axis=0, dtype=jnp.float32),
@@ -219,7 +219,7 @@
     return (result, grad_in, local_grads)
 
 
-def body(
+def body_generic(
     activations,
     cotangent,
     w_qkv,
@@ -255,10 +255,11 @@
             chain_ids[batch_index],
             key_keep[batch_index],
             weights,
+            lambda a: lax.psum(a, "mp"),
         )
         live_rows = (chain_ids[batch_index] >= 0).astype(jnp.float32)[:, None]
         output_rows, grad_in, local_grads = backward(
-            cotangent[batch_index].astype(jnp.float32) * live_rows, result, kept, weights
+            cotangent[batch_index].astype(jnp.float32) * live_rows, result, kept, weights, lambda a: lax.psum(a, "mp")
         )
         outputs.append(output_rows)
         input_grads.append(grad_in)
@@ -310,6 +311,95 @@
     )
 
 
+def cat_weights(w_qkv, w_o, w_up, w_down):
+    mixed_part = jnp.concatenate([w_qkv[0], w_qkv[1], w_qkv[2], w_o.T], axis=1)
+    return jnp.stack([w_up, w_down.T, mixed_part])
+
+
+def cat_small(b_qv, b_up, out_bias, norm_gain, norm_bias):
+    parts = [b_qv.reshape(-1), b_up.reshape(-1), out_bias.reshape(-1), norm_gain.reshape(-1), norm_bias.reshape(-1)]
+    return jnp.concatenate(parts)
+
+
+def body_split(
+    activations,
+    cotangent,
+    w_qkv,
+    w_o,
+    w_up,
+    w_down,
+    b_qv,
+    b_up,
+    out_bias,
+    norm_gain,
+    norm_bias,
+    chain_ids,
+    key_keep,
+):
+    own = lax.axis_index("mp")
+    mp = lax.axis_size("mp")
+    dp = lax.axis_size("dp")
+    width = out_bias.shape[1] * dp
+    local_heads, local_hd = b_qv.shape[1], b_qv.shape[2]
+    packed = cat_weights(w_qkv, w_o, w_up, w_down)
+    small = cat_small(b_qv, b_up, out_bias, norm_gain, norm_bias)
+    full = lax.all_gather(packed, ("mp", "dp"), axis=0, tiled=False)
+    full = full.reshape(mp, dp, 3, -1, packed.shape[2])
+    full = full.transpose(2, 0, 1, 3, 4).reshape(3, mp, width, packed.shape[2])
+    smalls = lax.all_gather(small, ("mp", "dp"), axis=0, tiled=False).reshape(mp, dp, -1)
+    sizes = [b_qv.size, b_up.size, out_bias.size, norm_gain.size, norm_bias.size]
+    offs = [0]
+    for s in sizes:
+        offs.append(offs[-1] + s)
+    piece = lambda k: smalls[:, :, offs[k] : offs[k + 1]]
+    bias_qv = piece(0).reshape(mp, dp, 2, local_heads, local_hd).transpose(2, 0, 3, 1, 4).reshape(2, mp * local_heads, dp * local_hd)
+    bias_up = piece(1).reshape(mp, dp, b_up.shape[0], b_up.shape[1]).transpose(0, 2, 1, 3).reshape(mp * b_up.shape[0], -1)
+    vec = lambda k: piece(k)[0].reshape(dp, 2, -1).transpose(1, 0, 2).reshape(2, width)
+    bias_out, gain_full, shift_full = vec(2), vec(3), vec(4)
+    q4 = packed.shape[2] // 4
+    pick = lambda c: full[2, :, :, c * q4 : (c + 1) * q4].transpose(1, 0, 2).reshape(width, mp * q4)
+    qkv_full = jnp.stack([pick(0), pick(1), pick(2)])
+    out_full = pick(3).T
+    up_full = full[0].transpose(1, 0, 2).reshape(width, -1)
+    down_full = full[1].transpose(0, 2, 1).reshape(-1, width)
+    weights = (qkv_full, out_full, up_full, down_full, bias_qv, bias_up, bias_out, gain_full, shift_full)
+    take = lambda a: lax.dynamic_index_in_dim(a, own, 0, keepdims=False)
+    chain_rows = take(chain_ids)
+    result, kept = forward(take(activations).astype(jnp.float32), chain_rows, take(key_keep), weights)
+    live_rows = (chain_rows >= 0).astype(jnp.float32)[:, None]
+    output_rows, grad_in, grads = backward(take(cotangent).astype(jnp.float32) * live_rows, result, kept, weights)
+    both = jnp.stack([output_rows, grad_in]).astype(jnp.bfloat16)
+    gathered = lax.all_gather(both, "mp", axis=0, tiled=False).astype(jnp.float32)
+    g_qkv, g_o, g_up, g_down, g_bqv, g_bup, g_bias, g_gain, g_shift = grads
+    halves = lambda a: a.reshape(a.shape[0], mp, -1).transpose(1, 0, 2)
+    g_mix = jnp.concatenate([halves(g_qkv[0]), halves(g_qkv[1]), halves(g_qkv[2]), halves(g_o.T)], axis=2)
+    g_all = jnp.stack([halves(g_up), halves(g_down.T), g_mix]).astype(jnp.bfloat16)
+    g_all = g_all.reshape(3, mp, dp, width // dp, -1).transpose(1, 2, 0, 3, 4)
+    g_all = g_all.reshape(mp * dp, 3, width // dp, -1)
+    g_own = lax.psum_scatter(g_all, ("mp", "dp"), scatter_dimension=0, tiled=False).astype(jnp.float32)
+    s_qv = g_bqv.reshape(2, mp, local_heads, dp, local_hd).transpose(1, 3, 0, 2, 4).reshape(mp, dp, -1)
+    s_up = g_bup.reshape(mp, b_up.shape[0], dp, b_up.shape[1]).transpose(0, 2, 1, 3).reshape(mp, dp, -1)
+    rep = lambda a: jnp.broadcast_to(a.reshape(2, dp, -1).transpose(1, 0, 2).reshape(1, dp, -1), (mp, dp, 2 * width // dp))
+    s_all = jnp.concatenate([s_qv, s_up, rep(g_bias), rep(g_gain), rep(g_shift)], axis=2)
+    s_all = s_all.reshape(mp * dp, -1)
+    s_sum = lax.psum(s_all, ("mp", "dp"))
+    s_own = lax.dynamic_index_in_dim(s_sum, own * dp + lax.axis_index("dp"), 0, keepdims=False)
+    part = lambda k, a: s_own[offs[k] : offs[k + 1]].reshape(a.shape)
+    mix = g_own[2]
+    return (
+        gathered[:, 0],
+        gathered[:, 1],
+        jnp.stack([mix[:, c * q4 : (c + 1) * q4] for c in range(3)]),
+        mix[:, 3 * q4 :].T,
+        g_own[0],
+        g_own[1].T,
+        part(0, b_qv),
+        part(1, b_up),
+        part(2, out_bias),
+        part(3, norm_gain),
+        part(4, norm_bias),
+    )
+
 def solution(mesh):
     placed = (
         P(None, "dp", None),
@@ -326,6 +416,7 @@
         P(None, "dp"),
         P(None, "dp"),
     )
+    body = body_split if mesh.shape["mp"] == 2 else body_generic
     return jax.shard_map(
         body,
         mesh=mesh,

time: 1250 us -> 532 us (0.43)
  waiting for transfers between devices: 740 us -> 99.7 us
  blocking collectives: 193 us -> 83.2 us
  local copies, waits for them, and re-layouts: 35.5 us -> 86.6 us
  other arithmetic: 78.4 us -> 58.2 us
    unnamed x25 -> x3, waiting for transfers between devices: 364 us -> 0.05 us
    psum x3 -> x0, waiting for transfers between devices: 215 us -> none  [the longest x1 108 us: forward(): lax.psum(partial_ffn.astype(jnp.bfloat16), 'mp').astype(jnp.float32)]
    all_gather x7 -> x0, blocking collectives: 136 us -> none  [the longest x1 23.3 us: body(): lax.all_gather(norm_gain, 'dp', axis=1, tiled=True)]
    reduce_scatter x6 -> x1, waiting for transfers between devices: 160 us -> 84 us  [body_split(): lax.psum_scatter(g_all, ('mp', 'dp'), scatter_dimension=0, tiled=False)]
    psum x0 -> x1, blocking collectives: none -> 40.5 us  [body_split(): s_sum = lax.psum(s_all, ('mp', 'dp'))]
    transpose x0 -> x19, local copies, waits for them, and re-layouts: none -> 24.1 us  [the longest x8 9.53 us: body_split(): full[2, :, :, c * q4:(c + 1) * q4].transpose(1, 0, 2)]
    reduce_sum x7 -> x0, other arithmetic: 16.6 us -> none  [the longest x1 6.31 us: backward(): jnp.sum(grad_out, axis=0)]
    unnamed x200 -> x91, local copies, waits for them, and re-layouts: 21.7 us -> 5.74 us
  transfers between devices with their start and end apart: 18 -> 3, of which waited for: 12 -> 2; matrix products, arithmetic and copies ran while one was open for 15% -> 13% of each run, Pallas kernels for 0% -> 0%
where the time goes in v1:
time: 532 us; the launch traced here: 523 us
  matrix products  179 us (34%)
  waiting for transfers between devices  99.7 us (19%)
  local copies, waits for them, and re-layouts  86.6 us (16%)
  blocking collectives  83.2 us (16%)
  other arithmetic  58.2 us (11%)
  between operations  15.6 us (3%)
    reduce_scatter x1, waiting for transfers between devices, body_split(): lax.psum_scatter(g_all, ('mp', 'dp'), scatter_dimension=0, tiled=False)  84 us
    dot_general x12, matrix products, product(): return jnp.dot(left, right, preferred_element_type=jnp.float32)  77.4 us
    unnamed x1, blocking collectives  42.7 us
    psum x1, blocking collectives, body_split(): s_sum = lax.psum(s_all, ('mp', 'dp'))  40.5 us
    convert_element_type x1, other arithmetic, backward(): grad_scores = (probs * (grad_probs - jnp.sum(grad_probs * probs, axis=-1,...  28.6 us
    dot_general x1, matrix products, backward(): jnp.einsum('qhd,khd->hqk', grad_mixed, value_heads, preferred_element_typ...  23.8 us
    dot_general x1, matrix products, backward(): jnp.einsum('hqk,qhd->khd', probs_low, grad_mixed, preferred_element_type=...  16.6 us
    dot_general x1, matrix products, forward(): jnp.einsum('hqk,khd->qhd', probs_low, value_rows.reshape(row_count, head_...  16.4 us
  transfers between devices with their start and end apart: 3, of which 2 were waited for; matrix products, arithmetic and copies ran while one was open for 13% of the time, Pallas kernels for 0%

profile of v1, /device:TPU:0, one launch (start us, length us, event | category | flops | bytes accessed | tf_op | source)
XLA Modules:
  0.0 522.7 jit_solution(7583278048740516211)
XLA Ops:
  16.5 42.7 %all-reduce = bf16[9216]{0:T(1024)(128)(2,1)S(1)} all-reduce(bf16[9216]{0:T(1024)(128)(2,1)S(1)} %dynamic-update-slice), channel_id=2, replica_groups=mesh['dp'=16,'mp'=2] {'mp','dp'}, use_global_device_ids=true, to_apply=%add | all-reduce | flops 9216 | bytes 36864
  68.1 15.7 %all-gather.7.cloned.1.call-done = bf16[96,32,1024]{2,1,0:T(8,128)(2,1)} async-done(((bf16[3,32,1024]{2,1,0:T(8,128)(2,1)}), bf16[96,32,1024]{2,1,0:T(8,128)(2,1)}) %all-gather.7.cloned.1.call-update) | async-done | bytes 6291472 | tf_op jit(solution)/shard_map/all_gather | solution.py:346
  83.8 5.2 fusion.143
  100.7 4.1 copy.275
  104.8 3.9 copy.272
  110.7 2.3 add_convert_fusion.2
  113.0 14.2 %fusion = (f32[8,1024]{1,0:T(8,128)S(1)}, f32[8,1024,1024]{1,2,0:T(8,128)}) fusion(pred[1024,1024]{0,1:T(8,128)(4,1)S(1)} %fusion.35, bf16[1024,8,64]{0,2,1:T(8,128)(2,1)S(1)} %bitcast.320, bf16[1024,8,64]{0,2,1:T(8,128)(2,1)S(1)} %bitcast.318), kind=kOutput, calls=%fused_computation.5 | convolution fusion | flops 1098899456 | bytes 36732928 | tf_op jit(solution)/shard_map/qhd,khd->hqk/dot_general | solution.py:51
  127.1 14.2 %exponential_reduce_fusion = f32[8,1024]{1,0:T(8,128)S(1)} fusion(f32[8,1024,1024]{1,2,0:T(8,128)} %get-tuple-element.136, f32[8,1024]{1,0:T(8,128)S(1)} %get-tuple-element.135, pred[1024,1024]{0,1:T(8,128)(4,1)S(1)} %fusion.35), kind=kLoop, calls=%fused_computation.3 | loop fusion | flops 33546240 | bytes 34668544 | tf_op jit(solution)/shard_map/reduce_sum | solution.py:76
  142.3 16.4 %convolution_convert_fusion.7 = bf16[8,64,1024]{2,1,0:T(8,128)(2,1)} fusion(bf16[1024,8,64]{0,2,1:T(8,128)(2,1)S(1)} %bitcast.337, f32[8,1024,1024]{1,2,0:T(8,128)} %get-tuple-element.136, f32[8,1024]{1,0:T(8,128)S(1)} %log_add_fusion, pred[1024,1024]{0,1:T(8,128)(4,1)S(1)} %fusion.35), kind=kOutput, calls=%fused_computation.134 | convolution fusion | flops 1107820544 | bytes 36732928 | tf_op jit(solution)/shard_map/hqk,khd->qhd/dot_general | solution.py:78
  161.2 21.9 %fusion.13 = (bf16[2048,1024]{0,1:T(8,128)(2,1)}, f32[1024,2048]{1,0:T(8,128)S(1)}) fusion(f32[2048]{0:T(1024)S(1)} %reshape.484, bf16[512,2048]{0,1:T(8,128)(2,1)S(1)} %bitcast.331, f32[1024,512]{0,1:T(8,128)S(1)} %get-tuple-element.138, f32[512]{0:T(512)S(1)} %add.155, f32[512]{0:T(512)S(1)} %mul.200, f32[1024]{0:T(1024)S(1)} %add_rsqrt_fusion, ...), kind=kOutput, calls=%fused_computation.21 | convolution fusion | flops 2288517120 | bytes 16797696 | tf_op jit(solution)/shard_map/dot_general | solution.py:13
  183.1 5.8 %convert_reduce_fusion = (f32[2048]{0:T(1024)}, bf16[1024,2048]{1,0:T(8,128)(2,1)S(1)}) fusion(f32[1024,2048]{1,0:T(8,128)S(1)} %get-tuple-element.144, f32[2048]{0:T(1024)S(1)} %reshape.484, bf16[2048,512]{1,0:T(8,128)(2,1)S(1)} %bitcast.330, f32[1024]{0:T(1024)S(1)} %copy-done.24, bf16[1,1024,512]{1,2,0:T(8,128)(2,1)S(1)} %copy-done.12), kind=kOutput, calls=%fused_computation.27 | convolution fusion | flops 2176317440 | bytes 15749120 | tf_op jit(solution)/shard_map/dot_general | solution.py:13
  188.9 3.4 fusion.70
  195.7 16.6 %convert_reduce_fusion.4 = (f32[8,64]{1,0:T(8,128)}, bf16[8,64,1024]{2,1,0:T(8,128)(2,1)}) fusion(bf16[1024,8,64]{0,2,1:T(8,128)(2,1)} %bitcast.322, f32[8,1024,1024]{1,2,0:T(8,128)} %get-tuple-element.136, f32[8,1024]{1,0:T(8,128)S(1)} %log_add_fusion, pred[1024,1024]{0,1:T(8,128)(4,1)S(1)} %fusion.35), kind=kOutput, calls=%fused_computation.112 | convolution fusion | flops 1108868608 | bytes 36734976 | tf_op jit(solution)/shard_map/hqk,qhd->khd/dot_general | solution.py:159
  212.3 23.8 %multiply_reduce_fusion = (f32[8,1024]{1,0:T(8,128)S(1)}, f32[8,1024,1024]{1,2,0:T(8,128)}) fusion(f32[8,1024,1024]{1,2,0:T(8,128)} %get-tuple-element.136, f32[8,1024]{1,0:T(8,128)S(1)} %log_add_fusion, pred[1024,1024]{0,1:T(8,128)(4,1)S(1)} %fusion.35, bf16[1024,8,64]{0,2,1:T(8,128)(2,1)} %bitcast.323, bf16[1024,8,64]{0,2,1:T(8,128)(2,1)} %bitcast.338), kind=kOutput, calls=%fused_computation.1 | convolution fusion | flops 1115676672 | bytes 70320128 | tf_op jit(solution)/shard_map/qhd,khd->hqk/dot_general | solution.py:162
  236.1 28.6 %multiply_convert_fusion = bf16[8,1024,1024]{1,2,0:T(8,128)(2,1)} fusion(f32[8,1024,1024]{1,2,0:T(8,128)} %get-tuple-element.141, f32[8,1024,1024]{1,2,0:T(8,128)} %get-tuple-element.136, f32[8,1024]{1,0:T(8,128)S(1)} %get-tuple-element.140, f32[8,1024]{1,0:T(8,128)S(1)} %log_add_fusion, pred[1024,1024]{0,1:T(8,128)(4,1)S(1)} %fusion.35), kind=kLoop, calls=%fused_computation | loop fusion | flops 50331648 | bytes 85000192 | tf_op jit(solution)/shard_map/convert_element_type | solution.py:167
  264.7 12.3 %multiply_convert_fusion.1 = bf16[8,64,1024]{2,1,0:T(8,128)(2,1)} fusion(bf16[1024,8,64]{0,2,1:T(8,128)(2,1)} %bitcast.321, bf16[8,1024,1024]{1,2,0:T(8,128)(2,1)} %multiply_convert_fusion), kind=kOutput, calls=%fused_computation.114 | convolution fusion | flops 1074790400 | bytes 18874368 | tf_op jit(solution)/shard_map/hqk,qhd->khd/dot_general | solution.py:176
  277.1 9.8 %convert_reduce_fusion.5 = (f32[8,64]{1,0:T(8,128)S(1)}, bf16[8,64,1024]{2,1,0:T(8,128)(2,1)}) fusion(bf16[1024,8,64]{0,2,1:T(8,128)(2,1)S(1)} %bitcast.319, bf16[8,1024,1024]{1,2,0:T(8,128)(2,1)} %multiply_convert_fusion), kind=kOutput, calls=%fused_computation.113 | convolution fusion | flops 1075838464 | bytes 18876416 | tf_op jit(solution)/shard_map/hqk,khd->qhd/dot_general | solution.py:172
  293.4 24.6 %fusion.83 = bf16[1,1,1024,512]{2,3,1,0:T(8,128)(2,1)} fusion(f32[1024,512]{0,1:T(8,128)} %copy-done.5, bf16[2048,512]{1,0:T(8,128)(2,1)} %bitcast.329, f32[1024,2048]{1,0:T(8,128)} %copy-done.41, f32[2048]{0:T(1024)S(1)} %reshape.484, f32[512]{0:T(512)S(1)} %copy-done.36), kind=kOutput, calls=%fused_computation.137 | convolution fusion | flops 2288517120 | bytes 13641728 | tf_op jit(solution)/shard_map/dot_general | solution.py:13
  324.9 4.8 fusion.71
  332.0 3.9 copy.289
  336.0 6.7 %copy.318 = bf16[2048,1024]{1,0:T(8,128)(2,1)} copy(bf16[2048,1024]{0,1:T(8,128)(2,1)} %get-tuple-element.143) | data formatting | bytes 8388608 | tf_op jit(solution)/shard_map/dot_general | solution.py:13
  342.7 7.2 %convolution_convert_fusion = bf16[512,2048]{1,0:T(8,128)(2,1)} fusion(bf16[1024,2048]{1,0:T(8,128)(2,1)} %copy-done.40, f32[1024,512]{0,1:T(8,128)} %copy-done.5, f32[512]{0:T(512)S(1)} %copy-done.35, f32[512]{0:T(512)S(1)} %mul.200, f32[1024]{0:T(1024)S(1)} %add_rsqrt_fusion, f32[1024]{0:T(1024)S(1)} %broadcast_multiply_fusion.4), kind=kOutput, calls=%fused_computation.72 | convolution fusion | flops 2151153664 | bytes 8400896 | tf_op jit(solution)/shard_map/dot_general | solution.py:13
  349.9 4.5 reshape.477
  354.4 3.6 copy.290
  358.0 4.0 fusion.77
  363.1 2.4 copy.295
  365.5 5.0 convolution_convert_fusion.1
  371.3 3.4 copy.296
  376.9 40.5 %psum.7 = f32[32,288]{1,0:T(8,128)S(1)} all-reduce(f32[32,288]{1,0:T(8,128)S(1)} %concatenate.49), channel_id=1, replica_groups=mesh['dp'=16,'mp'=2] {'mp','dp'}, use_global_device_ids=true, to_apply=%region_21.22 | all-reduce | flops 9216 | bytes 73728 | tf_op jit(solution)/shard_map/psum | solution.py:385
  420.9 3.5 convert_element_type.260
  424.4 4.4 slice_bitcast_fusion
  428.8 84.0 %reduce-scatter.2.cloned.1.call-done = bf16[1,3,32,1024]{3,2,1,0:T(8,128)(2,1)} async-done(((bf16[32,3,32,1024]{3,2,1,0:T(8,128)(2,1)}), bf16[1,3,32,1024]{3,2,1,0:T(8,128)(2,1)}) %reduce-scatter.2.cloned.1.call-update) | async-done | bytes 196624 | tf_op jit(solution)/shard_map/reduce_scatter | solution.py:379
  (220 shorter events, 63.7 us)
Async XLA Ops:
  7.2 58.3 %copy-start = (s32[2,1024]{1,0:T(2,128)S(1)}, s32[2,1024]{1,0:T(2,128)}, u32[]{:S(2)}) copy-start(s32[2,1024]{1,0:T(2,128)} %param.24) | copy-start | bytes 24580
  7.2 58.3 %copy-start.39 = (s32[2,1024]{1,0:T(2,128)S(1)}, s32[2,1024]{1,0:T(2,128)}, u32[]{:S(2)}) copy-start(s32[2,1024]{1,0:T(2,128)} %param.25) | copy-start | bytes 24580
  7.2 76.6 %all-gather.7.cloned.1.call-start = ((), (), s32[]{:S(2)}) async-start(), calls=%async_computation.3 | async-start | bytes 6488064 | tf_op jit(solution)/shard_map/all_gather | solution.py:346
  10.3 410.5 %all-gather.5.cloned.1.call-start = ((), (), s32[]{:S(2)}) async-start(), calls=%async_computation.1 | async-start | bytes 6291456 | tf_op jit(solution)/shard_map/all_gather | solution.py:372
  60.5 100.6 %copy-start.34 = (f32[512]{0:T(512)}, f32[512]{0:T(512)S(1)}, u32[]{:S(2)}) copy-start(f32[512]{0:T(512)S(1)} %add.155) | copy-start | bytes 6148
  60.6 80.8 %copy-start.32 = (f32[512]{0:T(512)}, f32[512]{0:T(512)S(1)}, u32[]{:S(2)}) copy-start(f32[512]{0:T(512)S(1)} %add.140) | copy-start | bytes 6148
  60.8 80.5 %copy-start.26 = (f32[512]{0:T(512)}, f32[512]{0:T(512)S(1)}, u32[]{:S(2)}) copy-start(f32[512]{0:T(512)S(1)} %mul.193) | copy-start | bytes 6148
  65.5 93.3 %copy-start.3 = (bf16[1,1024,512]{1,2,0:T(8,128)(2,1)}, bf16[1,1024,512]{1,2,0:T(8,128)(2,1)S(1)}, u32[]{:S(2)}) copy-start(bf16[1,1024,512]{1,2,0:T(8,128)(2,1)S(1)} %copy.321) | copy-start | bytes 3145732
  65.7 75.7 %copy-start.20 = (f32[1024]{0:T(1024)}, f32[1024]{0:T(1024)S(1)}, u32[]{:S(2)}) copy-start(f32[1024]{0:T(1024)S(1)} %broadcast_multiply_fusion.5) | copy-start | bytes 12292
  66.6 74.8 %copy-start.22 = (f32[1024]{0:T(1024)}, f32[1024]{0:T(1024)S(1)}, u32[]{:S(2)}) copy-start(f32[1024]{0:T(1024)S(1)} %add_rsqrt_fusion.1) | copy-start | bytes 12292
  83.8 5.2 copy-start.2
  100.6 58.1 %copy-start.13 = (bf16[512,2,256]{0,2,1:T(8,128)(2,1)}, bf16[512,2,256]{0,2,1:T(8,128)(2,1)S(1)}, u32[]{:S(2)}) copy-start(bf16[512,2,256]{0,2,1:T(8,128)(2,1)S(1)} %copy.270) | copy-start | bytes 1572868
  110.6 16.5 %copy-start.8 = (bf16[1024,512]{0,1:T(8,128)(2,1)}, bf16[1024,512]{0,1:T(8,128)(2,1)S(1)}, u32[]{:S(2)}) copy-start(bf16[1024,512]{0,1:T(8,128)(2,1)S(1)} %convolution_convert_fusion.4) | copy-start | bytes 3145732
  113.0 14.2 %copy-start.10 = (bf16[1024,512]{0,1:T(8,128)(2,1)}, bf16[1024,512]{0,1:T(8,128)(2,1)S(1)}, u32[]{:S(2)}) copy-start(bf16[1024,512]{0,1:T(8,128)(2,1)S(1)} %add_convert_fusion.2) | copy-start | bytes 3145732
  142.3 16.5 %copy-start.17 = (bf16[1024,512]{0,1:T(8,128)(2,1)}, bf16[1024,512]{0,1:T(8,128)(2,1)S(1)}, u32[]{:S(2)}) copy-start(bf16[1024,512]{0,1:T(8,128)(2,1)S(1)} %add_convert_fusion.3) | copy-start | bytes 3145732
  142.3 18.9 %copy-start.16 = (bf16[512,2,1024]{0,2,1:T(8,128)(2,1)S(1)}, bf16[512,2,1024]{0,2,1:T(8,128)(2,1)}, u32[]{:S(2)}) copy-start(bf16[512,2,1024]{0,2,1:T(8,128)(2,1)} %copy.272) | copy-start | bytes 6291460
  160.8 31.6 %copy-start.5 = (f32[1024,512]{0,1:T(8,128)}, f32[1024,512]{0,1:T(8,128)S(1)}, u32[]{:S(2)}) copy-start(f32[1024,512]{0,1:T(8,128)S(1)} %get-tuple-element.138) | copy-start | bytes 6291460
  161.1 22.0 %copy-start.12 = (bf16[1,1024,512]{1,2,0:T(8,128)(2,1)S(1)}, bf16[1,1024,512]{1,2,0:T(8,128)(2,1)}, u32[]{:S(2)}) copy-start(bf16[1,1024,512]{1,2,0:T(8,128)(2,1)} %copy.322) | copy-start | bytes 3145732
  161.1 22.0 %copy-start.15 = (bf16[2,1024,512]{2,1,0:T(8,128)(2,1)S(1)}, bf16[2,1024,512]{2,1,0:T(8,128)(2,1)}, u32[]{:S(2)}) copy-start(bf16[2,1024,512]{2,1,0:T(8,128)(2,1)} %copy.275) | copy-start | bytes 6291460
  161.2 22.0 %copy-start.24 = (f32[1024]{0:T(1024)S(1)}, f32[1024]{0:T(1024)}, u32[]{:S(2)}) copy-start(f32[1024]{0:T(1024)} %compare_convert_fusion) | copy-start | bytes 12292
  183.1 5.8 %copy-start.41 = (f32[1024,2048]{1,0:T(8,128)}, f32[1024,2048]{1,0:T(8,128)S(1)}, u32[]{:S(2)}) copy-start(f32[1024,2048]{1,0:T(8,128)S(1)} %get-tuple-element.144) | copy-start | bytes 25165828
  264.7 12.3 %copy-start.9 = (bf16[1024,512]{0,1:T(8,128)(2,1)S(1)}, bf16[1024,512]{0,1:T(8,128)(2,1)}, u32[]{:S(2)}) copy-start(bf16[1024,512]{0,1:T(8,128)(2,1)} %copy-done.8) | copy-start | bytes 3145732
  277.1 16.4 %copy-start.36 = (f32[512]{0:T(512)S(1)}, f32[512]{0:T(512)}, u32[]{:S(2)}) copy-start(f32[512]{0:T(512)} %add.161) | copy-start | bytes 6148
  293.4 31.5 %copy-start.4 = (bf16[1,1024,512]{1,2,0:T(8,128)(2,1)S(1)}, bf16[1,1024,512]{1,2,0:T(8,128)(2,1)}, u32[]{:S(2)}) copy-start(bf16[1,1024,512]{1,2,0:T(8,128)(2,1)} %copy-done.3) | copy-start | bytes 3145732
  293.4 31.5 %copy-start.21 = (f32[1024]{0:T(1024)S(1)}, f32[1024]{0:T(1024)}, u32[]{:S(2)}) copy-start(f32[1024]{0:T(1024)} %copy-done.20) | copy-start | bytes 12292
  293.4 31.5 %copy-start.23 = (f32[1024]{0:T(1024)S(1)}, f32[1024]{0:T(1024)}, u32[]{:S(2)}) copy-start(f32[1024]{0:T(1024)} %copy-done.22) | copy-start | bytes 12292
  293.4 31.5 %copy-start.27 = (f32[512]{0:T(512)S(1)}, f32[512]{0:T(512)}, u32[]{:S(2)}) copy-start(f32[512]{0:T(512)} %copy-done.26) | copy-start | bytes 6148
  324.9 5.6 %copy-start.19 = (bf16[1,1,1024,512]{2,3,1,0:T(8,128)(2,1)S(1)}, bf16[1,1,1024,512]{2,3,1,0:T(8,128)(2,1)}, u32[]{:S(2)}) copy-start(bf16[1,1,1024,512]{2,3,1,0:T(8,128)(2,1)} %fusion.83) | copy-start | bytes 3145732
  332.0 10.7 %copy-start.35 = (f32[512]{0:T(512)S(1)}, f32[512]{0:T(512)}, u32[]{:S(2)}) copy-start(f32[512]{0:T(512)} %copy-done.34) | copy-start | bytes 6148
  336.0 176.7 %reduce-scatter.2.cloned.1.call-start = ((), (), s32[]{:S(2)}) async-start(), calls=%async_computation.2 | async-start | bytes 6488064 | tf_op jit(solution)/shard_map/reduce_scatter | solution.py:379
  342.7 15.2 %copy-start.33 = (f32[512]{0:T(512)S(1)}, f32[512]{0:T(512)}, u32[]{:S(2)}) copy-start(f32[512]{0:T(512)} %copy-done.32) | copy-start | bytes 6148
  420.9 94.8 %copy-start.1 = (s32[2,1024]{1,0:T(2,128)S(1)}, s32[2,1024]{1,0:T(2,128)}, u32[]{:S(2)}) copy-start(s32[2,1024]{1,0:T(2,128)} %param.24) | copy-start | bytes 24580
  (13 other events, 50.0 us)
Sparse Core Ops, SparseCore 0:
  11.5 72.2 all-gather.6
  336.1 55.8 all-gather.4
  397.6 115.0 reduce-scatter.1

commit v2 on v1

--- a/solution.py
+++ b/solution.py
@@ -1,12 +1,311 @@
+import functools
 import math
 
 import jax
 import jax.numpy as jnp
 from jax import lax
+from jax.experimental import pallas as pl
+from jax.experimental.pallas import tpu as pltpu
 from jax.sharding import PartitionSpec as P
 
 epsilon = 1e-05
 masked_value = -1e30
+TILE = 256
+FULL = pl.BlockSpec(memory_space=pltpu.VMEM)
+
+GAIN1, SHIFT1, GAIN2, SHIFT2, BQ, BV, BO1, BO2 = range(8)
+
+
+def dot(left, right):
+    return jnp.dot(left, right, preferred_element_type=jnp.float32)
+
+
+def dot_last(left, right):
+    return lax.dot_general(left, right, (((1,), (1,)), ((), ())), preferred_element_type=jnp.float32)
+
+
+def dot_first(left, right):
+    return lax.dot_general(left, right, (((0,), (0,)), ((), ())), preferred_element_type=jnp.float32)
+
+
+def tile_rows(index):
+    return pl.ds(pl.multiple_of(index * TILE, TILE), TILE)
+
+
+def statistics(values):
+    centred = values - jnp.mean(values, axis=-1, keepdims=True)
+    inverse = lax.rsqrt(jnp.mean(centred * centred, axis=-1, keepdims=True) + epsilon)
+    return centred * inverse, inverse
+
+
+def norm_back(grad, scaled, inverse, gain):
+    inner = grad * gain
+    return inverse * (
+        inner - jnp.mean(inner, axis=-1, keepdims=True) - scaled * jnp.mean(inner * scaled, axis=-1, keepdims=True)
+    )
+
+
+def add_row(ref, row, values):
+    ref[row : row + 1, :] += jnp.sum(values, axis=0, keepdims=True)
+
+
+def qkv_phase(x, w_mix, vecs, h1t, query, key, value):
+    halves, quarter = query.shape[0], query.shape[2]
+    scale = 1.0 / math.sqrt(64)
+
+    def step(tile, _):
+        rows = tile_rows(tile)
+        scaled, _ = statistics(x[rows, :].astype(jnp.float32))
+        hidden = (scaled * vecs[GAIN1 : GAIN1 + 1, :] + vecs[SHIFT1 : SHIFT1 + 1, :]).astype(jnp.bfloat16)
+        h1t[:, rows] = hidden.T
+        for half in range(halves):
+            cols = slice(half * quarter, (half + 1) * quarter)
+            part = lambda c: dot(hidden, w_mix[half, :, c * quarter : (c + 1) * quarter])
+            query[half, rows, :] = ((part(0) + vecs[BQ : BQ + 1, cols]).astype(jnp.bfloat16) * scale).astype(jnp.bfloat16)
+            key[half, rows, :] = part(1).astype(jnp.bfloat16)
+            value[half, rows, :] = (part(2) + vecs[BV : BV + 1, cols]).astype(jnp.bfloat16)
+        return 0
+
+    lax.fori_loop(0, x.shape[0] // TILE, step, 0)
+
+
+def attend_phase(query, key, value, marks_row, marks_col, bias, mixed, logs):
+    halves, slots, quarter = query.shape
+
+    def tile_step(tile, _):
+        rows = tile_rows(tile)
+        same = marks_col[rows, 0:1] == marks_row[1:2, :]
+        here = lax.broadcasted_iota(jnp.int32, (TILE, slots), 0) + tile * TILE
+        there = lax.broadcasted_iota(jnp.int32, (TILE, slots), 1)
+        bias[...] = jnp.where(same | (here == there), 0.0, masked_value)
+
+        def half_step(half, _):
+            lane = lax.broadcasted_iota(jnp.int32, (TILE, 128), 1)
+            stats = jnp.zeros((TILE, 128), jnp.float32)
+            for pair in range(quarter // 128):
+                cols = slice(pair * 128, (pair + 1) * 128)
+                both = query[half, rows, cols]
+                keys = key[half, :, cols]
+                values = value[half, :, cols]
+                sums = []
+                for side in range(2):
+                    mine = (lane < 64) if side == 0 else (lane >= 64)
+                    scores = dot_last(jnp.where(mine, both, jnp.zeros_like(both)), keys) + bias[...]
+                    top = jnp.max(scores, axis=1, keepdims=True)
+                    expo = jnp.exp(scores - top)
+                    total = jnp.sum(expo, axis=1, keepdims=True)
+                    sums.append(dot(expo.astype(jnp.bfloat16), values) * (1.0 / total))
+                    stats = jnp.where(lane == pair * 2 + side, top + jnp.log(total), stats)
+                mixed[half, rows, cols] = jnp.where(lane < 64, sums[0], sums[1]).astype(jnp.bfloat16)
+            logs[half, :, rows] = stats.T[0:4, :]
+            return 0
+
+        lax.fori_loop(0, halves, half_step, 0)
+        return 0
+
+    lax.fori_loop(0, slots // TILE, tile_step, 0)
+
+
+def middle_phase(x, cot, live_col, w_up, w_down, w_mix, vecs, b_up, mixed, h2t, glowt, glow2t, act, gpre, gmix, dots, out, gres, sums, sums_up):
+    halves, quarter, hidden_half = mixed.shape[0], mixed.shape[2], w_up.shape[2]
+
+    def step(tile, _):
+        rows = tile_rows(tile)
+        attn = sum(dot_last(mixed[half, rows, :], w_mix[half, :, 3 * quarter : 4 * quarter]) for half in range(halves))
+        resid = x[rows, :].astype(jnp.float32) + attn + vecs[BO1 : BO1 + 1, :]
+        scaled, inverse = statistics(resid)
+        hidden = (scaled * vecs[GAIN2 : GAIN2 + 1, :] + vecs[SHIFT2 : SHIFT2 + 1, :]).astype(jnp.bfloat16)
+        h2t[:, rows] = hidden.T
+        grad_out = cot[rows, :].astype(jnp.float32) * live_col[rows, 2:3]
+        grad_low = grad_out.astype(jnp.bfloat16)
+        glowt[:, rows] = grad_low.T
+        ffn = jnp.zeros(resid.shape, jnp.float32)
+        grad_two = jnp.zeros(resid.shape, jnp.float32)
+        for half in range(halves):
+            pre = dot(hidden, w_up[half]) + b_up[half : half + 1, :]
+            cdf = 0.5 * (1.0 + lax.erf(pre * 0.7071067811865476))
+            slope = cdf + pre * (jnp.exp(-0.5 * pre * pre) * 0.3989422804014327)
+            active = (pre * cdf).astype(jnp.bfloat16)
+            act[half, rows, :] = active
+            ffn += dot_last(active, w_down[half])
+            grad_pre = (dot(grad_low, w_down[half]) * slope).astype(jnp.bfloat16)
+            gpre[half, rows, :] = grad_pre
+            grad_two += dot_last(grad_pre, w_up[half])
+            add_row(sums_up, half, grad_pre.astype(jnp.float32))
+        out[rows, :] = (resid + ffn + vecs[BO2 : BO2 + 1, :]).astype(out.dtype)
+        add_row(sums, GAIN2, grad_two * scaled)
+        add_row(sums, SHIFT2, grad_two)
+        grad_resid = grad_out + norm_back(grad_two, scaled, inverse, vecs[GAIN2 : GAIN2 + 1, :])
+        add_row(sums, BO1, grad_resid)
+        add_row(sums, BO2, grad_out)
+        gres[rows, :] = grad_resid
+        low = grad_resid.astype(jnp.bfloat16)
+        glow2t[:, rows] = low.T
+        for half in range(halves):
+            grad_mixed = dot(low, w_mix[half, :, 3 * quarter : 4 * quarter]).astype(jnp.bfloat16)
+            gmix[half, rows, :] = grad_mixed
+            both = grad_mixed.astype(jnp.float32) * mixed[half, rows, :].astype(jnp.float32)
+            dots[half, :, rows] = jnp.sum(both.T.reshape(quarter // 64, 64, TILE), axis=1)
+        return 0
+
+    sums[...] = jnp.zeros_like(sums)
+    sums_up[...] = jnp.zeros_like(sums_up)
+    lax.fori_loop(0, x.shape[0] // TILE, step, 0)
+
+
+def weight_phase(left_t, right, grads, where):
+    halves, _, columns = right.shape
+    chunk = min(columns, 512)
+
+    def step(half, _):
+        for start in range(0, columns, chunk):
+            cols = slice(start, start + chunk)
+            grads[where, half, :, cols] = dot(left_t[...], right[half, :, cols]).astype(jnp.bfloat16)
+        return 0
+
+    lax.fori_loop(0, halves, step, 0)
+
+
+def output_weight_phase(glow2t, mixed, grads):
+    halves, _, quarter = mixed.shape
+
+    def step(half, _):
+        grads[2, half, :, 3 * quarter : 4 * quarter] = dot(glow2t[...], mixed[half]).astype(jnp.bfloat16)
+        return 0
+
+    lax.fori_loop(0, halves, step, 0)
+
+
+def attend_back_phase(query, key, value, gmix, marks_row, marks_col, bias, logs, dots, grad_query, grad_key, grad_value):
+    halves, slots, quarter = query.shape
+    grad_query[...] = jnp.zeros_like(grad_query)
+
+    def tile_step(tile, _):
+        rows = tile_rows(tile)
+        same = marks_col[rows, 1:2] == marks_row[0:1, :]
+        here = lax.broadcasted_iota(jnp.int32, (TILE, slots), 0) + tile * TILE
+        there = lax.broadcasted_iota(jnp.int32, (TILE, slots), 1)
+        bias[...] = jnp.where(same | (here == there), 0.0, masked_value)
+
+        def half_step(half, _):
+            for pair in range(quarter // 128):
+                cols = slice(pair * 128, (pair + 1) * 128)
+                queries, grads = query[half, :, cols], gmix[half, :, cols]
+                keys, values = key[half, rows, cols], value[half, rows, cols]
+                lane = lax.broadcasted_iota(jnp.int32, (TILE, 128), 1)
+                wide = lax.broadcasted_iota(jnp.int32, (slots, 128), 1)
+                parts = []
+                for side in range(2):
+                    head = pair * 2 + side
+                    mine = (lane < 64) if side == 0 else (lane >= 64)
+                    zero = jnp.zeros_like(keys)
+                    scores = dot_last(jnp.where(mine, keys, zero), queries) + bias[...]
+                    probs = jnp.exp(scores - logs[half, head : head + 1, :])
+                    grad_probs = dot_last(jnp.where(mine, values, zero), grads)
+                    grad_scores = (probs * (grad_probs - dots[half, head : head + 1, :])).astype(jnp.bfloat16)
+                    parts.append(
+                        (dot(probs.astype(jnp.bfloat16), grads), dot(grad_scores, queries), dot_first(grad_scores, keys))
+                    )
+                grad_value[half, rows, cols] = jnp.where(lane < 64, parts[0][0], parts[1][0]).astype(jnp.bfloat16)
+                grad_key[half, rows, cols] = jnp.where(lane < 64, parts[0][1], parts[1][1]).astype(jnp.bfloat16)
+                grad_query[half, :, cols] += jnp.where(wide < 64, parts[0][2], parts[1][2])
+            return 0
+
+        lax.fori_loop(0, halves, half_step, 0)
+        return 0
+
+    lax.fori_loop(0, slots // TILE, tile_step, 0)
+
+
+def input_phase(x, w_mix, vecs, grad_query, grad_low, grad_key, grad_value, gres, sums, grad_x):
+    halves, slots, quarter = grad_key.shape
+    scale = 1.0 / math.sqrt(64)
+
+    def step(tile, _):
+        rows = tile_rows(tile)
+        scaled, inverse = statistics(x[rows, :].astype(jnp.float32))
+        grad_one = jnp.zeros((TILE, x.shape[1]), jnp.float32)
+        for half in range(halves):
+            cols = slice(half * quarter, (half + 1) * quarter)
+            low = (grad_query[half, rows, :] * scale).astype(jnp.bfloat16)
+            grad_low[half, rows, :] = low
+            three = (low, grad_key[half, rows, :], grad_value[half, rows, :])
+            for c in range(3):
+                grad_one += dot_last(three[c], w_mix[half, :, c * quarter : (c + 1) * quarter])
+            sums[BQ : BQ + 1, cols] += jnp.sum(three[0].astype(jnp.float32), axis=0, keepdims=True)
+            sums[BV : BV + 1, cols] += jnp.sum(three[2].astype(jnp.float32), axis=0, keepdims=True)
+        add_row(sums, GAIN1, grad_one * scaled)
+        add_row(sums, SHIFT1, grad_one)
+        grad_x[rows, :] = (gres[rows, :] + norm_back(grad_one, scaled, inverse, vecs[GAIN1 : GAIN1 + 1, :])).astype(grad_x.dtype)
+        return 0
+
+    lax.fori_loop(0, slots // TILE, step, 0)
+
+
+def qkv_weight_phase(h1t, grad_query, grad_key, grad_value, grads):
+    halves, _, quarter = grad_key.shape
+
+    def step(half, _):
+        for c, ref in enumerate((grad_query, grad_key, grad_value)):
+            grads[2, half, :, c * quarter : (c + 1) * quarter] = dot(h1t[...], ref[half]).astype(jnp.bfloat16)
+        return 0
+
+    lax.fori_loop(0, halves, step, 0)
+
+
+def compute_kernel(x, cot, weights, vecs, b_up, marks_row, out, grad_x, grads, sums, sums_up,
+                   h1t, query, key, value, bias, mixed, logs, h2t, glowt, glow2t, act, gpre, gmix, dots, gres,
+                   gq_wide, gq, gk, gv, marks_col):
+    marks_col[...] = marks_row[...].T
+    w_up, w_down, w_mix = weights.at[0], weights.at[1], weights.at[2]
+    qkv_phase(x, w_mix, vecs, h1t, query, key, value)
+    attend_phase(query, key, value, marks_row, marks_col, bias, mixed, logs)
+    middle_phase(x, cot, marks_col, w_up, w_down, w_mix, vecs, b_up, mixed, h2t, glowt, glow2t, act, gpre, gmix, dots, out, gres, sums, sums_up)
+    weight_phase(h2t, gpre, grads, 0)
+    weight_phase(glowt, act, grads, 1)
+    output_weight_phase(glow2t, mixed, grads)
+    attend_back_phase(query, key, value, gmix, marks_row, marks_col, bias, logs, dots, gq_wide, gk, gv)
+    input_phase(x, w_mix, vecs, gq_wide, gq, gk, gv, gres, sums, grad_x)
+    qkv_weight_phase(h1t, gq, gk, gv, grads)
+
+
+def compute_scratch(slots, width, hidden):
+    half = (2, slots, width // 2)
+    bf, f32 = jnp.bfloat16, jnp.float32
+    V = pltpu.VMEM
+    return [
+        V((width, slots), bf), V(half, bf), V(half, bf), V(half, bf), V((TILE, slots), f32), V(half, bf),
+        V((2, 4, slots), f32), V((width, slots), bf), V((width, slots), bf), V((width, slots), bf),
+        V((2, slots, hidden // 2), bf), V((2, slots, hidden // 2), bf), V(half, bf), V((2, 4, slots), f32),
+        V((slots, width), f32), V(half, f32), V(half, bf), V(half, bf), V(half, bf), V((slots, 8), f32),
+    ]
+
+
+def compute(x, cot, weights, vecs, b_up, marks_row):
+    slots, width = x.shape
+    hidden = b_up.shape[0] * b_up.shape[1]
+    bf, f32 = jnp.bfloat16, jnp.float32
+    return pl.pallas_call(
+        compute_kernel,
+        out_shape=(
+            jax.ShapeDtypeStruct((slots, width), bf),
+            jax.ShapeDtypeStruct((slots, width), bf),
+            jax.ShapeDtypeStruct(weights.shape, bf),
+            jax.ShapeDtypeStruct((8, width), f32),
+            jax.ShapeDtypeStruct(b_up.shape, f32),
+        ),
+        in_specs=[FULL] * 6,
+        out_specs=(FULL,) * 5,
+        scratch_shapes=compute_scratch(slots, width, hidden),
+        compiler_params=pltpu.CompilerParams(vmem_limit_bytes=67043328),
+    )(x, cot, weights, vecs, b_up, marks_row)
+
+
+def marks_of(chain, keep):
+    label = chain.astype(jnp.float32)
+    live = (chain >= 0).astype(jnp.float32)
+    as_key = jnp.where(keep == 1, label, -2.0)
+    return jnp.stack([label, as_key, live, live, live, live, live, live])
 
 
 def product(left, right):
@@ -311,14 +610,30 @@
     )
 
 
+def fits(mesh):
+    return mesh.shape["mp"] == 2
+
+
 def cat_weights(w_qkv, w_o, w_up, w_down):
     mixed_part = jnp.concatenate([w_qkv[0], w_qkv[1], w_qkv[2], w_o.T], axis=1)
     return jnp.stack([w_up, w_down.T, mixed_part])
 
 
 def cat_small(b_qv, b_up, out_bias, norm_gain, norm_bias):
-    parts = [b_qv.reshape(-1), b_up.reshape(-1), out_bias.reshape(-1), norm_gain.reshape(-1), norm_bias.reshape(-1)]
-    return jnp.concatenate(parts)
+    parts = [b_qv, b_up, norm_gain, norm_bias, out_bias]
+    return jnp.concatenate([part.reshape(-1) for part in parts])
+
+
+def spread_small(smalls, b_qv, b_up):
+    mp, dp = smalls.shape[:2]
+    n0, n1 = b_qv.size, b_qv.size + b_up.size
+    qv = smalls[:, :, :n0].reshape(mp, dp, 2, b_qv.shape[1], b_qv.shape[2])
+    qv = qv.transpose(2, 0, 3, 1, 4).reshape(2, -1)
+    up = smalls[:, :, n0:n1].reshape(mp, dp, b_up.shape[0], b_up.shape[1]).transpose(0, 2, 1, 3).reshape(mp, -1)
+    rest = smalls[0, :, n1:].reshape(dp, 3, 2, -1).transpose(1, 2, 0, 3).reshape(6, -1)
+    gain, shift, bias = rest[0:2], rest[2:4], rest[4:6]
+    vecs = jnp.stack([gain[0], shift[0], gain[1], shift[1], qv[0], qv[1], bias[0], bias[1]])
+    return vecs, up
 
 
 def body_split(
@@ -339,66 +654,43 @@
     own = lax.axis_index("mp")
     mp = lax.axis_size("mp")
     dp = lax.axis_size("dp")
-    width = out_bias.shape[1] * dp
-    local_heads, local_hd = b_qv.shape[1], b_qv.shape[2]
     packed = cat_weights(w_qkv, w_o, w_up, w_down)
     small = cat_small(b_qv, b_up, out_bias, norm_gain, norm_bias)
+    depth = packed.shape[1]
     full = lax.all_gather(packed, ("mp", "dp"), axis=0, tiled=False)
-    full = full.reshape(mp, dp, 3, -1, packed.shape[2])
-    full = full.transpose(2, 0, 1, 3, 4).reshape(3, mp, width, packed.shape[2])
+    full = full.reshape(mp, dp, 3, depth, -1).transpose(2, 0, 1, 3, 4).reshape(3, mp, dp * depth, -1)
     smalls = lax.all_gather(small, ("mp", "dp"), axis=0, tiled=False).reshape(mp, dp, -1)
-    sizes = [b_qv.size, b_up.size, out_bias.size, norm_gain.size, norm_bias.size]
-    offs = [0]
-    for s in sizes:
-        offs.append(offs[-1] + s)
-    piece = lambda k: smalls[:, :, offs[k] : offs[k + 1]]
-    bias_qv = piece(0).reshape(mp, dp, 2, local_heads, local_hd).transpose(2, 0, 3, 1, 4).reshape(2, mp * local_heads, dp * local_hd)
-    bias_up = piece(1).reshape(mp, dp, b_up.shape[0], b_up.shape[1]).transpose(0, 2, 1, 3).reshape(mp * b_up.shape[0], -1)
-    vec = lambda k: piece(k)[0].reshape(dp, 2, -1).transpose(1, 0, 2).reshape(2, width)
-    bias_out, gain_full, shift_full = vec(2), vec(3), vec(4)
-    q4 = packed.shape[2] // 4
-    pick = lambda c: full[2, :, :, c * q4 : (c + 1) * q4].transpose(1, 0, 2).reshape(width, mp * q4)
-    qkv_full = jnp.stack([pick(0), pick(1), pick(2)])
-    out_full = pick(3).T
-    up_full = full[0].transpose(1, 0, 2).reshape(width, -1)
-    down_full = full[1].transpose(0, 2, 1).reshape(-1, width)
-    weights = (qkv_full, out_full, up_full, down_full, bias_qv, bias_up, bias_out, gain_full, shift_full)
+    vecs, up_bias = spread_small(smalls.astype(jnp.float32), b_qv, b_up)
     take = lambda a: lax.dynamic_index_in_dim(a, own, 0, keepdims=False)
-    chain_rows = take(chain_ids)
-    result, kept = forward(take(activations).astype(jnp.float32), chain_rows, take(key_keep), weights)
-    live_rows = (chain_rows >= 0).astype(jnp.float32)[:, None]
-    output_rows, grad_in, grads = backward(take(cotangent).astype(jnp.float32) * live_rows, result, kept, weights)
-    both = jnp.stack([output_rows, grad_in]).astype(jnp.bfloat16)
-    gathered = lax.all_gather(both, "mp", axis=0, tiled=False).astype(jnp.float32)
-    g_qkv, g_o, g_up, g_down, g_bqv, g_bup, g_bias, g_gain, g_shift = grads
-    halves = lambda a: a.reshape(a.shape[0], mp, -1).transpose(1, 0, 2)
-    g_mix = jnp.concatenate([halves(g_qkv[0]), halves(g_qkv[1]), halves(g_qkv[2]), halves(g_o.T)], axis=2)
-    g_all = jnp.stack([halves(g_up), halves(g_down.T), g_mix]).astype(jnp.bfloat16)
-    g_all = g_all.reshape(3, mp, dp, width // dp, -1).transpose(1, 2, 0, 3, 4)
-    g_all = g_all.reshape(mp * dp, 3, width // dp, -1)
+    marks = marks_of(take(chain_ids), take(key_keep))
+    out, grad_x, grads, sums, sums_up = compute(
+        take(activations), take(cotangent), full, vecs, up_bias, marks
+    )
+    gathered = lax.all_gather(jnp.stack([out, grad_x]), "mp", axis=0, tiled=False).astype(jnp.float32)
+    g_all = grads.reshape(3, mp, dp, depth, -1).transpose(1, 2, 0, 3, 4).reshape(mp * dp, 3, depth, -1)
     g_own = lax.psum_scatter(g_all, ("mp", "dp"), scatter_dimension=0, tiled=False).astype(jnp.float32)
-    s_qv = g_bqv.reshape(2, mp, local_heads, dp, local_hd).transpose(1, 3, 0, 2, 4).reshape(mp, dp, -1)
-    s_up = g_bup.reshape(mp, b_up.shape[0], dp, b_up.shape[1]).transpose(0, 2, 1, 3).reshape(mp, dp, -1)
-    rep = lambda a: jnp.broadcast_to(a.reshape(2, dp, -1).transpose(1, 0, 2).reshape(1, dp, -1), (mp, dp, 2 * width // dp))
-    s_all = jnp.concatenate([s_qv, s_up, rep(g_bias), rep(g_gain), rep(g_shift)], axis=2)
-    s_all = s_all.reshape(mp * dp, -1)
-    s_sum = lax.psum(s_all, ("mp", "dp"))
-    s_own = lax.dynamic_index_in_dim(s_sum, own * dp + lax.axis_index("dp"), 0, keepdims=False)
-    part = lambda k, a: s_own[offs[k] : offs[k + 1]].reshape(a.shape)
-    mix = g_own[2]
+    total = lax.psum(jnp.concatenate([sums.reshape(-1), sums_up.reshape(-1)]), ("mp", "dp"))
+    s_vec, s_up = total[: sums.size].reshape(sums.shape), total[sums.size :].reshape(sums_up.shape)
+    at = lax.axis_index("dp")
+    pick = lambda a, axis: lax.dynamic_index_in_dim(a, at, axis, keepdims=False)
+    pairs = lambda r0, r1: pick(jnp.stack([s_vec[r0], s_vec[r1]]).reshape(2, dp, -1), 1)
+    s_qv = pick(take(s_vec[BQ : BV + 1].reshape(2, mp, -1).transpose(1, 0, 2)).reshape(2, b_qv.shape[1], dp, -1), 2)
+    s_bup = pick(take(s_up).reshape(b_up.shape[0], dp, -1), 1)
+    mix, quarter = g_own[2], packed.shape[2] // 4
     return (
         gathered[:, 0],
         gathered[:, 1],
-        jnp.stack([mix[:, c * q4 : (c + 1) * q4] for c in range(3)]),
-        mix[:, 3 * q4 :].T,
+        jnp.stack([mix[:, c * quarter : (c + 1) * quarter] for c in range(3)]),
+        mix[:, 3 * quarter :].T,
         g_own[0],
         g_own[1].T,
-        part(0, b_qv),
-        part(1, b_up),
-        part(2, out_bias),
-        part(3, norm_gain),
-        part(4, norm_bias),
-    )
+        s_qv,
+        s_bup,
+        pairs(BO1, BO2),
+        pairs(GAIN1, GAIN2),
+        pairs(SHIFT1, SHIFT2),
+    )
+
 
 def solution(mesh):
     placed = (
@@ -416,7 +708,7 @@
         P(None, "dp"),
         P(None, "dp"),
     )
-    body = body_split if mesh.shape["mp"] == 2 else body_generic
+    body = body_split if fits(mesh) else body_generic
     return jax.shard_map(
         body,
         mesh=mesh,

time: 532 us -> 359 us (0.67); the launches traced: 523 us -> 358 us
  matrix products: 179 us -> 0 us
  Pallas kernels: 0 us -> 78.4 us
  local copies, waits for them, and re-layouts: 86.6 us -> 35.6 us
  other arithmetic: 58.2 us -> 14.2 us
  waiting for transfers between devices: 99.7 us -> 133 us
    dot_general x20 -> x0, matrix products: 179 us -> none  [the longest x12 77.4 us: product(): return jnp.dot(left, right, preferred_element_type=jnp.float32)]
    pallas_call x0 -> x1, Pallas kernels: none -> 78.4 us  [compute(): pl.pallas_call(compute_kernel, out_shape=(jax.ShapeDtypeStruct((slots, wi...]
    reduce_scatter x1, waiting for transfers between devices: 84 us -> 113 us  [body_split(): lax.psum_scatter(g_all, ('mp', 'dp'), scatter_dimension=0, tiled=False)]
    convert_element_type x6 -> x3, other arithmetic: 32.9 us -> 4.78 us  [the longest x1 3.37 us: body_split(): lax.all_gather(jnp.stack([out, grad_x]), 'mp', axis=0, tiled=False)]
    reduce_sum x5 -> x0, other arithmetic: 16.7 us -> none  [the longest x1 14.2 us: forward(): jnp.sum(jnp.exp(scores - row_top), axis=-1, keepdims=True)]
    another operation x18 -> x10, local copies, waits for them, and re-layouts: 18.5 us -> 1.94 us  [the longest x1 0.67 us: marks_of(): return jnp.stack([label, as_key, live, live, live, live, live, live])]
    transpose x18 -> x3, local copies, waits for them, and re-layouts: 23.4 us -> 8.07 us  [the longest x1 7.18 us: body_split(): grads.reshape(3, mp, dp, depth, -1).transpose(1, 2, 0, 3, 4)]
    dot_general x1 -> x0, local copies, waits for them, and re-layouts: 6.69 us -> none  [product(): return jnp.dot(left, right, preferred_element_type=jnp.float32)]
  transfers between devices with their start and end apart: 3 -> 3, of which waited for: 2 -> 3; matrix products, arithmetic and copies ran while one was open for 13% -> 9% of each run, Pallas kernels for 0% -> 0%
where the time goes in v2:
time: 359 us; the launch traced here: 358 us
  waiting for transfers between devices  133 us (37%)
  blocking collectives  82.8 us (23%)
  Pallas kernels  78.4 us (22%)
  local copies, waits for them, and re-layouts  35.6 us (10%)
  between operations  14.5 us (4%)
  other arithmetic  14.2 us (4%)
    reduce_scatter x1, waiting for transfers between devices, body_split(): lax.psum_scatter(g_all, ('mp', 'dp'), scatter_dimension=0, tiled=False)  113 us
    pallas_call x1, Pallas kernels, compute(): pl.pallas_call(compute_kernel, out_shape=(jax.ShapeDtypeStruct((slots, wi...  78.4 us
    unnamed x1, blocking collectives  42.3 us
    psum x1, blocking collectives, body_split(): lax.psum(jnp.concatenate([sums.reshape(-1), sums_up.reshape(-1)]), ('mp',...  40.5 us
    all_gather x1, waiting for transfers between devices, body_split(): full = lax.all_gather(packed, ('mp', 'dp'), axis=0, tiled=False)  15.2 us
    transpose x1, local copies, waits for them, and re-layouts, body_split(): grads.reshape(3, mp, dp, depth, -1).transpose(1, 2, 0, 3, 4)  7.18 us
  transfers between devices with their start and end apart: 3, of which 3 were waited for; matrix products, arithmetic and copies ran while one was open for 9% of the time, Pallas kernels for 0%

profile of v2, /device:TPU:0, one launch (start us, length us, event | category | flops | bytes accessed | tf_op | source)
XLA Modules:
  0.0 358.3 jit_solution(2915950676793201004)
XLA Ops:
  7.2 0.8 slice_bitcast_fusion.11
  8.0 0.7 maximum_bitcast_fusion
  8.7 1.6 pad_maximum_fusion.1
  10.4 0.8 copy.51
  11.2 0.8 reshape.179
  12.0 0.7 reshape.181
  12.7 0.7 reshape.182
  13.5 0.7 reshape.183
  14.2 1.2 dynamic-slice.4
  16.4 42.3 %all-reduce = bf16[9216]{0:T(1024)(128)(2,1)S(1)} all-reduce(bf16[9216]{0:T(1024)(128)(2,1)S(1)} %dynamic-update-slice), channel_id=3, replica_groups=mesh['dp'=16,'mp'=2] {'mp','dp'}, use_global_device_ids=true, to_apply=%add | all-reduce | flops 9216 | bytes 36864
  60.7 0.8 reshape.186.b_up
  61.4 0.7 compare_convert_fusion
  62.1 0.7 fusion.1
  62.8 0.7 compare_select_fusion
  63.6 0.7 stack.73.marks_row
  64.2 0.6 stack.72.vecs
  64.9 3.0 dynamic-slice_bitcast_fusion
  67.9 15.2 %all-gather.6.cloned.1.call-done = bf16[96,32,1024]{2,1,0:T(8,128)(2,1)} async-done(((bf16[3,32,1024]{2,1,0:T(8,128)(2,1)}), bf16[96,32,1024]{2,1,0:T(8,128)(2,1)}) %all-gather.6.cloned.1.call-update) | async-done | bytes 6291472 | tf_op jit(solution)/shard_map/all_gather | solution.py:660
  83.1 6.8 %copy.50 = bf16[2,16,3,32,1024]{4,3,1,0,2:T(8,128)(2,1)} copy(bf16[2,16,3,32,1024]{4,3,2,1,0:T(8,128)(2,1)} %bitcast.83) | data formatting | bytes 12582912 | tf_op jit(solution)/shard_map/reshape | solution.py:661
  89.9 78.4 %shard_map.212 = (bf16[1024,512]{1,0:T(8,128)(2,1)}, bf16[1024,512]{1,0:T(8,128)(2,1)}, bf16[3,2,512,1024]{3,2,1,0:T(8,128)(2,1)}, f32[8,512]{1,0:T(8,128)}, f32[2,1024]{1,0:T(2,128)}) custom-call(bf16[1024,512]{1,0:T(8,128)(2,1)} %get-tuple-element.48.x, bf16[1024,512]{1,0:T(8,128)(2,1)} %get-tuple-element.47.cot, bf16[3,2,512,1024]{3,2,1,0:T(8,128)(2,1)} %bitcast.82, ...), custom_call_target="tpu_custom_call" | custom-call | tf_op jit(solution)/shard_map/pallas_call | solution.py:288
  168.3 3.1 pad_maximum_fusion
  171.4 7.2 %copy.59 = bf16[2,16,3,32,1024]{4,3,2,1,0:T(8,128)(2,1)} copy(bf16[2,16,3,32,1024]{4,3,1,0,2:T(8,128)(2,1)} %bitcast.84) | data formatting | bytes 12582912 | tf_op jit(solution)/shard_map/transpose | solution.py:670
  178.6 0.7 copy-done
  179.3 40.5 %psum.7 = f32[6144]{0:T(1024)S(1)} all-reduce(f32[6144]{0:T(1024)S(1)} %pad_maximum_fusion.3), channel_id=1, replica_groups=mesh['dp'=16,'mp'=2] {'mp','dp'}, use_global_device_ids=true, to_apply=%region_1.2 | all-reduce | flops 6144 | bytes 49152 | tf_op jit(solution)/shard_map/psum | solution.py:672
  220.5 0.7 copy.60
  223.7 4.4 %all-gather.8.cloned.1.call-done = bf16[4,1024,512]{2,1,0:T(8,128)(2,1)} async-done(((bf16[2,1024,512]{2,1,0:T(8,128)(2,1)}), bf16[4,1024,512]{2,1,0:T(8,128)(2,1)}) %all-gather.8.cloned.1.call-update) | async-done | bytes 4194320 | tf_op jit(solution)/shard_map/all_gather | solution.py:669
  228.1 3.4 convert.1
  231.5 4.4 %slice_bitcast_fusion = (f32[2,1024,512]{2,1,0:T(8,128)}, f32[2,1024,512]{2,1,0:T(8,128)}) fusion(f32[2,2,1024,512]{3,2,1,0:T(8,128)S(1)} %convert.1), kind=kLoop, calls=%fused_computation | loop fusion | bytes 16777216 | tf_op jit(solution)/shard_map/squeeze | solution.py:682
  235.9 112.9 %reduce-scatter.2.cloned.1.call-done = bf16[1,3,32,1024]{3,2,1,0:T(8,128)(2,1)} async-done(((bf16[32,3,32,1024]{3,2,1,0:T(8,128)(2,1)}), bf16[1,3,32,1024]{3,2,1,0:T(8,128)(2,1)}) %reduce-scatter.2.cloned.1.call-update) | async-done | bytes 196624 | tf_op jit(solution)/shard_map/reduce_scatter | solution.py:671
  348.8 1.0 convert_element_type.27
  349.7 0.7 slice_bitcast_fusion.2
  351.1 0.6 pad_maximum_fusion.2
  (57 shorter events, 6.2 us)
Async XLA Ops:
  7.2 75.9 %all-gather.6.cloned.1.call-start = ((), (), s32[]{:S(2)}) async-start(), calls=%async_computation.2 | async-start | bytes 6488064 | tf_op jit(solution)/shard_map/all_gather | solution.py:660
  10.3 217.8 %all-gather.8.cloned.1.call-start = ((), (), s32[]{:S(2)}) async-start(), calls=%async_computation.3 | async-start | bytes 6291456 | tf_op jit(solution)/shard_map/all_gather | solution.py:669
  171.4 177.4 %reduce-scatter.2.cloned.1.call-start = ((), (), s32[]{:S(2)}) async-start(), calls=%async_computation.1 | async-start | bytes 6488064 | tf_op jit(solution)/shard_map/reduce_scatter | solution.py:671
  178.6 0.7 copy-start
  178.6 0.7 copy-start.1
Sparse Core Ops, SparseCore 0:
  10.9 72.1 all-gather.5
  171.5 56.5 all-gather.7
  233.7 115.0 reduce-scatter.1

commit v3 on v2

--- a/solution.py
+++ b/solution.py
@@ -69,11 +69,13 @@
     lax.fori_loop(0, x.shape[0] // TILE, step, 0)
 
 
-def attend_phase(query, key, value, marks_row, marks_col, bias, mixed, logs):
+def attend_phase(query, key, value, marks_row, marks_col, bias, mixed, logs, beside):
     halves, slots, quarter = query.shape
 
     def tile_step(tile, _):
         rows = tile_rows(tile)
+        for when, action in beside:
+            pl.when(tile == when)(action)
         same = marks_col[rows, 0:1] == marks_row[1:2, :]
         here = lax.broadcasted_iota(jnp.int32, (TILE, slots), 0) + tile * TILE
         there = lax.broadcasted_iota(jnp.int32, (TILE, slots), 1)
@@ -106,7 +108,7 @@
     lax.fori_loop(0, slots // TILE, tile_step, 0)
 
 
-def middle_phase(x, cot, live_col, w_up, w_down, w_mix, vecs, b_up, mixed, h2t, glowt, glow2t, act, gpre, gmix, dots, out, gres, sums, sums_up):
+def middle_phase(x, cot, live_col, w_up, w_down, w_mix, vecs, b_up, mixed, h2t, glowt, glow2t, act, gpre, gmix, dots, out, gres, sums, sums_up, send):
     halves, quarter, hidden_half = mixed.shape[0], mixed.shape[2], w_up.shape[2]
 
     def step(tile, _):
@@ -146,6 +148,7 @@
             gmix[half, rows, :] = grad_mixed
             both = grad_mixed.astype(jnp.float32) * mixed[half, rows, :].astype(jnp.float32)
             dots[half, :, rows] = jnp.sum(both.T.reshape(quarter // 64, 64, TILE), axis=1)
+        send(tile)
         return 0
 
     sums[...] = jnp.zeros_like(sums)
@@ -176,12 +179,14 @@
     lax.fori_loop(0, halves, step, 0)
 
 
-def attend_back_phase(query, key, value, gmix, marks_row, marks_col, bias, logs, dots, grad_query, grad_key, grad_value):
+def attend_back_phase(query, key, value, gmix, marks_row, marks_col, bias, logs, dots, grad_query, grad_key, grad_value, beside):
     halves, slots, quarter = query.shape
     grad_query[...] = jnp.zeros_like(grad_query)
 
     def tile_step(tile, _):
         rows = tile_rows(tile)
+        for when, action in beside:
+            pl.when(tile == when)(action)
         same = marks_col[rows, 1:2] == marks_row[0:1, :]
         here = lax.broadcasted_iota(jnp.int32, (TILE, slots), 0) + tile * TILE
         there = lax.broadcasted_iota(jnp.int32, (TILE, slots), 1)
@@ -217,9 +222,29 @@
     lax.fori_loop(0, slots // TILE, tile_step, 0)
 
 
-def input_phase(x, w_mix, vecs, grad_query, grad_low, grad_key, grad_value, gres, sums, grad_x):
+def round_phase(wide, low):
+    scale = 1.0 / math.sqrt(64)
+
+    def step(half, _):
+        low[half] = (wide[half] * scale).astype(jnp.bfloat16)
+        return 0
+
+    lax.fori_loop(0, low.shape[0], step, 0)
+
+
+def qkv_weight_phase(h1t, grad_query, grad_key, grad_value, grads):
+    halves, _, quarter = grad_key.shape
+
+    def step(half, _):
+        for c, ref in enumerate((grad_query, grad_key, grad_value)):
+            grads[2, half, :, c * quarter : (c + 1) * quarter] = dot(h1t[...], ref[half]).astype(jnp.bfloat16)
+        return 0
+
+    lax.fori_loop(0, halves, step, 0)
+
+
+def input_phase(x, w_mix, vecs, grad_query, grad_key, grad_value, gres, sums, grad_x, send):
     halves, slots, quarter = grad_key.shape
-    scale = 1.0 / math.sqrt(64)
 
     def step(tile, _):
         rows = tile_rows(tile)
@@ -227,9 +252,7 @@
         grad_one = jnp.zeros((TILE, x.shape[1]), jnp.float32)
         for half in range(halves):
             cols = slice(half * quarter, (half + 1) * quarter)
-            low = (grad_query[half, rows, :] * scale).astype(jnp.bfloat16)
-            grad_low[half, rows, :] = low
-            three = (low, grad_key[half, rows, :], grad_value[half, rows, :])
+            three = (grad_query[half, rows, :], grad_key[half, rows, :], grad_value[half, rows, :])
             for c in range(3):
                 grad_one += dot_last(three[c], w_mix[half, :, c * quarter : (c + 1) * quarter])
             sums[BQ : BQ + 1, cols] += jnp.sum(three[0].astype(jnp.float32), axis=0, keepdims=True)
@@ -237,75 +260,448 @@
         add_row(sums, GAIN1, grad_one * scaled)
         add_row(sums, SHIFT1, grad_one)
         grad_x[rows, :] = (gres[rows, :] + norm_back(grad_one, scaled, inverse, vecs[GAIN1 : GAIN1 + 1, :])).astype(grad_x.dtype)
+        send(tile)
         return 0
 
     lax.fori_loop(0, slots // TILE, step, 0)
 
 
-def qkv_weight_phase(h1t, grad_query, grad_key, grad_value, grads):
-    halves, _, quarter = grad_key.shape
-
-    def step(half, _):
-        for c, ref in enumerate((grad_query, grad_key, grad_value)):
-            grads[2, half, :, c * quarter : (c + 1) * quarter] = dot(h1t[...], ref[half]).astype(jnp.bfloat16)
+class Place:
+    def __init__(self, depth_z):
+        at = lax.axis_index("dp")
+        self.x, self.z, self.y, self.c = lax.axis_index("mp"), at // 4, (at // 2) % 2, at % 2
+        self.count = depth_z
+
+    def other(self, axis):
+        x, z, y, c = self.x, self.z, self.y, self.c
+        x, y, c = (1 - x if axis == "x" else x), (1 - y if axis == "y" else y), (1 - c if axis == "c" else c)
+        return {"dp": z * 4 + y * 2 + c, "mp": x}
+
+    def along(self, hop):
+        z = lax.rem(self.z + hop, self.count)
+        return {"dp": z * 4 + self.y * 2 + self.c, "mp": self.x}, z
+
+
+class Wire:
+    def __init__(self, send, recv):
+        self.send_sems, self.recv_sems = send, recv
+
+    def copy(self, src, dst, number, device):
+        return pltpu.make_async_remote_copy(
+            src_ref=src,
+            dst_ref=dst,
+            send_sem=self.send_sems.at[number],
+            recv_sem=self.recv_sems.at[number],
+            device_id=device,
+            device_id_type=pl.DeviceIdType.MESH,
+        )
+
+
+GATHER_SEMS = 15
+REDUCE_SEMS = 9
+SMALL_SEMS = 7
+
+
+class Gather:
+    def __init__(self, ref, base, wire, place):
+        self.ref, self.base, self.wire, self.place = ref, base, wire, place
+        self.top = pl.ds(0, ref.shape[4] // 2)
+        self.low = pl.ds(ref.shape[4] // 2, ref.shape[4] // 2)
+
+    def own(self, axis, src, number):
+        return self.wire.copy(src, src, self.base + number, self.place.other(axis))
+
+    def z_copies(self):
+        p, ref = self.place, self.ref
+        mine = ref.at[p.x, p.z, p.y, p.c]
+        for hop in range(1, p.count):
+            device, _ = p.along(hop)
+            yield self.wire.copy(mine, mine, self.base + hop - 1, device)
+
+    def second(self):
+        p, ref = self.place, self.ref
+        return (
+            self.own("y", ref.at[p.x, :, p.y, p.c, self.top], 3),
+            self.own("x", ref.at[p.x, :, p.y, p.c, self.low], 4),
+        )
+
+    def third(self):
+        p, ref = self.place, self.ref
+        return (
+            self.own("x", ref.at[p.x, :, :, p.c, self.top], 5),
+            self.own("y", ref.at[:, :, p.y, p.c, self.low], 6),
+        )
+
+    def core(self, step):
+        p, ref = self.place, self.ref
+        if step == 1:
+            return (self.own("c", ref.at[p.x, :, p.y, p.c], 7),)
+        if step == 2:
+            return (
+                self.own("c", ref.at[p.x, :, 1 - p.y, p.c, self.top], 8),
+                self.own("c", ref.at[1 - p.x, :, p.y, p.c, self.low], 9),
+            )
+        return (
+            self.own("c", ref.at[1 - p.x, :, :, p.c, self.top], 10),
+            self.own("c", ref.at[:, :, 1 - p.y, p.c, self.low], 11),
+        )
+
+    def start(self):
+        for copy in self.z_copies():
+            copy.start()
+
+    def after_start(self):
+        for copy in self.z_copies():
+            copy.wait_recv()
+        for copy in self.second() + self.core(1):
+            copy.start()
+
+    def after_second(self):
+        for copy in self.second():
+            copy.wait_recv()
+        for copy in self.third() + self.core(2):
+            copy.start()
+
+    def after_third(self):
+        for copy in self.third():
+            copy.wait_recv()
+        for copy in self.core(3):
+            copy.start()
+
+    def finish(self):
+        for step in (1, 2, 3):
+            for copy in self.core(step):
+                copy.wait_recv()
+
+    def drain(self):
+        for copy in self.z_copies():
+            copy.wait_send()
+        for copy in self.second() + self.third() + self.core(1) + self.core(2) + self.core(3):
+            copy.wait_send()
+
+
+class SmallGather:
+    def __init__(self, ref, base, wire, place):
+        self.ref, self.base, self.wire, self.place = ref, base, wire, place
+
+    def z_copies(self):
+        p = self.place
+        mine = self.ref.at[p.x, p.z, p.y, p.c]
+        return [self.wire.copy(mine, mine, self.base + hop - 1, p.along(hop)[0]) for hop in range(1, p.count)]
+
+    def step(self, axis):
+        p, ref = self.place, self.ref
+        src = {"y": ref.at[p.x, :, p.y, p.c], "x": ref.at[p.x, :, :, p.c], "c": ref.at[:, :, :, p.c]}[axis]
+        return self.wire.copy(src, src, self.base + {"y": 3, "x": 4, "c": 5}[axis], p.other(axis))
+
+
+class Reduce:
+    def __init__(self, grads, from_core, from_a, from_b, from_c, from_d, from_z, base, wire, place):
+        self.grads, self.base, self.wire, self.place = grads, base, wire, place
+        self.from_core, self.from_a, self.from_b = from_core, from_a, from_b
+        self.from_c, self.from_d, self.from_z = from_c, from_d, from_z
+        rows = grads.shape[4]
+        self.top, self.low = pl.ds(0, rows // 2), pl.ds(rows // 2, rows // 2)
+
+    def copies(self, step):
+        p, g, w, base = self.place, self.grads, self.wire, self.base
+        if step == 0:
+            return [w.copy(g.at[:, :, :, 1 - p.c], self.from_core, base, p.other("c"))]
+        if step == 1:
+            return [
+                w.copy(g.at[1 - p.x, :, :, p.c, self.top], self.from_a, base + 1, p.other("x")),
+                w.copy(g.at[:, :, 1 - p.y, p.c, self.low], self.from_b, base + 2, p.other("y")),
+            ]
+        if step == 2:
+            return [
+                w.copy(g.at[p.x, :, 1 - p.y, p.c, self.top], self.from_c, base + 3, p.other("y")),
+                w.copy(g.at[1 - p.x, :, p.y, p.c, self.low], self.from_d, base + 4, p.other("x")),
+            ]
+        out = []
+        for hop in range(1, p.count):
+            device, z = p.along(hop)
+            out.append(w.copy(g.at[p.x, z, p.y, p.c], self.from_z.at[hop - 1], base + 4 + hop, device))
+        return out
+
+    def send(self, step):
+        for copy in self.copies(step):
+            copy.start()
+
+    def take(self, step):
+        p, g = self.place, self.grads
+        for copy in self.copies(step):
+            copy.wait_recv()
+        if step == 0:
+
+            def add(index, _):
+                x, z = index // p.count, lax.rem(index, p.count)
+                for y in range(2):
+                    g[x, z, y, p.c] += self.from_core[x, z, y]
+                return 0
+
+            lax.fori_loop(0, 2 * p.count, add, 0)
+        elif step == 1:
+
+            def add(z, _):
+                for k in range(2):
+                    g[p.x, z, k, p.c, self.top] += self.from_a[z, k]
+                    g[k, z, p.y, p.c, self.low] += self.from_b[k, z]
+                return 0
+
+            lax.fori_loop(0, p.count, add, 0)
+        elif step == 2:
+
+            def add(z, _):
+                g[p.x, z, p.y, p.c, self.top] += self.from_c[z]
+                g[p.x, z, p.y, p.c, self.low] += self.from_d[z]
+                return 0
+
+            lax.fori_loop(0, p.count, add, 0)
+
+    def result(self):
+        p = self.place
+        total = self.grads[p.x, p.z, p.y, p.c].astype(jnp.float32)
+        for hop in range(1, p.count):
+            total += self.from_z[hop - 1].astype(jnp.float32)
+        return total
+
+    def drain(self):
+        for step in range(4):
+            for copy in self.copies(step):
+                copy.wait_send()
+
+
+def whole_kernel(
+    acts, cots, chain_ids, key_keep, w_up, w_down_t, w_mix, small,
+    outs, grads_x, g_up, g_down, g_mix, small_sum,
+    weights, smalls, x, cot, vecs, b_up, marks, marks_col, sums, sums_up,
+    h1t, query, key, value, bias, mixed, logs, h2t, glowt, glow2t, act, gpre, gmix, dots, gres,
+    gq_wide, gq, gk, gv, grads, from_core, from_a, from_b, from_c, from_d, from_z, small_from, small_tot,
+    local, send, recv,
+):
+    count = weights.shape[2]
+    place = Place(count)
+    wire = Wire(send, recv)
+    me = (place.x, place.z, place.y, place.c)
+    loads = [pltpu.make_async_copy(acts.at[place.x], x, local.at[0]), pltpu.make_async_copy(cots.at[place.x], cot, local.at[1])]
+    for part, ref in enumerate((w_up, w_down_t, w_mix)):
+        loads.append(pltpu.make_async_copy(ref, weights.at[(part, *me)], local.at[2 + part]))
+    loads.append(pltpu.make_async_copy(small, smalls.at[me], local.at[5]))
+    for load in loads:
+        load.start()
+
+    barrier = pltpu.get_barrier_semaphore()
+    partners = [place.other(axis) for axis in "xyc"] + [place.along(hop)[0] for hop in range(1, count)]
+    for device in partners:
+        pl.semaphore_signal(barrier, inc=1, device_id=device, device_id_type=pl.DeviceIdType.MESH)
+    pl.semaphore_wait(barrier, len(partners))
+
+    gathers = [Gather(weights.at[part], part * GATHER_SEMS, wire, place) for part in range(3)]
+    tiny = SmallGather(smalls, 3 * GATHER_SEMS, wire, place)
+    base = 3 * GATHER_SEMS + SMALL_SEMS
+    reduces = [
+        Reduce(
+            grads.at[part], from_core.at[part], from_a.at[part], from_b.at[part], from_c.at[part], from_d.at[part],
+            from_z.at[part], base + part * REDUCE_SEMS, wire, place,
+        )
+        for part in range(3)
+    ]
+    base += 3 * REDUCE_SEMS
+    forward_rows = lambda ref, first, tile: wire.copy(
+        ref.at[place.x, tile_rows(tile)], ref.at[place.x, tile_rows(tile)], first + tile, place.other("x")
+    )
+    out_base, gx_base, small_base = base, base + 8, base + 16
+    tiles = x.shape[0] // TILE
+
+    loads[5].wait()
+    for copy in tiny.z_copies():
+        copy.start()
+    loads[4].wait()
+    gathers[2].start()
+    loads[0].wait()
+    loads[1].wait()
+    loads[2].wait()
+    loads[3].wait()
+    for copy in tiny.z_copies():
+        copy.wait_recv()
+    tiny.step("y").start()
+    gathers[2].after_start()
+    gathers[0].start()
+    gathers[1].start()
+    tiny.step("y").wait_recv()
+    tiny.step("x").start()
+    gathers[2].after_second()
+    tiny.step("x").wait_recv()
+    tiny.step("c").start()
+    gathers[2].after_third()
+    gathers[0].after_start()
+    gathers[1].after_start()
+
+    x_label = chain_ids[pl.ds(place.x, 1), :]
+    label = x_label.astype(jnp.float32)
+    marks[0:1, :] = label
+    marks[1:2, :] = jnp.where(key_keep[pl.ds(place.x, 1), :] == 1, label, -2.0)
+    marks[2:8, :] = jnp.broadcast_to((x_label >= 0).astype(jnp.float32), (6, label.shape[1]))
+    marks_col[...] = marks[...].T
+
+    tiny.step("c").wait_recv()
+    total = jnp.zeros(smalls.shape[4:], jnp.float32)
+    for px in range(2):
+        for pz in range(count):
+            for py in range(2):
+                for pc in range(2):
+                    total += smalls[px, pz, py, pc].astype(jnp.float32)
+    vecs[...] = total[0:8, :]
+    wide = vecs.shape[1]
+    for half in range(2):
+        for k in range(2):
+            row = 8 + half * 2 + k
+            b_up[half : half + 1, k * wide : (k + 1) * wide] = total[row : row + 1, :]
+    gathers[2].finish()
+
+    flat = weights.reshape(3, 2, vecs.shape[1], weights.shape[6])
+    g_flat = grads.reshape(3, 2, vecs.shape[1], weights.shape[6])
+    w0, w1, w2 = flat.at[0], flat.at[1], flat.at[2]
+    qkv_phase(x, w2, vecs, h1t, query, key, value)
+
+    def second_step():
+        gathers[0].after_second()
+        gathers[1].after_second()
+
+    def third_step():
+        gathers[0].after_third()
+        gathers[1].after_third()
+
+    attend_phase(query, key, value, marks, marks_col, bias, mixed, logs, ((0, second_step), (3, third_step)))
+    gathers[0].finish()
+    gathers[1].finish()
+    send_out = lambda tile: forward_rows(outs, out_base, tile).start()
+    middle_phase(x, cot, marks_col, w0, w1, w2, vecs, b_up, mixed, h2t, glowt, glow2t, act, gpre, gmix, dots,
+                 outs.at[place.x], gres, sums, sums_up, send_out)
+    weight_phase(h2t, gpre, g_flat, 0)
+    reduces[0].send(0)
+    weight_phase(glowt, act, g_flat, 1)
+    reduces[1].send(0)
+    output_weight_phase(glow2t, mixed, g_flat)
+
+    def back_first():
+        for part in range(2):
+            reduces[part].take(0)
+            reduces[part].send(1)
+
+    def back_second():
+        for part in range(2):
+            reduces[part].take(1)
+            reduces[part].send(2)
+
+    attend_back_phase(query, key, value, gmix, marks, marks_col, bias, logs, dots, gq_wide, gk, gv,
+                      ((1, back_first), (3, back_second)))
+    for part in range(2):
+        reduces[part].take(2)
+        reduces[part].send(3)
+    round_phase(gq_wide, gq)
+    qkv_weight_phase(h1t, gq, gk, gv, g_flat)
+    reduces[2].send(0)
+    send_gx = lambda tile: forward_rows(grads_x, gx_base, tile).start()
+    input_phase(x, w2, vecs, gq, gk, gv, gres, sums, grads_x.at[place.x], send_gx)
+    small_tot[0:8, :] = sums[...]
+    for half in range(2):
+        for k in range(2):
+            row = 8 + half * 2 + k
+            small_tot[row : row + 1, :] = sums_up[half : half + 1, k * wide : (k + 1) * wide]
+    small_tot[12:16, :] = jnp.zeros((4, wide), jnp.float32)
+
+    def small_copy(number, axis):
+        return wire.copy(small_tot, small_from.at[number], small_base + number, place.other(axis))
+
+    for number, axis in enumerate("cyx"):
+        small_copy(number, axis).start()
+        reduces[2].take(number)
+        reduces[2].send(number + 1)
+        small_copy(number, axis).wait()
+        small_tot[...] += small_from[number]
+    last = []
+    for hop in range(1, count):
+        device, z = place.along(hop)
+        copy = wire.copy(small_tot, small_from.at[2 + hop], small_base + 2 + hop, device)
+        copy.start()
+        last.append(copy)
+    for part in range(2):
+        reduces[part].take(3)
+    g_up[...] = reduces[0].result()
+    g_down[...] = reduces[1].result()
+    for copy in last:
+        copy.wait_recv()
+    ordered = jnp.zeros(small_tot.shape, jnp.float32)
+    for z in range(count):
+        term = small_tot[...]
+        for hop in range(1, count):
+            term = jnp.where(lax.rem(place.z + count - hop, count) == z, small_from[2 + hop], term)
+        ordered += term
+    small_sum[...] = ordered
+    reduces[2].take(3)
+    g_mix[...] = reduces[2].result()
+
+    def land(tile, _):
+        forward_rows(outs, out_base, tile).wait()
+        forward_rows(grads_x, gx_base, tile).wait()
         return 0
 
-    lax.fori_loop(0, halves, step, 0)
-
-
-def compute_kernel(x, cot, weights, vecs, b_up, marks_row, out, grad_x, grads, sums, sums_up,
-                   h1t, query, key, value, bias, mixed, logs, h2t, glowt, glow2t, act, gpre, gmix, dots, gres,
-                   gq_wide, gq, gk, gv, marks_col):
-    marks_col[...] = marks_row[...].T
-    w_up, w_down, w_mix = weights.at[0], weights.at[1], weights.at[2]
-    qkv_phase(x, w_mix, vecs, h1t, query, key, value)
-    attend_phase(query, key, value, marks_row, marks_col, bias, mixed, logs)
-    middle_phase(x, cot, marks_col, w_up, w_down, w_mix, vecs, b_up, mixed, h2t, glowt, glow2t, act, gpre, gmix, dots, out, gres, sums, sums_up)
-    weight_phase(h2t, gpre, grads, 0)
-    weight_phase(glowt, act, grads, 1)
-    output_weight_phase(glow2t, mixed, grads)
-    attend_back_phase(query, key, value, gmix, marks_row, marks_col, bias, logs, dots, gq_wide, gk, gv)
-    input_phase(x, w_mix, vecs, gq_wide, gq, gk, gv, gres, sums, grad_x)
-    qkv_weight_phase(h1t, gq, gk, gv, grads)
-
-
-def compute_scratch(slots, width, hidden):
-    half = (2, slots, width // 2)
+    lax.fori_loop(0, tiles, land, 0)
+    for gather in gathers:
+        gather.drain()
+    for copy in tiny.z_copies():
+        copy.wait_send()
+    for axis in "yxc":
+        tiny.step(axis).wait_send()
+    for reduce in reduces:
+        reduce.drain()
+    for copy in last:
+        copy.wait_send()
+
+
+def whole(acts, cots, chain_ids, key_keep, w_up, w_down_t, w_mix, small, count):
+    slots, width = acts.shape[1], acts.shape[2]
+    rows, columns = w_up.shape
     bf, f32 = jnp.bfloat16, jnp.float32
     V = pltpu.VMEM
-    return [
+    half = (2, slots, width // 2)
+    any_space = pl.BlockSpec(memory_space=pl.ANY)
+    sems = 3 * GATHER_SEMS + SMALL_SEMS + 3 * REDUCE_SEMS + 16 + 8
+    out_shape = (
+        jax.ShapeDtypeStruct((2, slots, width), bf),
+        jax.ShapeDtypeStruct((2, slots, width), bf),
+        jax.ShapeDtypeStruct((rows, columns), f32),
+        jax.ShapeDtypeStruct((rows, columns), f32),
+        jax.ShapeDtypeStruct((rows, columns), f32),
+        jax.ShapeDtypeStruct(small.shape, f32),
+    )
+    scratch = [
+        V((3, 2, count, 2, 2, rows, columns), bf), V((2, count, 2, 2, *small.shape), bf),
+        V((slots, width), bf), V((slots, width), bf), V((8, width), f32), V((2, columns), f32),
+        V((8, slots), f32), V((slots, 8), f32), V((8, width), f32), V((2, columns), f32),
         V((width, slots), bf), V(half, bf), V(half, bf), V(half, bf), V((TILE, slots), f32), V(half, bf),
         V((2, 4, slots), f32), V((width, slots), bf), V((width, slots), bf), V((width, slots), bf),
-        V((2, slots, hidden // 2), bf), V((2, slots, hidden // 2), bf), V(half, bf), V((2, 4, slots), f32),
-        V((slots, width), f32), V(half, f32), V(half, bf), V(half, bf), V(half, bf), V((slots, 8), f32),
+        V((2, slots, columns), bf), V((2, slots, columns), bf), V(half, bf), V((2, 4, slots), f32),
+        V((slots, width), f32), V(half, f32), V(half, bf), V(half, bf), V(half, bf),
+        V((3, 2, count, 2, 2, rows, columns), bf),
+        V((3, 2, count, 2, rows, columns), bf),
+        V((3, count, 2, rows // 2, columns), bf), V((3, 2, count, rows // 2, columns), bf),
+        V((3, count, rows // 2, columns), bf), V((3, count, rows // 2, columns), bf),
+        V((3, count - 1, rows, columns), bf),
+        V((count + 2, *small.shape), f32), V(small.shape, f32),
+        pltpu.SemaphoreType.DMA((6,)), pltpu.SemaphoreType.DMA((sems,)), pltpu.SemaphoreType.DMA((sems,)),
     ]
-
-
-def compute(x, cot, weights, vecs, b_up, marks_row):
-    slots, width = x.shape
-    hidden = b_up.shape[0] * b_up.shape[1]
-    bf, f32 = jnp.bfloat16, jnp.float32
     return pl.pallas_call(
-        compute_kernel,
-        out_shape=(
-            jax.ShapeDtypeStruct((slots, width), bf),
-            jax.ShapeDtypeStruct((slots, width), bf),
-            jax.ShapeDtypeStruct(weights.shape, bf),
-            jax.ShapeDtypeStruct((8, width), f32),
-            jax.ShapeDtypeStruct(b_up.shape, f32),
+        whole_kernel,
+        out_shape=out_shape,
+        in_specs=[any_space, any_space, FULL, FULL, any_space, any_space, any_space, any_space],
+        out_specs=(FULL,) * 6,
+        scratch_shapes=scratch,
+        compiler_params=pltpu.CompilerParams(
+            vmem_limit_bytes=67043328, collective_id=0, has_side_effects=True
         ),
-        in_specs=[FULL] * 6,
-        out_specs=(FULL,) * 5,
-        scratch_shapes=compute_scratch(slots, width, hidden),
-        compiler_params=pltpu.CompilerParams(vmem_limit_bytes=67043328),
-    )(x, cot, weights, vecs, b_up, marks_row)
-
-
-def marks_of(chain, keep):
-    label = chain.astype(jnp.float32)
-    live = (chain >= 0).astype(jnp.float32)
-    as_key = jnp.where(keep == 1, label, -2.0)
-    return jnp.stack([label, as_key, live, live, live, live, live, live])
+    )(acts, cots, chain_ids, key_keep, w_up, w_down_t, w_mix, small)
 
 
 def product(left, right):
@@ -611,29 +1007,22 @@
 
 
 def fits(mesh):
-    return mesh.shape["mp"] == 2
-
-
-def cat_weights(w_qkv, w_o, w_up, w_down):
-    mixed_part = jnp.concatenate([w_qkv[0], w_qkv[1], w_qkv[2], w_o.T], axis=1)
-    return jnp.stack([w_up, w_down.T, mixed_part])
-
-
-def cat_small(b_qv, b_up, out_bias, norm_gain, norm_bias):
-    parts = [b_qv, b_up, norm_gain, norm_bias, out_bias]
-    return jnp.concatenate([part.reshape(-1) for part in parts])
-
-
-def spread_small(smalls, b_qv, b_up):
-    mp, dp = smalls.shape[:2]
-    n0, n1 = b_qv.size, b_qv.size + b_up.size
-    qv = smalls[:, :, :n0].reshape(mp, dp, 2, b_qv.shape[1], b_qv.shape[2])
-    qv = qv.transpose(2, 0, 3, 1, 4).reshape(2, -1)
-    up = smalls[:, :, n0:n1].reshape(mp, dp, b_up.shape[0], b_up.shape[1]).transpose(0, 2, 1, 3).reshape(mp, -1)
-    rest = smalls[0, :, n1:].reshape(dp, 3, 2, -1).transpose(1, 2, 0, 3).reshape(6, -1)
-    gain, shift, bias = rest[0:2], rest[2:4], rest[4:6]
-    vecs = jnp.stack([gain[0], shift[0], gain[1], shift[1], qv[0], qv[1], bias[0], bias[1]])
-    return vecs, up
+    return mesh.shape["mp"] == 2 and mesh.shape["dp"] == 16
+
+
+def place_small(b_qv, b_up, out_bias, norm_gain, norm_bias):
+    own, at, mp, dp = lax.axis_index("mp"), lax.axis_index("dp"), lax.axis_size("mp"), lax.axis_size("dp")
+    here = jnp.arange(dp) == at
+    mine = jnp.arange(mp) == own
+    zero = jnp.zeros((), b_qv.dtype)
+    spread = lambda a: jnp.where((here & (own == 0))[None, :, None], a[:, None, :], zero).reshape(2, -1)
+    gain, shift, bias = spread(norm_gain), spread(norm_bias), spread(out_bias)
+    qv = jnp.where(mine[None, :, None, None, None] & here[None, None, None, :, None], b_qv[:, None, :, None, :], zero)
+    up = jnp.where(mine[:, None, None, None] & here[None, None, :, None], b_up[None, :, None, :], zero)
+    width = gain.shape[1]
+    rows = [gain[0:1], shift[0:1], gain[1:2], shift[1:2], qv.reshape(2, width), bias, up.reshape(-1, width)]
+    table = jnp.concatenate(rows)
+    return jnp.pad(table, ((0, 16 - table.shape[0]), (0, 0)))
 
 
 def body_split(
@@ -651,39 +1040,26 @@
     chain_ids,
     key_keep,
 ):
-    own = lax.axis_index("mp")
-    mp = lax.axis_size("mp")
-    dp = lax.axis_size("dp")
-    packed = cat_weights(w_qkv, w_o, w_up, w_down)
-    small = cat_small(b_qv, b_up, out_bias, norm_gain, norm_bias)
-    depth = packed.shape[1]
-    full = lax.all_gather(packed, ("mp", "dp"), axis=0, tiled=False)
-    full = full.reshape(mp, dp, 3, depth, -1).transpose(2, 0, 1, 3, 4).reshape(3, mp, dp * depth, -1)
-    smalls = lax.all_gather(small, ("mp", "dp"), axis=0, tiled=False).reshape(mp, dp, -1)
-    vecs, up_bias = spread_small(smalls.astype(jnp.float32), b_qv, b_up)
+    own, at = lax.axis_index("mp"), lax.axis_index("dp")
+    mp, dp = lax.axis_size("mp"), lax.axis_size("dp")
+    w_mix = jnp.concatenate([w_qkv[0], w_qkv[1], w_qkv[2], w_o.T], axis=1)
+    small = place_small(b_qv, b_up, out_bias, norm_gain, norm_bias)
+    out, grad_x, g_up, g_down, g_mix, total = whole(
+        activations, cotangent, chain_ids, key_keep, w_up, w_down.T, w_mix, small, dp // 4
+    )
+    pick = lambda a, axis: lax.dynamic_index_in_dim(a, at, axis, keepdims=False)
     take = lambda a: lax.dynamic_index_in_dim(a, own, 0, keepdims=False)
-    marks = marks_of(take(chain_ids), take(key_keep))
-    out, grad_x, grads, sums, sums_up = compute(
-        take(activations), take(cotangent), full, vecs, up_bias, marks
-    )
-    gathered = lax.all_gather(jnp.stack([out, grad_x]), "mp", axis=0, tiled=False).astype(jnp.float32)
-    g_all = grads.reshape(3, mp, dp, depth, -1).transpose(1, 2, 0, 3, 4).reshape(mp * dp, 3, depth, -1)
-    g_own = lax.psum_scatter(g_all, ("mp", "dp"), scatter_dimension=0, tiled=False).astype(jnp.float32)
-    total = lax.psum(jnp.concatenate([sums.reshape(-1), sums_up.reshape(-1)]), ("mp", "dp"))
-    s_vec, s_up = total[: sums.size].reshape(sums.shape), total[sums.size :].reshape(sums_up.shape)
-    at = lax.axis_index("dp")
-    pick = lambda a, axis: lax.dynamic_index_in_dim(a, at, axis, keepdims=False)
-    pairs = lambda r0, r1: pick(jnp.stack([s_vec[r0], s_vec[r1]]).reshape(2, dp, -1), 1)
-    s_qv = pick(take(s_vec[BQ : BV + 1].reshape(2, mp, -1).transpose(1, 0, 2)).reshape(2, b_qv.shape[1], dp, -1), 2)
-    s_bup = pick(take(s_up).reshape(b_up.shape[0], dp, -1), 1)
-    mix, quarter = g_own[2], packed.shape[2] // 4
+    pairs = lambda r0, r1: pick(jnp.stack([total[r0], total[r1]]).reshape(2, dp, -1), 1)
+    s_qv = pick(take(total[BQ : BV + 1].reshape(2, mp, -1).transpose(1, 0, 2)).reshape(2, b_qv.shape[1], dp, -1), 2)
+    s_bup = pick(take(total[8:12].reshape(mp, -1)).reshape(b_up.shape[0], dp, -1), 1)
+    quarter = w_qkv.shape[2]
     return (
-        gathered[:, 0],
-        gathered[:, 1],
-        jnp.stack([mix[:, c * quarter : (c + 1) * quarter] for c in range(3)]),
-        mix[:, 3 * quarter :].T,
-        g_own[0],
-        g_own[1].T,
+        out.astype(jnp.float32),
+        grad_x.astype(jnp.float32),
+        jnp.stack([g_mix[:, c * quarter : (c + 1) * quarter] for c in range(3)]),
+        g_mix[:, 3 * quarter :].T,
+        g_up,
+        g_down.T,
         s_qv,
         s_bup,
         pairs(BO1, BO2),

time: 359 us -> 173 us (0.48)
  waiting for transfers between devices: 133 us -> 0 us
  blocking collectives: 82.8 us -> 0 us
  Pallas kernels: 78.4 us -> 148 us
  local copies, waits for them, and re-layouts: 35.6 us -> 13.3 us
  between operations: 14.5 us -> 0.74 us
  other arithmetic: 14.2 us -> 9.92 us
    reduce_scatter x1 -> x0, waiting for transfers between devices: 113 us -> none  [body_split(): lax.psum_scatter(g_all, ('mp', 'dp'), scatter_dimension=0, tiled=False)]
    pallas_call x1, Pallas kernels: 78.4 us -> 148 us  [whole(): pl.pallas_call(whole_kernel, out_shape=out_shape, in_specs=[any_space, an...]
    unnamed x1 -> x0, blocking collectives: 42.3 us -> none
    psum x1 -> x0, blocking collectives: 40.5 us -> none  [body_split(): lax.psum(jnp.concatenate([sums.reshape(-1), sums_up.reshape(-1)]), ('mp',...]
    all_gather x2 -> x0, waiting for transfers between devices: 19.6 us -> none  [the longest x1 15.2 us: body_split(): full = lax.all_gather(packed, ('mp', 'dp'), axis=0, tiled=False)]
    reshape x9 -> x6, local copies, waits for them, and re-layouts: 10.9 us -> 0.48 us  [the longest x3 0.23 us: body_split(): jnp.stack([total[r0], total[r1]]).reshape(2, dp, -1)]
    squeeze x3 -> x1, local copies, waits for them, and re-layouts: 8.15 us -> 0.76 us  [body_split(): w_mix = jnp.concatenate([w_qkv[0], w_qkv[1], w_qkv[2], w_o.T], axis=1)]
    transpose x4 -> x1, local copies, waits for them, and re-layouts: 8.79 us -> 1.43 us  [body_split(): g_mix[:, 3 * quarter:]]
  transfers between devices with their start and end apart: 3 -> 0, of which waited for: 3 -> 0; matrix products, arithmetic and copies ran while one was open for 9% -> 0% of each run, Pallas kernels for 0% -> 0%
where the time goes in v3:
time: 173 us; the launch traced here: 172 us
  Pallas kernels  148 us (86%)
  local copies, waits for them, and re-layouts  13.3 us (8%)
  other arithmetic  9.92 us (6%)
    pallas_call x1, Pallas kernels, whole(): pl.pallas_call(whole_kernel, out_shape=out_shape, in_specs=[any_space, an...  148 us
    convert_element_type x1, other arithmetic, body_split(): out.astype(jnp.float32)  4.35 us

profile of v3, /device:TPU:0, one launch (start us, length us, event | category | flops | bytes accessed | tf_op | source)
XLA Modules:
  0.0 172.0 jit_solution(17868773910071941563)
XLA Ops:
  0.8 0.1 broadcast_in_dim.115
  0.9 0.8 copy.28
  1.7 0.7 broadcast_in_dim.117
  2.3 0.1 broadcast_in_dim.118
  2.4 0.7 broadcast_select_fusion.1
  3.2 0.1 slice.76
  3.3 0.1 slice.72
  3.4 0.1 slice.74
  3.6 0.1 broadcast_in_dim.109
  3.8 0.8 slice_bitcast_fusion.6
  4.5 1.4 pad_maximum_fusion.1.w_mix
  5.9 0.7 broadcast_in_dim.111
  6.6 0.1 broadcast_in_dim.112
  6.8 0.2 select_n.45
  7.0 0.6 pad.4.small
  7.6 148.0 %shard_map.212 = (bf16[2,1024,512]{2,1,0:T(8,128)(2,1)}, bf16[2,1024,512]{2,1,0:T(8,128)(2,1)}, f32[32,1024]{1,0:T(8,128)}, f32[32,1024]{1,0:T(8,128)}, f32[32,1024]{1,0:T(8,128)}, /*index=5*/f32[16,512]{1,0:T(8,128)}) custom-call(bf16[2,1024,512]{2,1,0:T(8,128)(2,1)} %acts.1, bf16[2,1024,512]{2,1,0:T(8,128)(2,1)} %cots.1, s32[2,1024]{1,0:T(2,128)} %chain_ids.1, ...), custom_call_target="tpu_custom_call" | custom-call | tf_op jit(solution)/shard_map/pallas_call | solution.py:695
  155.7 0.7 slice.82
  156.5 0.9 fusion
  157.3 0.8 fusion.1
  158.2 0.6 constant_dynamic-slice_fusion.1
  158.9 0.6 constant_dynamic-slice_fusion
  159.5 0.6 constant_dynamic-slice_fusion.2
  160.1 0.1 reshape.160
  160.2 0.6 constant_dynamic-slice_fusion.4
  160.8 0.1 reshape.162
  161.0 0.7 copy.30
  161.6 1.4 slice_bitcast_fusion
  163.1 0.6 pad_maximum_fusion
  163.7 4.3 %convert_element_type.8 = f32[2,1024,512]{2,1,0:T(8,128)} convert(bf16[2,1024,512]{2,1,0:T(8,128)(2,1)} %get-tuple-element.17) | non-fusion elementwise | flops 1048576 | bytes 6291456 | tf_op jit(solution)/shard_map/convert_element_type | solution.py:1057
  168.1 2.6 %convert_element_type.9 = f32[2,1024,512]{2,1,0:T(8,128)} convert(bf16[2,1024,512]{2,1,0:T(8,128)(2,1)S(1)} %copy-done) | non-fusion elementwise | flops 1048576 | bytes 6291456 | tf_op jit(solution)/shard_map/convert_element_type | solution.py:1058
  170.7 0.7 copy.39
  171.3 0.7 copy.40
  (27 shorter events, 0.8 us)
Async XLA Ops:
  163.7 4.4 %copy-start = (bf16[2,1024,512]{2,1,0:T(8,128)(2,1)S(1)}, bf16[2,1024,512]{2,1,0:T(8,128)(2,1)}, u32[]{:S(2)}) copy-start(bf16[2,1024,512]{2,1,0:T(8,128)(2,1)} %get-tuple-element.18) | copy-start | bytes 6291460
  168.1 2.6 %copy-start.2 = (f32[32,1024]{1,0:T(8,128)S(1)}, f32[32,1024]{1,0:T(8,128)}, u32[]{:S(2)}) copy-start(f32[32,1024]{1,0:T(8,128)} %get-tuple-element.59) | copy-start | bytes 393220
  168.1 3.3 %copy-start.1 = (f32[32,1024]{1,0:T(8,128)S(1)}, f32[32,1024]{1,0:T(8,128)}, u32[]{:S(2)}) copy-start(f32[32,1024]{1,0:T(8,128)} %get-tuple-element.21) | copy-start | bytes 393220

commit v4 on v3

--- a/solution.py
+++ b/solution.py
@@ -74,14 +74,14 @@
 
     def tile_step(tile, _):
         rows = tile_rows(tile)
-        for when, action in beside:
-            pl.when(tile == when)(action)
         same = marks_col[rows, 0:1] == marks_row[1:2, :]
         here = lax.broadcasted_iota(jnp.int32, (TILE, slots), 0) + tile * TILE
         there = lax.broadcasted_iota(jnp.int32, (TILE, slots), 1)
         bias[...] = jnp.where(same | (here == there), 0.0, masked_value)
 
         def half_step(half, _):
+            for when, action in beside:
+                pl.when(tile * halves + half == when)(action)
             lane = lax.broadcasted_iota(jnp.int32, (TILE, 128), 1)
             stats = jnp.zeros((TILE, 128), jnp.float32)
             for pair in range(quarter // 128):
@@ -108,12 +108,12 @@
     lax.fori_loop(0, slots // TILE, tile_step, 0)
 
 
-def middle_phase(x, cot, live_col, w_up, w_down, w_mix, vecs, b_up, mixed, h2t, glowt, glow2t, act, gpre, gmix, dots, out, gres, sums, sums_up, send):
+def middle_phase(x, cot, live_col, w_up, w_down, w_o, vecs, b_up, mixed, h2t, glowt, glow2t, act, gpre, gmix, dots, out, gres, sums, sums_up, send):
     halves, quarter, hidden_half = mixed.shape[0], mixed.shape[2], w_up.shape[2]
 
     def step(tile, _):
         rows = tile_rows(tile)
-        attn = sum(dot_last(mixed[half, rows, :], w_mix[half, :, 3 * quarter : 4 * quarter]) for half in range(halves))
+        attn = sum(dot_last(mixed[half, rows, :], w_o[half]) for half in range(halves))
         resid = x[rows, :].astype(jnp.float32) + attn + vecs[BO1 : BO1 + 1, :]
         scaled, inverse = statistics(resid)
         hidden = (scaled * vecs[GAIN2 : GAIN2 + 1, :] + vecs[SHIFT2 : SHIFT2 + 1, :]).astype(jnp.bfloat16)
@@ -144,7 +144,7 @@
         low = grad_resid.astype(jnp.bfloat16)
         glow2t[:, rows] = low.T
         for half in range(halves):
-            grad_mixed = dot(low, w_mix[half, :, 3 * quarter : 4 * quarter]).astype(jnp.bfloat16)
+            grad_mixed = dot(low, w_o[half]).astype(jnp.bfloat16)
             gmix[half, rows, :] = grad_mixed
             both = grad_mixed.astype(jnp.float32) * mixed[half, rows, :].astype(jnp.float32)
             dots[half, :, rows] = jnp.sum(both.T.reshape(quarter // 64, 64, TILE), axis=1)
@@ -156,24 +156,14 @@
     lax.fori_loop(0, x.shape[0] // TILE, step, 0)
 
 
-def weight_phase(left_t, right, grads, where):
+def weight_phase(left_t, right, grads):
     halves, _, columns = right.shape
     chunk = min(columns, 512)
 
     def step(half, _):
         for start in range(0, columns, chunk):
             cols = slice(start, start + chunk)
-            grads[where, half, :, cols] = dot(left_t[...], right[half, :, cols]).astype(jnp.bfloat16)
-        return 0
-
-    lax.fori_loop(0, halves, step, 0)
-
-
-def output_weight_phase(glow2t, mixed, grads):
-    halves, _, quarter = mixed.shape
-
-    def step(half, _):
-        grads[2, half, :, 3 * quarter : 4 * quarter] = dot(glow2t[...], mixed[half]).astype(jnp.bfloat16)
+            grads[half, :, cols] = dot(left_t[...], right[half, :, cols]).astype(jnp.bfloat16)
         return 0
 
     lax.fori_loop(0, halves, step, 0)
@@ -185,14 +175,14 @@
 
     def tile_step(tile, _):
         rows = tile_rows(tile)
-        for when, action in beside:
-            pl.when(tile == when)(action)
         same = marks_col[rows, 1:2] == marks_row[0:1, :]
         here = lax.broadcasted_iota(jnp.int32, (TILE, slots), 0) + tile * TILE
         there = lax.broadcasted_iota(jnp.int32, (TILE, slots), 1)
         bias[...] = jnp.where(same | (here == there), 0.0, masked_value)
 
         def half_step(half, _):
+            for when, action in beside:
+                pl.when(tile * halves + half == when)(action)
             for pair in range(quarter // 128):
                 cols = slice(pair * 128, (pair + 1) * 128)
                 queries, grads = query[half, :, cols], gmix[half, :, cols]
@@ -232,12 +222,13 @@
     lax.fori_loop(0, low.shape[0], step, 0)
 
 
-def qkv_weight_phase(h1t, grad_query, grad_key, grad_value, grads):
+def qkv_weight_phase(h1t, grad_query, grad_key, grad_value, grads, then):
     halves, _, quarter = grad_key.shape
 
     def step(half, _):
         for c, ref in enumerate((grad_query, grad_key, grad_value)):
-            grads[2, half, :, c * quarter : (c + 1) * quarter] = dot(h1t[...], ref[half]).astype(jnp.bfloat16)
+            grads[half, :, c * quarter : (c + 1) * quarter] = dot(h1t[...], ref[half]).astype(jnp.bfloat16)
+        then(half)
         return 0
 
     lax.fori_loop(0, halves, step, 0)
@@ -471,22 +462,147 @@
                 copy.wait_send()
 
 
+class ReduceLast:
+    def __init__(self, grads, from_core, from_y, from_z, from_x, base, wire, place):
+        self.grads, self.base, self.wire, self.place = grads, base, wire, place
+        self.from_core, self.from_y, self.from_z, self.from_x = from_core, from_y, from_z, from_x
+
+    def copies(self, step, chunk):
+        p, g, w, base = self.place, self.grads, self.wire, self.base + 5 * chunk
+        if step == 0:
+            return [w.copy(g.at[chunk, :, :, 1 - p.c], self.from_core.at[chunk], base, p.other("c"))]
+        if step == 1:
+            return [w.copy(g.at[chunk, :, 1 - p.y, p.c], self.from_y.at[chunk], base + 1, p.other("y"))]
+        out = []
+        for hop in range(1, p.count):
+            device, z = p.along(hop)
+            out.append(w.copy(g.at[chunk, z, p.y, p.c], self.from_z.at[chunk, hop - 1], base + 1 + hop, device))
+        return out
+
+    def send(self, step, chunk):
+        for copy in self.copies(step, chunk):
+            copy.start()
+
+    def take(self, step, chunk):
+        p, g = self.place, self.grads
+        for copy in self.copies(step, chunk):
+            copy.wait_recv()
+
+        def add(z, _):
+            if step == 0:
+                for y in range(2):
+                    g[chunk, z, y, p.c] += self.from_core[chunk, z, y]
+            else:
+                g[chunk, z, p.y, p.c] += self.from_y[chunk, z]
+            return 0
+
+        if step < 2:
+            lax.fori_loop(0, p.count, add, 0)
+
+    def total(self, chunk):
+        p = self.place
+        total = self.grads[chunk, p.z, p.y, p.c].astype(jnp.float32)
+        for hop in range(1, p.count):
+            total += self.from_z[chunk, hop - 1].astype(jnp.float32)
+        return total
+
+    def last(self):
+        p = self.place
+        mine = self.grads.at[1 - p.x, p.z, p.y, p.c]
+        return self.wire.copy(mine, self.from_x, self.base + 10, p.other("x"))
+
+    def send_last(self):
+        p = self.place
+        self.grads[1 - p.x, p.z, p.y, p.c] = self.total(1 - p.x).astype(jnp.bfloat16)
+        self.last().start()
+
+    def result(self):
+        total = self.total(self.place.x)
+        self.last().wait()
+        return total + self.from_x[...].astype(jnp.float32)
+
+    def drain(self):
+        for chunk in range(2):
+            for step in range(3):
+                for copy in self.copies(step, chunk):
+                    copy.wait_send()
+
+
+LAST_SEMS = 11
+
+
+def lane_is(rows, lanes, test):
+    row = lax.broadcasted_iota(jnp.int32, (rows, lanes), 0)
+    lane = lax.broadcasted_iota(jnp.int32, (rows, lanes), 1)
+    return jnp.where(test(row, lane), 1.0, 0.0)
+
+
+def place_small(b_qv, b_up_t, out_bias, norm_gain, norm_bias, width, own, at):
+    heads, hd = b_qv.shape[1], b_qv.shape[2]
+    span = out_bias.shape[1]
+    groups = width // 64
+    first = jnp.where(own == 0, 1.0, 0.0)
+    wide = lane_is(span, width, lambda row, lane: lane == at * span + row).astype(jnp.bfloat16)
+    narrow = lane_is(hd, width, lambda row, lane: lane % 64 == at * hd + row).astype(jnp.bfloat16)
+    gain, shift, bias = [dot(ref[...], wide) * first for ref in (norm_gain, norm_bias, out_bias)]
+    spot = lane_is(heads, width, lambda row, lane: lane // 64 == own * heads + row)
+    qv = [jnp.sum(dot(b_qv[k], narrow) * spot, axis=0, keepdims=True) for k in range(2)]
+    ups = dot_first(b_up_t[...], narrow) * lane_is(b_up_t.shape[1], width, lambda row, lane: lane // 64 == row % groups)
+    ups = [jnp.sum(ups[k * groups : (k + 1) * groups], axis=0, keepdims=True) for k in range(2)]
+    ups = [row * scale for scale in (first, 1.0 - first) for row in ups]
+    rows = [gain[0:1], shift[0:1], gain[1:2], shift[1:2], *qv, bias[0:1], bias[1:2], *ups]
+    return rows
+
+
+def exact(left, right):
+    return lax.dot_general(
+        left, right, (((1,), (1,)), ((), ())), precision=lax.Precision.HIGHEST, preferred_element_type=jnp.float32
+    )
+
+
+def pick_small(total, own, at, s_qv, s_up, s_bias, s_gain, s_shift):
+    width = total.shape[1]
+    heads, hd = s_qv.shape[1], s_qv.shape[2]
+    span, groups = s_bias.shape[1], width // 64
+    wide = lane_is(span, width, lambda row, lane: lane == at * span + row)
+    narrow = lane_is(hd, width, lambda row, lane: lane % 64 == at * hd + row)
+    vectors = exact(total[0:8, :], wide)
+    for ref, (one, two) in ((s_gain, (GAIN1, GAIN2)), (s_shift, (SHIFT1, SHIFT2)), (s_bias, (BO1, BO2))):
+        ref[0:1, :] = vectors[one : one + 1, :]
+        ref[1:2, :] = vectors[two : two + 1, :]
+    spot = lane_is(heads, width, lambda row, lane: lane // 64 == own * heads + row)
+    for k in range(2):
+        s_qv[k] = exact(total[BQ + k : BQ + k + 1, :] * spot, narrow)
+    mine = jnp.where(own == 0, total[8:10, :], total[10:12, :])
+    rows = [jnp.broadcast_to(mine[k : k + 1, :], (groups, width)) for k in range(2)]
+    spot = lane_is(2 * groups, width, lambda row, lane: lane // 64 == row % groups)
+    s_up[...] = exact(narrow, jnp.concatenate(rows) * spot)
+
+
 def whole_kernel(
-    acts, cots, chain_ids, key_keep, w_up, w_down_t, w_mix, small,
-    outs, grads_x, g_up, g_down, g_mix, small_sum,
-    weights, smalls, x, cot, vecs, b_up, marks, marks_col, sums, sums_up,
+    acts, cots, chain_ids, key_keep, w_up, w_down_t, w_o_t, w_qkv, b_qv, b_up_t, out_bias, norm_gain, norm_bias,
+    outs, grads_x, g_up, g_down, g_out, g_qkv, small_sum,
+    w_0, w_1, w_2, w_3, smalls, x, cot, vecs, b_up, marks, marks_col, sums, sums_up,
     h1t, query, key, value, bias, mixed, logs, h2t, glowt, glow2t, act, gpre, gmix, dots, gres,
-    gq_wide, gq, gk, gv, grads, from_core, from_a, from_b, from_c, from_d, from_z, small_from, small_tot,
-    local, send, recv,
+    gq_wide, gq, gk, gv, *rest,
 ):
-    count = weights.shape[2]
+    weights = (w_0, w_1, w_2, w_3)
+    g_parts, rest = rest[:4], rest[4:]
+    froms, rest = rest[:22], rest[22:]
+    small_from, small_tot, local, send, recv = rest
+    count, wide = w_0.shape[1], vecs.shape[1]
     place = Place(count)
     wire = Wire(send, recv)
     me = (place.x, place.z, place.y, place.c)
-    loads = [pltpu.make_async_copy(acts.at[place.x], x, local.at[0]), pltpu.make_async_copy(cots.at[place.x], cot, local.at[1])]
-    for part, ref in enumerate((w_up, w_down_t, w_mix)):
-        loads.append(pltpu.make_async_copy(ref, weights.at[(part, *me)], local.at[2 + part]))
-    loads.append(pltpu.make_async_copy(small, smalls.at[me], local.at[5]))
+    quarter = w_qkv.shape[2]
+    loads = [
+        pltpu.make_async_copy(w_qkv.at[c], w_3.at[(*me, slice(None), pl.ds(c * quarter, quarter))], local.at[c])
+        for c in range(3)
+    ]
+    for k, (ref, full) in enumerate(((w_up, w_0), (w_down_t, w_1), (w_o_t, w_2))):
+        loads.append(pltpu.make_async_copy(ref, full.at[me], local.at[3 + k]))
+    loads.append(pltpu.make_async_copy(acts.at[place.x], x, local.at[6]))
+    loads.append(pltpu.make_async_copy(cots.at[place.x], cot, local.at[7]))
     for load in loads:
         load.start()
 
@@ -494,55 +610,54 @@
     partners = [place.other(axis) for axis in "xyc"] + [place.along(hop)[0] for hop in range(1, count)]
     for device in partners:
         pl.semaphore_signal(barrier, inc=1, device_id=device, device_id_type=pl.DeviceIdType.MESH)
+
+    rows = place_small(b_qv, b_up_t, out_bias, norm_gain, norm_bias, wide, place.x, lax.axis_index("dp"))
+    rows = jnp.concatenate([*rows, jnp.zeros((16 - len(rows), wide), jnp.float32)])
+    smalls[me] = rows.astype(jnp.bfloat16)
     pl.semaphore_wait(barrier, len(partners))
 
-    gathers = [Gather(weights.at[part], part * GATHER_SEMS, wire, place) for part in range(3)]
-    tiny = SmallGather(smalls, 3 * GATHER_SEMS, wire, place)
-    base = 3 * GATHER_SEMS + SMALL_SEMS
+    gathers = [Gather(weights[part], part * GATHER_SEMS, wire, place) for part in range(4)]
+    tiny = SmallGather(smalls, 4 * GATHER_SEMS, wire, place)
+    base = 4 * GATHER_SEMS + SMALL_SEMS
     reduces = [
-        Reduce(
-            grads.at[part], from_core.at[part], from_a.at[part], from_b.at[part], from_c.at[part], from_d.at[part],
-            from_z.at[part], base + part * REDUCE_SEMS, wire, place,
-        )
-        for part in range(3)
+        Reduce(g_parts[part], *froms[6 * part : 6 * part + 6], base + part * REDUCE_SEMS, wire, place) for part in range(3)
     ]
     base += 3 * REDUCE_SEMS
-    forward_rows = lambda ref, first, tile: wire.copy(
-        ref.at[place.x, tile_rows(tile)], ref.at[place.x, tile_rows(tile)], first + tile, place.other("x")
-    )
+    final = ReduceLast(g_parts[3], *froms[18:22], base, wire, place)
+    base += LAST_SEMS
     out_base, gx_base, small_base = base, base + 8, base + 16
     tiles = x.shape[0] // TILE
 
-    loads[5].wait()
+    def forward_rows(ref, first, tile):
+        part = ref.at[place.x, tile_rows(tile)]
+        return wire.copy(part, part, first + tile, place.other("x"))
+
+    for load in loads[:3]:
+        load.wait()
+    gathers[3].start()
     for copy in tiny.z_copies():
         copy.start()
-    loads[4].wait()
-    gathers[2].start()
-    loads[0].wait()
-    loads[1].wait()
-    loads[2].wait()
-    loads[3].wait()
+    for load in loads[3:]:
+        load.wait()
     for copy in tiny.z_copies():
         copy.wait_recv()
     tiny.step("y").start()
-    gathers[2].after_start()
-    gathers[0].start()
-    gathers[1].start()
+    gathers[3].after_start()
+    for part in range(3):
+        gathers[part].start()
     tiny.step("y").wait_recv()
     tiny.step("x").start()
-    gathers[2].after_second()
-    tiny.step("x").wait_recv()
-    tiny.step("c").start()
-    gathers[2].after_third()
-    gathers[0].after_start()
-    gathers[1].after_start()
-
+    gathers[3].after_second()
     x_label = chain_ids[pl.ds(place.x, 1), :]
     label = x_label.astype(jnp.float32)
     marks[0:1, :] = label
     marks[1:2, :] = jnp.where(key_keep[pl.ds(place.x, 1), :] == 1, label, -2.0)
     marks[2:8, :] = jnp.broadcast_to((x_label >= 0).astype(jnp.float32), (6, label.shape[1]))
     marks_col[...] = marks[...].T
+    tiny.step("x").wait_recv()
+    tiny.step("c").start()
+    gathers[3].after_third()
+    gathers[0].after_start()
 
     tiny.step("c").wait_recv()
     total = jnp.zeros(smalls.shape[4:], jnp.float32)
@@ -552,58 +667,54 @@
                 for pc in range(2):
                     total += smalls[px, pz, py, pc].astype(jnp.float32)
     vecs[...] = total[0:8, :]
-    wide = vecs.shape[1]
     for half in range(2):
         for k in range(2):
             row = 8 + half * 2 + k
             b_up[half : half + 1, k * wide : (k + 1) * wide] = total[row : row + 1, :]
-    gathers[2].finish()
-
-    flat = weights.reshape(3, 2, vecs.shape[1], weights.shape[6])
-    g_flat = grads.reshape(3, 2, vecs.shape[1], weights.shape[6])
-    w0, w1, w2 = flat.at[0], flat.at[1], flat.at[2]
-    qkv_phase(x, w2, vecs, h1t, query, key, value)
-
-    def second_step():
+    gathers[3].finish()
+
+    flat = [ref.reshape(2, wide, ref.shape[5]) for ref in weights]
+    g_flat = [ref.reshape(2, wide, ref.shape[5]) for ref in g_parts]
+    qkv_phase(x, flat[3], vecs, h1t, query, key, value)
+    gathers[1].after_start()
+    gathers[2].after_start()
+
+    def up_second():
         gathers[0].after_second()
+
+    def down_second():
         gathers[1].after_second()
-
-    def third_step():
+        gathers[2].after_second()
+
+    def up_third():
         gathers[0].after_third()
-        gathers[1].after_third()
-
-    attend_phase(query, key, value, marks, marks_col, bias, mixed, logs, ((0, second_step), (3, third_step)))
-    gathers[0].finish()
-    gathers[1].finish()
+
+    attend_phase(query, key, value, marks, marks_col, bias, mixed, logs, ((0, up_second), (2, down_second), (5, up_third)))
+    gathers[1].after_third()
+    gathers[2].after_third()
+    for part in range(3):
+        gathers[part].finish()
     send_out = lambda tile: forward_rows(outs, out_base, tile).start()
-    middle_phase(x, cot, marks_col, w0, w1, w2, vecs, b_up, mixed, h2t, glowt, glow2t, act, gpre, gmix, dots,
-                 outs.at[place.x], gres, sums, sums_up, send_out)
-    weight_phase(h2t, gpre, g_flat, 0)
-    reduces[0].send(0)
-    weight_phase(glowt, act, g_flat, 1)
-    reduces[1].send(0)
-    output_weight_phase(glow2t, mixed, g_flat)
-
-    def back_first():
-        for part in range(2):
-            reduces[part].take(0)
-            reduces[part].send(1)
-
-    def back_second():
-        for part in range(2):
-            reduces[part].take(1)
-            reduces[part].send(2)
+    middle_phase(x, cot, marks_col, flat[0], flat[1], flat[2], vecs, b_up, mixed, h2t, glowt, glow2t, act, gpre, gmix,
+                 dots, outs.at[place.x], gres, sums, sums_up, send_out)
+    for part, (left, right) in enumerate(((h2t, gpre), (glowt, act), (glow2t, mixed))):
+        weight_phase(left, right, g_flat[part])
+        reduces[part].send(0)
+
+    def back_step(step):
+        def act_now():
+            for reduce in reduces:
+                reduce.take(step)
+                reduce.send(step + 1)
+
+        return act_now
 
     attend_back_phase(query, key, value, gmix, marks, marks_col, bias, logs, dots, gq_wide, gk, gv,
-                      ((1, back_first), (3, back_second)))
-    for part in range(2):
-        reduces[part].take(2)
-        reduces[part].send(3)
+                      ((1, back_step(0)), (5, back_step(1)), (7, back_step(2))))
     round_phase(gq_wide, gq)
-    qkv_weight_phase(h1t, gq, gk, gv, g_flat)
-    reduces[2].send(0)
     send_gx = lambda tile: forward_rows(grads_x, gx_base, tile).start()
-    input_phase(x, w2, vecs, gq, gk, gv, gres, sums, grads_x.at[place.x], send_gx)
+    input_phase(x, flat[3], vecs, gq, gk, gv, gres, sums, grads_x.at[place.x], send_gx)
+    qkv_weight_phase(h1t, gq, gk, gv, g_flat[3], lambda half: final.send(0, half))
     small_tot[0:8, :] = sums[...]
     for half in range(2):
         for k in range(2):
@@ -614,22 +725,32 @@
     def small_copy(number, axis):
         return wire.copy(small_tot, small_from.at[number], small_base + number, place.other(axis))
 
-    for number, axis in enumerate("cyx"):
-        small_copy(number, axis).start()
-        reduces[2].take(number)
-        reduces[2].send(number + 1)
+    def small_add(number, axis):
         small_copy(number, axis).wait()
         small_tot[...] += small_from[number]
-    last = []
-    for hop in range(1, count):
-        device, z = place.along(hop)
-        copy = wire.copy(small_tot, small_from.at[2 + hop], small_base + 2 + hop, device)
+
+    small_copy(0, "c").start()
+    for chunk in range(2):
+        final.take(0, chunk)
+        final.send(1, chunk)
+    small_add(0, "c")
+    small_copy(1, "y").start()
+    for part, ref in enumerate((g_up, g_down, g_out)):
+        reduces[part].take(3)
+        ref[...] = reduces[part].result()
+    final.take(1, 0)
+    final.send(2, 0)
+    small_add(1, "y")
+    small_copy(2, "x").start()
+    final.take(1, 1)
+    final.send(2, 1)
+    small_add(2, "x")
+    last = [wire.copy(small_tot, small_from.at[2 + hop], small_base + 2 + hop, place.along(hop)[0]) for hop in range(1, count)]
+    for copy in last:
         copy.start()
-        last.append(copy)
-    for part in range(2):
-        reduces[part].take(3)
-    g_up[...] = reduces[0].result()
-    g_down[...] = reduces[1].result()
+    for chunk in range(2):
+        final.take(2, chunk)
+    final.send_last()
     for copy in last:
         copy.wait_recv()
     ordered = jnp.zeros(small_tot.shape, jnp.float32)
@@ -639,69 +760,110 @@
             term = jnp.where(lax.rem(place.z + count - hop, count) == z, small_from[2 + hop], term)
         ordered += term
     small_sum[...] = ordered
-    reduces[2].take(3)
-    g_mix[...] = reduces[2].result()
+    mine = final.result()
+    for c in range(3):
+        g_qkv[c] = mine[:, c * quarter : (c + 1) * quarter]
 
     def land(tile, _):
         forward_rows(outs, out_base, tile).wait()
         forward_rows(grads_x, gx_base, tile).wait()
         return 0
 
-    lax.fori_loop(0, tiles, land, 0)
     for gather in gathers:
         gather.drain()
     for copy in tiny.z_copies():
         copy.wait_send()
     for axis in "yxc":
         tiny.step(axis).wait_send()
-    for reduce in reduces:
+    for reduce in (*reduces, final):
         reduce.drain()
     for copy in last:
         copy.wait_send()
-
-
-def whole(acts, cots, chain_ids, key_keep, w_up, w_down_t, w_mix, small, count):
+    lax.fori_loop(0, tiles, land, 0)
+
+
+def whole(operands, count):
+    acts, w_up, w_qkv = operands[0], operands[4], operands[7]
     slots, width = acts.shape[1], acts.shape[2]
     rows, columns = w_up.shape
+    quarter = w_qkv.shape[2]
     bf, f32 = jnp.bfloat16, jnp.float32
     V = pltpu.VMEM
     half = (2, slots, width // 2)
     any_space = pl.BlockSpec(memory_space=pl.ANY)
-    sems = 3 * GATHER_SEMS + SMALL_SEMS + 3 * REDUCE_SEMS + 16 + 8
-    out_shape = (
+    sems = 4 * GATHER_SEMS + SMALL_SEMS + 3 * REDUCE_SEMS + LAST_SEMS + 16 + 8
+    out_shape = [
         jax.ShapeDtypeStruct((2, slots, width), bf),
         jax.ShapeDtypeStruct((2, slots, width), bf),
         jax.ShapeDtypeStruct((rows, columns), f32),
         jax.ShapeDtypeStruct((rows, columns), f32),
-        jax.ShapeDtypeStruct((rows, columns), f32),
-        jax.ShapeDtypeStruct(small.shape, f32),
-    )
+        jax.ShapeDtypeStruct((rows, quarter), f32),
+        jax.ShapeDtypeStruct((3, rows, quarter), f32),
+        jax.ShapeDtypeStruct((16, width), f32),
+    ]
+    sizes = (columns, columns, quarter, 3 * quarter)
+    fulls = [V((2, count, 2, 2, rows, size), bf) for size in sizes]
     scratch = [
-        V((3, 2, count, 2, 2, rows, columns), bf), V((2, count, 2, 2, *small.shape), bf),
+        *fulls, V((2, count, 2, 2, 16, width), bf),
         V((slots, width), bf), V((slots, width), bf), V((8, width), f32), V((2, columns), f32),
         V((8, slots), f32), V((slots, 8), f32), V((8, width), f32), V((2, columns), f32),
         V((width, slots), bf), V(half, bf), V(half, bf), V(half, bf), V((TILE, slots), f32), V(half, bf),
         V((2, 4, slots), f32), V((width, slots), bf), V((width, slots), bf), V((width, slots), bf),
         V((2, slots, columns), bf), V((2, slots, columns), bf), V(half, bf), V((2, 4, slots), f32),
-        V((slots, width), f32), V(half, f32), V(half, bf), V(half, bf), V(half, bf),
-        V((3, 2, count, 2, 2, rows, columns), bf),
-        V((3, 2, count, 2, rows, columns), bf),
-        V((3, count, 2, rows // 2, columns), bf), V((3, 2, count, rows // 2, columns), bf),
-        V((3, count, rows // 2, columns), bf), V((3, count, rows // 2, columns), bf),
-        V((3, count - 1, rows, columns), bf),
-        V((count + 2, *small.shape), f32), V(small.shape, f32),
-        pltpu.SemaphoreType.DMA((6,)), pltpu.SemaphoreType.DMA((sems,)), pltpu.SemaphoreType.DMA((sems,)),
+        V((slots, width), f32), V(half, f32), V(half, bf), V(half, bf), V(half, bf), *fulls,
+    ]
+    for size in sizes[:3]:
+        scratch += [
+            V((2, count, 2, rows, size), bf),
+            V((count, 2, rows // 2, size), bf), V((2, count, rows // 2, size), bf),
+            V((count, rows // 2, size), bf), V((count, rows // 2, size), bf),
+            V((count - 1, rows, size), bf),
+        ]
+    scratch += [
+        V((2, count, 2, rows, 3 * quarter), bf), V((2, count, rows, 3 * quarter), bf),
+        V((2, count - 1, rows, 3 * quarter), bf), V((rows, 3 * quarter), bf),
+        V((count + 2, 16, width), f32), V((16, width), f32),
+        pltpu.SemaphoreType.DMA((8,)), pltpu.SemaphoreType.DMA((sems,)), pltpu.SemaphoreType.DMA((sems,)),
     ]
     return pl.pallas_call(
         whole_kernel,
         out_shape=out_shape,
-        in_specs=[any_space, any_space, FULL, FULL, any_space, any_space, any_space, any_space],
-        out_specs=(FULL,) * 6,
+        in_specs=[any_space] * 2 + [FULL] * 2 + [any_space] * 4 + [FULL] * 5,
+        out_specs=[FULL] * 7,
         scratch_shapes=scratch,
         compiler_params=pltpu.CompilerParams(
             vmem_limit_bytes=67043328, collective_id=0, has_side_effects=True
         ),
-    )(acts, cots, chain_ids, key_keep, w_up, w_down_t, w_mix, small)
+    )(*operands)
+
+
+def finish_kernel(out, grad_x, up, down, o_t, qkv, total, r_out, r_gx, r_qkv, r_o, r_up, r_down, r_qv, r_bup, r_bias, r_gain, r_shift):
+    r_out[...] = out[...].astype(jnp.float32)
+    r_gx[...] = grad_x[...].astype(jnp.float32)
+
+    @pl.when(pl.program_id(0) == 0)
+    def _():
+        r_qkv[...] = qkv[...]
+        r_o[...] = o_t[...]
+        r_up[...] = up[...]
+        r_down[...] = down[...]
+        pick_small(total, lax.axis_index("mp"), lax.axis_index("dp"), r_qv, r_bup, r_bias, r_gain, r_shift)
+
+
+def finish(parts, qv_shape, up_shape, pair_shape):
+    out, grad_x = parts[0], parts[1]
+    block = pl.BlockSpec((1, 512, out.shape[2]), lambda step: (step // 2, step % 2, 0))
+    fixed = lambda shape: pl.BlockSpec(shape, lambda step: (0,) * len(shape))
+    f32 = jnp.float32
+    order = (5, 4, 2, 3)
+    shapes = [parts[k].shape for k in order] + [qv_shape, up_shape, pair_shape, pair_shape, pair_shape]
+    return pl.pallas_call(
+        finish_kernel,
+        grid=(2 * out.shape[1] // 512,),
+        out_shape=[jax.ShapeDtypeStruct(out.shape, f32)] * 2 + [jax.ShapeDtypeStruct(shape, f32) for shape in shapes],
+        in_specs=[block, block] + [fixed(part.shape) for part in parts[2:]],
+        out_specs=[block, block] + [fixed(shape) for shape in shapes],
+    )(*parts)
 
 
 def product(left, right):
@@ -1010,21 +1172,6 @@
     return mesh.shape["mp"] == 2 and mesh.shape["dp"] == 16
 
 
-def place_small(b_qv, b_up, out_bias, norm_gain, norm_bias):
-    own, at, mp, dp = lax.axis_index("mp"), lax.axis_index("dp"), lax.axis_size("mp"), lax.axis_size("dp")
-    here = jnp.arange(dp) == at
-    mine = jnp.arange(mp) == own
-    zero = jnp.zeros((), b_qv.dtype)
-    spread = lambda a: jnp.where((here & (own == 0))[None, :, None], a[:, None, :], zero).reshape(2, -1)
-    gain, shift, bias = spread(norm_gain), spread(norm_bias), spread(out_bias)
-    qv = jnp.where(mine[None, :, None, None, None] & here[None, None, None, :, None], b_qv[:, None, :, None, :], zero)
-    up = jnp.where(mine[:, None, None, None] & here[None, None, :, None], b_up[None, :, None, :], zero)
-    width = gain.shape[1]
-    rows = [gain[0:1], shift[0:1], gain[1:2], shift[1:2], qv.reshape(2, width), bias, up.reshape(-1, width)]
-    table = jnp.concatenate(rows)
-    return jnp.pad(table, ((0, 16 - table.shape[0]), (0, 0)))
-
-
 def body_split(
     activations,
     cotangent,
@@ -1040,32 +1187,12 @@
     chain_ids,
     key_keep,
 ):
-    own, at = lax.axis_index("mp"), lax.axis_index("dp")
-    mp, dp = lax.axis_size("mp"), lax.axis_size("dp")
-    w_mix = jnp.concatenate([w_qkv[0], w_qkv[1], w_qkv[2], w_o.T], axis=1)
-    small = place_small(b_qv, b_up, out_bias, norm_gain, norm_bias)
-    out, grad_x, g_up, g_down, g_mix, total = whole(
-        activations, cotangent, chain_ids, key_keep, w_up, w_down.T, w_mix, small, dp // 4
-    )
-    pick = lambda a, axis: lax.dynamic_index_in_dim(a, at, axis, keepdims=False)
-    take = lambda a: lax.dynamic_index_in_dim(a, own, 0, keepdims=False)
-    pairs = lambda r0, r1: pick(jnp.stack([total[r0], total[r1]]).reshape(2, dp, -1), 1)
-    s_qv = pick(take(total[BQ : BV + 1].reshape(2, mp, -1).transpose(1, 0, 2)).reshape(2, b_qv.shape[1], dp, -1), 2)
-    s_bup = pick(take(total[8:12].reshape(mp, -1)).reshape(b_up.shape[0], dp, -1), 1)
-    quarter = w_qkv.shape[2]
-    return (
-        out.astype(jnp.float32),
-        grad_x.astype(jnp.float32),
-        jnp.stack([g_mix[:, c * quarter : (c + 1) * quarter] for c in range(3)]),
-        g_mix[:, 3 * quarter :].T,
-        g_up,
-        g_down.T,
-        s_qv,
-        s_bup,
-        pairs(BO1, BO2),
-        pairs(GAIN1, GAIN2),
-        pairs(SHIFT1, SHIFT2),
-    )
+    parts = whole(
+        (activations, cotangent, chain_ids, key_keep, w_up, w_down.T, w_o.T, w_qkv, b_qv, b_up.T, out_bias, norm_gain, norm_bias),
+        lax.axis_size("dp") // 4,
+    )
+    out, grad_x, qkv, o_t, up, down_t, qv, bup_t, bias, gain, shift = finish(parts, b_qv.shape, b_up.shape[::-1], out_bias.shape)
+    return (out, grad_x, qkv, o_t.T, up, down_t.T, qv, bup_t.T, bias, gain, shift)
 
 
 def solution(mesh):

time: 173 us -> 140 us (0.81)
  local copies, waits for them, and re-layouts: 13.3 us -> 0 us
  other arithmetic: 9.92 us -> 0 us
  Pallas kernels: 148 us -> 139 us
    pallas_call x1 -> x2, Pallas kernels: 148 us -> 139 us  [the longest x1 133 us: whole(): pl.pallas_call(whole_kernel, out_shape=out_shape, in_specs=[any_space] *...]
    convert_element_type x2 -> x0, other arithmetic: 6.96 us -> none  [the longest x1 4.35 us: body_split(): out.astype(jnp.float32)]
    dynamic_slice x7 -> x0, local copies, waits for them, and re-layouts: 3 us -> none  [the longest x6 2.98 us: body_split(): pick = lambda a, axis: lax.dynamic_index_in_dim(a, at, axis, keepdims=False)]
    unnamed x9 -> x0, local copies, waits for them, and re-layouts: 2.09 us -> none
    slice x8 -> x0, local copies, waits for them, and re-layouts: 1.95 us -> none  [the longest x1 0.87 us: body_split(): total[r0]]
    broadcast_in_dim x8 -> x0, local copies, waits for them, and re-layouts: 1.93 us -> none  [the longest x4 1.02 us: place_small(): jnp.where(mine[None, :, None, None, None] & here[None, None, None, :, Non...]
where the time goes in v4:
time: 140 us
  Pallas kernels  139 us (99%)
    pallas_call x1, Pallas kernels, whole(): pl.pallas_call(whole_kernel, out_shape=out_shape, in_specs=[any_space] *...  133 us
    pallas_call x1, Pallas kernels, finish(): pl.pallas_call(finish_kernel, grid=(2 * out.shape[1] // 512,), out_shape=...  6.48 us

profile of v4, /device:TPU:0, one launch (start us, length us, event | category | flops | bytes accessed | tf_op | source)
XLA Modules:
  0.0 139.8 jit_solution(9150993392074209796)
XLA Ops:
  0.6 132.5 %shard_map.212 = (bf16[2,1024,512]{2,1,0:T(8,128)(2,1)}, bf16[2,1024,512]{2,1,0:T(8,128)(2,1)}, f32[32,1024]{1,0:T(8,128)}, f32[32,1024]{1,0:T(8,128)}, f32[32,2...) custom-call(bf16[2,1024,512]{2,1,0:T(8,128)(2,1)} %acts.1, bf16[2,1024,512]{2,1,0:T(8,128)(2,1)} %cots.1, ...), custom_call_target="tpu_custom_call" | custom-call | tf_op jit(solution)/shard_map/pallas_call | solution.py:828
  133.2 6.5 %shard_map.213 = (f32[2,1024,512]{2,1,0:T(8,128)}, f32[2,1024,512]{2,1,0:T(8,128)}, f32[3,32,256]{2,1,0:T(8,128)}, f32[32,256]{1,0:T(8,128)}, f32[32,1024]{1,0:T...) custom-call(bf16[2,1024,512]{2,1,0:T(8,128)(2,1)} %get-tuple-element, ...), custom_call_target="tpu_custom_call" | custom-call | tf_op jit(solution)/shard_map/pallas_call | solution.py:860

commit v5 on v4

--- a/solution.py
+++ b/solution.py
@@ -10,7 +10,9 @@
 
 epsilon = 1e-05
 masked_value = -1e30
+LOG2E = math.log2(math.e)
 TILE = 256
+AHEAD = 3
 FULL = pl.BlockSpec(memory_space=pltpu.VMEM)
 
 GAIN1, SHIFT1, GAIN2, SHIFT2, BQ, BV, BO1, BO2 = range(8)
@@ -49,9 +51,11 @@
     ref[row : row + 1, :] += jnp.sum(values, axis=0, keepdims=True)
 
 
-def qkv_phase(x, w_mix, vecs, h1t, query, key, value):
-    halves, quarter = query.shape[0], query.shape[2]
+def qkv_phase(x, w_mix, vecs, h1t, query_t, key, key_t, value, value_t):
+    halves, quarter = key.shape[0], key.shape[2]
+    heads = quarter // 64
     scale = 1.0 / math.sqrt(64)
+    value_t[:, 64:, :] = jnp.ones((value_t.shape[0], value_t.shape[1] - 64, value_t.shape[2]), value_t.dtype)
 
     def step(tile, _):
         rows = tile_rows(tile)
@@ -61,59 +65,85 @@
         for half in range(halves):
             cols = slice(half * quarter, (half + 1) * quarter)
             part = lambda c: dot(hidden, w_mix[half, :, c * quarter : (c + 1) * quarter])
-            query[half, rows, :] = ((part(0) + vecs[BQ : BQ + 1, cols]).astype(jnp.bfloat16) * scale).astype(jnp.bfloat16)
-            key[half, rows, :] = part(1).astype(jnp.bfloat16)
-            value[half, rows, :] = (part(2) + vecs[BV : BV + 1, cols]).astype(jnp.bfloat16)
+            query = ((part(0) + vecs[BQ : BQ + 1, cols]).astype(jnp.bfloat16) * scale).astype(jnp.bfloat16)
+            query_t[cols, rows] = query.T
+            keys = part(1).astype(jnp.bfloat16)
+            key[half, rows, :] = keys
+            key_t[cols, rows] = keys.T
+            values = (part(2) + vecs[BV : BV + 1, cols]).astype(jnp.bfloat16)
+            value[half, rows, :] = values
+            turned = values.T
+            for head in range(heads):
+                value_t[half * heads + head, 0:64, rows] = turned[head * 64 : (head + 1) * 64, :]
         return 0
 
     lax.fori_loop(0, x.shape[0] // TILE, step, 0)
 
 
-def attend_phase(query, key, value, marks_row, marks_col, bias, mixed, logs, beside):
-    halves, slots, quarter = query.shape
+def attend_phase(query_t, key, value_t, marks_row, marks_col, bias, mixed_t, inverse, expos, store, beside):
+    halves, slots, quarter = key.shape
+    heads = quarter // 64
 
     def tile_step(tile, _):
-        rows = tile_rows(tile)
-        same = marks_col[rows, 0:1] == marks_row[1:2, :]
-        here = lax.broadcasted_iota(jnp.int32, (TILE, slots), 0) + tile * TILE
-        there = lax.broadcasted_iota(jnp.int32, (TILE, slots), 1)
+        lanes = tile_rows(tile)
+        same = marks_col[:, 1:2] == marks_row[0:1, lanes]
+        here = lax.broadcasted_iota(jnp.int32, (slots, TILE), 0)
+        there = lax.broadcasted_iota(jnp.int32, (slots, TILE), 1) + tile * TILE
         bias[...] = jnp.where(same | (here == there), 0.0, masked_value)
 
         def half_step(half, _):
             for when, action in beside:
                 pl.when(tile * halves + half == when)(action)
+
+            @pl.when(tile > 0)
+            def _():
+                store(tile - 1, half).wait()
+
             lane = lax.broadcasted_iota(jnp.int32, (TILE, 128), 1)
-            stats = jnp.zeros((TILE, 128), jnp.float32)
-            for pair in range(quarter // 128):
-                cols = slice(pair * 128, (pair + 1) * 128)
-                both = query[half, rows, cols]
-                keys = key[half, :, cols]
-                values = value[half, :, cols]
-                sums = []
-                for side in range(2):
-                    mine = (lane < 64) if side == 0 else (lane >= 64)
-                    scores = dot_last(jnp.where(mine, both, jnp.zeros_like(both)), keys) + bias[...]
-                    top = jnp.max(scores, axis=1, keepdims=True)
-                    expo = jnp.exp(scores - top)
-                    total = jnp.sum(expo, axis=1, keepdims=True)
-                    sums.append(dot(expo.astype(jnp.bfloat16), values) * (1.0 / total))
-                    stats = jnp.where(lane == pair * 2 + side, top + jnp.log(total), stats)
-                mixed[half, rows, cols] = jnp.where(lane < 64, sums[0], sums[1]).astype(jnp.bfloat16)
-            logs[half, :, rows] = stats.T[0:4, :]
+
+            def scores_of(head, chunk):
+                part = slice(chunk * TILE, (chunk + 1) * TILE)
+                pair = head // 2
+                keys = key[half, part, pair * 128 : (pair + 1) * 128]
+                first = pl.multiple_of(half * quarter + pair * 128, 128)
+                mine = (lane < 64) if head % 2 == 0 else (lane >= 64)
+                return dot(jnp.where(mine, keys, jnp.zeros_like(keys)), query_t[pl.ds(first, 128), lanes]) + bias[part, :]
+
+            chunks = slots // TILE
+            scores = [scores_of(0, chunk) for chunk in range(chunks)]
+            for head in range(heads):
+                top = functools.reduce(jnp.maximum, [jnp.max(part, axis=0, keepdims=True) for part in scores])
+                summed, following = 0.0, []
+                for chunk in range(chunks):
+                    part = slice(chunk * TILE, (chunk + 1) * TILE)
+                    expo = jnp.exp2(((scores[chunk] - top) * LOG2E).astype(jnp.bfloat16))
+                    expos[half, head, part, :] = expo
+                    if head + 1 < heads:
+                        following.append(scores_of(head + 1, chunk))
+                    summed = summed + dot(value_t[half * heads + head, :, part], expo)
+                share = 1.0 / summed[64:65, :]
+                inverse[half * heads + head, 0:1, lanes] = share
+                at = pl.multiple_of(half * quarter + head * 64, 64)
+                mixed_t[pl.ds(at, 64), lanes] = (summed[0:64, :] * share).astype(jnp.bfloat16)
+                scores = following
+            store(tile, half).start()
             return 0
 
         lax.fori_loop(0, halves, half_step, 0)
         return 0
 
     lax.fori_loop(0, slots // TILE, tile_step, 0)
-
-
-def middle_phase(x, cot, live_col, w_up, w_down, w_o, vecs, b_up, mixed, h2t, glowt, glow2t, act, gpre, gmix, dots, out, gres, sums, sums_up, send):
-    halves, quarter, hidden_half = mixed.shape[0], mixed.shape[2], w_up.shape[2]
+    for half in range(halves):
+        store(slots // TILE - 1, half).wait()
+
+
+def middle_phase(x, cot, live_col, w_up, w_down, w_o, vecs, b_up, mixed_t, inverse_sum, h2t, glowt, glow2t, act, gpre, gmix_t, dots, out, gres, sums, sums_up, send):
+    halves, quarter, hidden_half = w_up.shape[0], w_o.shape[2], w_up.shape[2]
+    heads = quarter // 64
 
     def step(tile, _):
         rows = tile_rows(tile)
-        attn = sum(dot_last(mixed[half, rows, :], w_o[half]) for half in range(halves))
+        attn = sum(dot_last(mixed_t[half * quarter : (half + 1) * quarter, rows].T, w_o[half]) for half in range(halves))
         resid = x[rows, :].astype(jnp.float32) + attn + vecs[BO1 : BO1 + 1, :]
         scaled, inverse = statistics(resid)
         hidden = (scaled * vecs[GAIN2 : GAIN2 + 1, :] + vecs[SHIFT2 : SHIFT2 + 1, :]).astype(jnp.bfloat16)
@@ -144,10 +174,14 @@
         low = grad_resid.astype(jnp.bfloat16)
         glow2t[:, rows] = low.T
         for half in range(halves):
-            grad_mixed = dot(low, w_o[half]).astype(jnp.bfloat16)
-            gmix[half, rows, :] = grad_mixed
-            both = grad_mixed.astype(jnp.float32) * mixed[half, rows, :].astype(jnp.float32)
-            dots[half, :, rows] = jnp.sum(both.T.reshape(quarter // 64, 64, TILE), axis=1)
+            grads = dot(low, w_o[half]).T
+            for head in range(heads):
+                at = half * quarter + head * 64
+                share = inverse_sum[half * heads + head, 0:1, rows]
+                scaled_grads = grads[head * 64 : (head + 1) * 64, :] * share
+                gmix_t[at : at + 64, rows] = scaled_grads.astype(jnp.bfloat16)
+                both = scaled_grads * mixed_t[at : at + 64, rows].astype(jnp.float32)
+                dots[half * heads + head, 0:1, rows] = jnp.sum(both, axis=0, keepdims=True)
         send(tile)
         return 0
 
@@ -156,7 +190,7 @@
     lax.fori_loop(0, x.shape[0] // TILE, step, 0)
 
 
-def weight_phase(left_t, right, grads):
+def weight_phase(left_t, right, grads, then):
     halves, _, columns = right.shape
     chunk = min(columns, 512)
 
@@ -164,46 +198,68 @@
         for start in range(0, columns, chunk):
             cols = slice(start, start + chunk)
             grads[half, :, cols] = dot(left_t[...], right[half, :, cols]).astype(jnp.bfloat16)
+        then(half)
         return 0
 
     lax.fori_loop(0, halves, step, 0)
 
 
-def attend_back_phase(query, key, value, gmix, marks_row, marks_col, bias, logs, dots, grad_query, grad_key, grad_value, beside):
-    halves, slots, quarter = query.shape
-    grad_query[...] = jnp.zeros_like(grad_query)
+def turned_weight_phase(left_t, right_t, grads, then):
+    halves, _, quarter = grads.shape
+
+    def step(half, _):
+        grads[half] = dot_last(left_t[...], right_t[tile_rows(half), :]).astype(jnp.bfloat16)
+        then(half)
+        return 0
+
+    lax.fori_loop(0, halves, step, 0)
+
+
+def attend_back_phase(query_t, key_t, value, gmix_t, dots, expos, load, grad_query, wide_key, wide_value, beside):
+    halves, slots, quarter = value.shape
+    heads = quarter // 64
+    wide_key[...] = jnp.zeros_like(wide_key)
+    wide_value[...] = jnp.zeros_like(wide_value)
+    scale = 1.0 / math.sqrt(64)
 
     def tile_step(tile, _):
-        rows = tile_rows(tile)
-        same = marks_col[rows, 1:2] == marks_row[0:1, :]
-        here = lax.broadcasted_iota(jnp.int32, (TILE, slots), 0) + tile * TILE
-        there = lax.broadcasted_iota(jnp.int32, (TILE, slots), 1)
-        bias[...] = jnp.where(same | (here == there), 0.0, masked_value)
+        lanes = tile_rows(tile)
 
         def half_step(half, _):
             for when, action in beside:
                 pl.when(tile * halves + half == when)(action)
-            for pair in range(quarter // 128):
-                cols = slice(pair * 128, (pair + 1) * 128)
-                queries, grads = query[half, :, cols], gmix[half, :, cols]
-                keys, values = key[half, rows, cols], value[half, rows, cols]
-                lane = lax.broadcasted_iota(jnp.int32, (TILE, 128), 1)
-                wide = lax.broadcasted_iota(jnp.int32, (slots, 128), 1)
-                parts = []
-                for side in range(2):
-                    head = pair * 2 + side
-                    mine = (lane < 64) if side == 0 else (lane >= 64)
-                    zero = jnp.zeros_like(keys)
-                    scores = dot_last(jnp.where(mine, keys, zero), queries) + bias[...]
-                    probs = jnp.exp(scores - logs[half, head : head + 1, :])
-                    grad_probs = dot_last(jnp.where(mine, values, zero), grads)
-                    grad_scores = (probs * (grad_probs - dots[half, head : head + 1, :])).astype(jnp.bfloat16)
-                    parts.append(
-                        (dot(probs.astype(jnp.bfloat16), grads), dot(grad_scores, queries), dot_first(grad_scores, keys))
-                    )
-                grad_value[half, rows, cols] = jnp.where(lane < 64, parts[0][0], parts[1][0]).astype(jnp.bfloat16)
-                grad_key[half, rows, cols] = jnp.where(lane < 64, parts[0][1], parts[1][1]).astype(jnp.bfloat16)
-                grad_query[half, :, cols] += jnp.where(wide < 64, parts[0][2], parts[1][2])
+            load(tile, half).wait()
+            lane = lax.broadcasted_iota(jnp.int32, (TILE, 128), 1)
+            chunks = slots // TILE
+
+            def grad_probs_of(step):
+                head, chunk = step // chunks, step % chunks
+                pair = head // 2
+                values = value[half, chunk * TILE : (chunk + 1) * TILE, pair * 128 : (pair + 1) * 128]
+                first = pl.multiple_of(half * quarter + pair * 128, 128)
+                mine = (lane < 64) if head % 2 == 0 else (lane >= 64)
+                return dot(jnp.where(mine, values, jnp.zeros_like(values)), gmix_t[pl.ds(first, 128), lanes])
+
+            ahead = [grad_probs_of(step) for step in range(AHEAD)]
+            for step in range(heads * chunks):
+                head, chunk = step // chunks, step % chunks
+                part = slice(chunk * TILE, (chunk + 1) * TILE)
+                at = pl.ds(pl.multiple_of(half * quarter + head * 64, 64), 64)
+                if step + AHEAD < heads * chunks:
+                    ahead.append(grad_probs_of(step + AHEAD))
+                expo = expos[half, head, part, :]
+                grad_scores = expo * (ahead[step] - dots[half * heads + head, 0:1, lanes]).astype(jnp.bfloat16)
+                wide_value[at, part] += dot_last(gmix_t[at, lanes], expo)
+                wide_key[at, part] += dot_last(query_t[at, lanes], grad_scores)
+                term = dot(key_t[at, part], grad_scores)
+                total = term if chunk == 0 else total + term
+                if chunk == chunks - 1:
+                    grad_query[at, lanes] = (total * scale).astype(jnp.bfloat16)
+
+            @pl.when(tile + 1 < slots // TILE)
+            def _():
+                load(tile + 1, half).start()
+
             return 0
 
         lax.fori_loop(0, halves, half_step, 0)
@@ -213,43 +269,44 @@
 
 
 def round_phase(wide, low):
-    scale = 1.0 / math.sqrt(64)
-
-    def step(half, _):
-        low[half] = (wide[half] * scale).astype(jnp.bfloat16)
+    def step(tile, _):
+        rows = tile_rows(tile)
+        low[rows, :] = wide[rows, :].astype(jnp.bfloat16)
         return 0
 
-    lax.fori_loop(0, low.shape[0], step, 0)
+    lax.fori_loop(0, low.shape[0] // TILE, step, 0)
 
 
 def qkv_weight_phase(h1t, grad_query, grad_key, grad_value, grads, then):
-    halves, _, quarter = grad_key.shape
+    halves, quarter = grads.shape[0], grads.shape[2] // 3
 
     def step(half, _):
         for c, ref in enumerate((grad_query, grad_key, grad_value)):
-            grads[half, :, c * quarter : (c + 1) * quarter] = dot(h1t[...], ref[half]).astype(jnp.bfloat16)
+            grads[half, :, c * quarter : (c + 1) * quarter] = dot_last(h1t[...], ref[tile_rows(half), :]).astype(jnp.bfloat16)
         then(half)
         return 0
 
     lax.fori_loop(0, halves, step, 0)
 
 
-def input_phase(x, w_mix, vecs, grad_query, grad_key, grad_value, gres, sums, grad_x, send):
-    halves, slots, quarter = grad_key.shape
+def input_phase(x, w_mix, vecs, grad_query, grad_key, grad_value, gres, sums, grad_x, free, send):
+    slots, halves, quarter = x.shape[0], w_mix.shape[0], w_mix.shape[2] // 3
+    ones = jnp.ones((8, slots), jnp.bfloat16)
+    for row, ref in ((BQ, grad_query), (BV, grad_value)):
+        sums[row : row + 1, :] = dot_last(ones, ref[...])[0:1, :]
 
     def step(tile, _):
         rows = tile_rows(tile)
         scaled, inverse = statistics(x[rows, :].astype(jnp.float32))
-        grad_one = jnp.zeros((TILE, x.shape[1]), jnp.float32)
+        turned = jnp.zeros((x.shape[1], TILE), jnp.float32)
         for half in range(halves):
-            cols = slice(half * quarter, (half + 1) * quarter)
-            three = (grad_query[half, rows, :], grad_key[half, rows, :], grad_value[half, rows, :])
-            for c in range(3):
-                grad_one += dot_last(three[c], w_mix[half, :, c * quarter : (c + 1) * quarter])
-            sums[BQ : BQ + 1, cols] += jnp.sum(three[0].astype(jnp.float32), axis=0, keepdims=True)
-            sums[BV : BV + 1, cols] += jnp.sum(three[2].astype(jnp.float32), axis=0, keepdims=True)
+            for c, ref in enumerate((grad_query, grad_key, grad_value)):
+                part = ref[half * quarter : (half + 1) * quarter, rows]
+                turned += dot(w_mix[half, :, c * quarter : (c + 1) * quarter], part)
+        grad_one = turned.T
         add_row(sums, GAIN1, grad_one * scaled)
         add_row(sums, SHIFT1, grad_one)
+        free(tile)
         grad_x[rows, :] = (gres[rows, :] + norm_back(grad_one, scaled, inverse, vecs[GAIN1 : GAIN1 + 1, :])).astype(grad_x.dtype)
         send(tile)
         return 0
@@ -289,7 +346,7 @@
 
 
 GATHER_SEMS = 15
-REDUCE_SEMS = 9
+REDUCE_SEMS = 11
 SMALL_SEMS = 7
 
 
@@ -371,98 +428,34 @@
             copy.wait_send()
 
 
-class SmallGather:
-    def __init__(self, ref, base, wire, place):
-        self.ref, self.base, self.wire, self.place = ref, base, wire, place
+class SmallSum:
+    def __init__(self, held, arrived, base, wire, place):
+        self.held, self.arrived, self.base, self.wire, self.place = held, arrived, base, wire, place
 
     def z_copies(self):
         p = self.place
-        mine = self.ref.at[p.x, p.z, p.y, p.c]
-        return [self.wire.copy(mine, mine, self.base + hop - 1, p.along(hop)[0]) for hop in range(1, p.count)]
+        return [
+            self.wire.copy(self.held.at[0], self.arrived.at[hop - 1], self.base + hop - 1, p.along(hop)[0])
+            for hop in range(1, p.count)
+        ]
 
     def step(self, axis):
-        p, ref = self.place, self.ref
-        src = {"y": ref.at[p.x, :, p.y, p.c], "x": ref.at[p.x, :, :, p.c], "c": ref.at[:, :, :, p.c]}[axis]
-        return self.wire.copy(src, src, self.base + {"y": 3, "x": 4, "c": 5}[axis], p.other(axis))
+        p, k = self.place, {"y": 1, "x": 2, "c": 3}[axis]
+        number = p.count - 2 + k
+        return self.wire.copy(self.held.at[k], self.arrived.at[number], self.base + number, p.other(axis))
+
+    def add_z(self):
+        total = self.held[0]
+        for hop in range(1, self.place.count):
+            total += self.arrived[hop - 1]
+        self.held[1] = total
+
+    def add(self, axis):
+        k = {"y": 1, "x": 2, "c": 3}[axis]
+        self.held[k + 1] = self.held[k] + self.arrived[self.place.count - 2 + k]
 
 
 class Reduce:
-    def __init__(self, grads, from_core, from_a, from_b, from_c, from_d, from_z, base, wire, place):
-        self.grads, self.base, self.wire, self.place = grads, base, wire, place
-        self.from_core, self.from_a, self.from_b = from_core, from_a, from_b
-        self.from_c, self.from_d, self.from_z = from_c, from_d, from_z
-        rows = grads.shape[4]
-        self.top, self.low = pl.ds(0, rows // 2), pl.ds(rows // 2, rows // 2)
-
-    def copies(self, step):
-        p, g, w, base = self.place, self.grads, self.wire, self.base
-        if step == 0:
-            return [w.copy(g.at[:, :, :, 1 - p.c], self.from_core, base, p.other("c"))]
-        if step == 1:
-            return [
-                w.copy(g.at[1 - p.x, :, :, p.c, self.top], self.from_a, base + 1, p.other("x")),
-                w.copy(g.at[:, :, 1 - p.y, p.c, self.low], self.from_b, base + 2, p.other("y")),
-            ]
-        if step == 2:
-            return [
-                w.copy(g.at[p.x, :, 1 - p.y, p.c, self.top], self.from_c, base + 3, p.other("y")),
-                w.copy(g.at[1 - p.x, :, p.y, p.c, self.low], self.from_d, base + 4, p.other("x")),
-            ]
-        out = []
-        for hop in range(1, p.count):
-            device, z = p.along(hop)
-            out.append(w.copy(g.at[p.x, z, p.y, p.c], self.from_z.at[hop - 1], base + 4 + hop, device))
-        return out
-
-    def send(self, step):
-        for copy in self.copies(step):
-            copy.start()
-
-    def take(self, step):
-        p, g = self.place, self.grads
-        for copy in self.copies(step):
-            copy.wait_recv()
-        if step == 0:
-
-            def add(index, _):
-                x, z = index // p.count, lax.rem(index, p.count)
-                for y in range(2):
-                    g[x, z, y, p.c] += self.from_core[x, z, y]
-                return 0
-
-            lax.fori_loop(0, 2 * p.count, add, 0)
-        elif step == 1:
-
-            def add(z, _):
-                for k in range(2):
-                    g[p.x, z, k, p.c, self.top] += self.from_a[z, k]
-                    g[k, z, p.y, p.c, self.low] += self.from_b[k, z]
-                return 0
-
-            lax.fori_loop(0, p.count, add, 0)
-        elif step == 2:
-
-            def add(z, _):
-                g[p.x, z, p.y, p.c, self.top] += self.from_c[z]
-                g[p.x, z, p.y, p.c, self.low] += self.from_d[z]
-                return 0
-
-            lax.fori_loop(0, p.count, add, 0)
-
-    def result(self):
-        p = self.place
-        total = self.grads[p.x, p.z, p.y, p.c].astype(jnp.float32)
-        for hop in range(1, p.count):
-            total += self.from_z[hop - 1].astype(jnp.float32)
-        return total
-
-    def drain(self):
-        for step in range(4):
-            for copy in self.copies(step):
-                copy.wait_send()
-
-
-class ReduceLast:
     def __init__(self, grads, from_core, from_y, from_z, from_x, base, wire, place):
         self.grads, self.base, self.wire, self.place = grads, base, wire, place
         self.from_core, self.from_y, self.from_z, self.from_x = from_core, from_y, from_z, from_x
@@ -526,9 +519,6 @@
             for step in range(3):
                 for copy in self.copies(step, chunk):
                     copy.wait_send()
-
-
-LAST_SEMS = 11
 
 
 def lane_is(rows, lanes, test):
@@ -581,14 +571,15 @@
 
 def whole_kernel(
     acts, cots, chain_ids, key_keep, w_up, w_down_t, w_o_t, w_qkv, b_qv, b_up_t, out_bias, norm_gain, norm_bias,
-    outs, grads_x, g_up, g_down, g_out, g_qkv, small_sum,
-    w_0, w_1, w_2, w_3, smalls, x, cot, vecs, b_up, marks, marks_col, sums, sums_up,
-    h1t, query, key, value, bias, mixed, logs, h2t, glowt, glow2t, act, gpre, gmix, dots, gres,
-    gq_wide, gq, gk, gv, *rest,
+    outs, grads_x, g_up, g_down, g_out, g_qkv, small_sum, kept,
+    w_0, w_1, w_2, w_3, smalls, smalls_from, x, cot, vecs, b_up, marks, marks_col, sums, sums_up,
+    h1t, query_t, key, key_t, value, value_t, bias, mixed_t, inverse_sum, expos, h2t, glowt, glow2t, act, gpre,
+    gmix_t, dots, gres, wide_key, wide_value, stage, *rest,
 ):
     weights = (w_0, w_1, w_2, w_3)
+    gq, gk, gv = [act.at[k // 2, pl.ds(k % 2 * vecs.shape[1], vecs.shape[1])] for k in range(3)]
     g_parts, rest = rest[:4], rest[4:]
-    froms, rest = rest[:22], rest[22:]
+    froms, rest = rest[:16], rest[16:]
     small_from, small_tot, local, send, recv = rest
     count, wide = w_0.shape[1], vecs.shape[1]
     place = Place(count)
@@ -613,39 +604,55 @@
 
     rows = place_small(b_qv, b_up_t, out_bias, norm_gain, norm_bias, wide, place.x, lax.axis_index("dp"))
     rows = jnp.concatenate([*rows, jnp.zeros((16 - len(rows), wide), jnp.float32)])
-    smalls[me] = rows.astype(jnp.bfloat16)
+    smalls[0] = rows.astype(jnp.bfloat16)
     pl.semaphore_wait(barrier, len(partners))
 
     gathers = [Gather(weights[part], part * GATHER_SEMS, wire, place) for part in range(4)]
-    tiny = SmallGather(smalls, 4 * GATHER_SEMS, wire, place)
+    tiny = SmallSum(smalls, smalls_from, 4 * GATHER_SEMS, wire, place)
     base = 4 * GATHER_SEMS + SMALL_SEMS
     reduces = [
-        Reduce(g_parts[part], *froms[6 * part : 6 * part + 6], base + part * REDUCE_SEMS, wire, place) for part in range(3)
+        Reduce(g_parts[part], *froms[4 * part : 4 * part + 4], base + part * REDUCE_SEMS, wire, place) for part in range(4)
     ]
-    base += 3 * REDUCE_SEMS
-    final = ReduceLast(g_parts[3], *froms[18:22], base, wire, place)
-    base += LAST_SEMS
+    final = reduces[3]
+    base += 4 * REDUCE_SEMS
     out_base, gx_base, small_base = base, base + 8, base + 16
     tiles = x.shape[0] // TILE
 
     def forward_rows(ref, first, tile):
         part = ref.at[place.x, tile_rows(tile)]
-        return wire.copy(part, part, first + tile, place.other("x"))
+        return wire.copy(stage.at[tile_rows(tile)], part, first + tile, place.other("x"))
+
+    def keep_rows(ref, first, tile):
+        return pltpu.make_async_copy(stage.at[tile_rows(tile)], ref.at[place.x, tile_rows(tile)], local.at[first + tile])
+
+    def send_out(tile):
+        forward_rows(outs, out_base, tile).start()
+        keep_rows(outs, 12, tile).start()
+
+    def free_stage(tile):
+        forward_rows(outs, out_base, tile).wait_send()
+        keep_rows(outs, 12, tile).wait()
+
+    def send_gx(tile):
+        forward_rows(grads_x, gx_base, tile).start()
+        keep_rows(grads_x, 16, tile).start()
 
     for load in loads[:3]:
         load.wait()
-    gathers[3].start()
     for copy in tiny.z_copies():
         copy.start()
+    gathers[3].start()
     for load in loads[3:]:
         load.wait()
     for copy in tiny.z_copies():
         copy.wait_recv()
+    tiny.add_z()
     tiny.step("y").start()
     gathers[3].after_start()
     for part in range(3):
         gathers[part].start()
     tiny.step("y").wait_recv()
+    tiny.add("y")
     tiny.step("x").start()
     gathers[3].after_second()
     x_label = chain_ids[pl.ds(place.x, 1), :]
@@ -655,17 +662,14 @@
     marks[2:8, :] = jnp.broadcast_to((x_label >= 0).astype(jnp.float32), (6, label.shape[1]))
     marks_col[...] = marks[...].T
     tiny.step("x").wait_recv()
+    tiny.add("x")
     tiny.step("c").start()
     gathers[3].after_third()
     gathers[0].after_start()
 
     tiny.step("c").wait_recv()
-    total = jnp.zeros(smalls.shape[4:], jnp.float32)
-    for px in range(2):
-        for pz in range(count):
-            for py in range(2):
-                for pc in range(2):
-                    total += smalls[px, pz, py, pc].astype(jnp.float32)
+    tiny.add("c")
+    total = smalls[4].astype(jnp.float32)
     vecs[...] = total[0:8, :]
     for half in range(2):
         for k in range(2):
@@ -673,9 +677,11 @@
             b_up[half : half + 1, k * wide : (k + 1) * wide] = total[row : row + 1, :]
     gathers[3].finish()
 
+    keep = lambda tile, half: pltpu.make_async_copy(expos.at[half], kept.at[tile, half], local.at[8 + half])
+    fetch = lambda tile, half: pltpu.make_async_copy(kept.at[tile, half], expos.at[half], local.at[10 + half])
     flat = [ref.reshape(2, wide, ref.shape[5]) for ref in weights]
     g_flat = [ref.reshape(2, wide, ref.shape[5]) for ref in g_parts]
-    qkv_phase(x, flat[3], vecs, h1t, query, key, value)
+    qkv_phase(x, flat[3], vecs, h1t, query_t, key, key_t, value, value_t)
     gathers[1].after_start()
     gathers[2].after_start()
 
@@ -689,32 +695,34 @@
     def up_third():
         gathers[0].after_third()
 
-    attend_phase(query, key, value, marks, marks_col, bias, mixed, logs, ((0, up_second), (2, down_second), (5, up_third)))
+    attend_phase(query_t, key, value_t, marks, marks_col, bias, mixed_t, inverse_sum, expos, keep, ((0, up_second), (2, down_second), (5, up_third)))
     gathers[1].after_third()
     gathers[2].after_third()
     for part in range(3):
         gathers[part].finish()
-    send_out = lambda tile: forward_rows(outs, out_base, tile).start()
-    middle_phase(x, cot, marks_col, flat[0], flat[1], flat[2], vecs, b_up, mixed, h2t, glowt, glow2t, act, gpre, gmix,
-                 dots, outs.at[place.x], gres, sums, sums_up, send_out)
-    for part, (left, right) in enumerate(((h2t, gpre), (glowt, act), (glow2t, mixed))):
-        weight_phase(left, right, g_flat[part])
-        reduces[part].send(0)
-
-    def back_step(step):
-        def act_now():
-            for reduce in reduces:
-                reduce.take(step)
-                reduce.send(step + 1)
-
-        return act_now
-
-    attend_back_phase(query, key, value, gmix, marks, marks_col, bias, logs, dots, gq_wide, gk, gv,
-                      ((1, back_step(0)), (5, back_step(1)), (7, back_step(2))))
-    round_phase(gq_wide, gq)
-    send_gx = lambda tile: forward_rows(grads_x, gx_base, tile).start()
-    input_phase(x, flat[3], vecs, gq, gk, gv, gres, sums, grads_x.at[place.x], send_gx)
+    middle_phase(x, cot, marks_col, flat[0], flat[1], flat[2], vecs, b_up, mixed_t, inverse_sum, h2t, glowt, glow2t, act, gpre,
+                 gmix_t, dots, stage, gres, sums, sums_up, send_out)
+    for half in range(2):
+        fetch(0, half).start()
+    def step_on(part, step, *chunks):
+        for chunk in chunks:
+            reduces[part].take(step, chunk)
+            reduces[part].send(step + 1, chunk)
+
+    weight_phase(h2t, gpre, g_flat[0], lambda half: reduces[0].send(0, half))
+    weight_phase(glowt, act, g_flat[1], lambda half: reduces[1].send(0, half))
+    step_on(0, 0, 0, 1)
+    turned_weight_phase(glow2t, mixed_t, g_flat[2], lambda half: reduces[2].send(0, half))
+    step_on(1, 0, 0, 1)
+    attend_back_phase(query_t, key_t, value, gmix_t, dots, expos, fetch, gq, wide_key, wide_value, (
+        (0, lambda: step_on(2, 0, 0, 1)), (3, lambda: step_on(0, 1, 0)), (6, lambda: step_on(0, 1, 1)),
+    ))
+    round_phase(wide_key, gk)
+    round_phase(wide_value, gv)
     qkv_weight_phase(h1t, gq, gk, gv, g_flat[3], lambda half: final.send(0, half))
+    step_on(1, 1, 0)
+    step_on(3, 0, 0, 1)
+    input_phase(x, flat[3], vecs, gq, gk, gv, gres, sums, stage, free_stage, send_gx)
     small_tot[0:8, :] = sums[...]
     for half in range(2):
         for k in range(2):
@@ -730,43 +738,44 @@
         small_tot[...] += small_from[number]
 
     small_copy(0, "c").start()
-    for chunk in range(2):
-        final.take(0, chunk)
-        final.send(1, chunk)
+    step_on(1, 1, 1)
     small_add(0, "c")
     small_copy(1, "y").start()
-    for part, ref in enumerate((g_up, g_down, g_out)):
-        reduces[part].take(3)
-        ref[...] = reduces[part].result()
-    final.take(1, 0)
-    final.send(2, 0)
+    for chunk in range(2):
+        reduces[0].take(2, chunk)
+    reduces[0].send_last()
+    step_on(2, 1, 0, 1)
+    step_on(3, 1, 0, 1)
     small_add(1, "y")
-    small_copy(2, "x").start()
-    final.take(1, 1)
-    final.send(2, 1)
-    small_add(2, "x")
     last = [wire.copy(small_tot, small_from.at[2 + hop], small_base + 2 + hop, place.along(hop)[0]) for hop in range(1, count)]
     for copy in last:
         copy.start()
-    for chunk in range(2):
-        final.take(2, chunk)
-    final.send_last()
+    for part in range(1, 4):
+        for chunk in range(2):
+            reduces[part].take(2, chunk)
+        reduces[part].send_last()
     for copy in last:
-        copy.wait_recv()
+        copy.wait()
     ordered = jnp.zeros(small_tot.shape, jnp.float32)
     for z in range(count):
         term = small_tot[...]
         for hop in range(1, count):
             term = jnp.where(lax.rem(place.z + count - hop, count) == z, small_from[2 + hop], term)
         ordered += term
-    small_sum[...] = ordered
+    small_tot[...] = ordered
+    small_copy(2, "x").start()
+    for part, ref in enumerate((g_up, g_down, g_out)):
+        ref[...] = reduces[part].result()
+    small_add(2, "x")
+    small_sum[...] = small_tot[...]
     mine = final.result()
     for c in range(3):
         g_qkv[c] = mine[:, c * quarter : (c + 1) * quarter]
 
     def land(tile, _):
-        forward_rows(outs, out_base, tile).wait()
+        forward_rows(outs, out_base, tile).wait_recv()
         forward_rows(grads_x, gx_base, tile).wait()
+        keep_rows(grads_x, 16, tile).wait()
         return 0
 
     for gather in gathers:
@@ -775,10 +784,8 @@
         copy.wait_send()
     for axis in "yxc":
         tiny.step(axis).wait_send()
-    for reduce in (*reduces, final):
+    for reduce in reduces:
         reduce.drain()
-    for copy in last:
-        copy.wait_send()
     lax.fori_loop(0, tiles, land, 0)
 
 
@@ -790,8 +797,9 @@
     bf, f32 = jnp.bfloat16, jnp.float32
     V = pltpu.VMEM
     half = (2, slots, width // 2)
+    turned = V((width, slots), bf)
     any_space = pl.BlockSpec(memory_space=pl.ANY)
-    sems = 4 * GATHER_SEMS + SMALL_SEMS + 3 * REDUCE_SEMS + LAST_SEMS + 16 + 8
+    sems = 4 * GATHER_SEMS + SMALL_SEMS + 4 * REDUCE_SEMS + 16 + 8
     out_shape = [
         jax.ShapeDtypeStruct((2, slots, width), bf),
         jax.ShapeDtypeStruct((2, slots, width), bf),
@@ -800,36 +808,33 @@
         jax.ShapeDtypeStruct((rows, quarter), f32),
         jax.ShapeDtypeStruct((3, rows, quarter), f32),
         jax.ShapeDtypeStruct((16, width), f32),
+        jax.ShapeDtypeStruct((slots // TILE, 2, width // 128, slots, TILE), bf),
     ]
     sizes = (columns, columns, quarter, 3 * quarter)
     fulls = [V((2, count, 2, 2, rows, size), bf) for size in sizes]
     scratch = [
-        *fulls, V((2, count, 2, 2, 16, width), bf),
+        *fulls, V((5, 16, width), bf), V((count + 2, 16, width), bf),
         V((slots, width), bf), V((slots, width), bf), V((8, width), f32), V((2, columns), f32),
         V((8, slots), f32), V((slots, 8), f32), V((8, width), f32), V((2, columns), f32),
-        V((width, slots), bf), V(half, bf), V(half, bf), V(half, bf), V((TILE, slots), f32), V(half, bf),
-        V((2, 4, slots), f32), V((width, slots), bf), V((width, slots), bf), V((width, slots), bf),
-        V((2, slots, columns), bf), V((2, slots, columns), bf), V(half, bf), V((2, 4, slots), f32),
-        V((slots, width), f32), V(half, f32), V(half, bf), V(half, bf), V(half, bf), *fulls,
+        turned, turned, V(half, bf), turned, V(half, bf), V((width // 64, 80, slots), bf), V((slots, TILE), f32),
+        turned, V((width // 64, 1, slots), f32), V((2, width // 128, slots, TILE), bf), turned, turned, turned,
+        V((2, slots, columns), bf), V((2, slots, columns), bf), turned, V((width // 64, 1, slots), f32),
+        V((slots, width), f32), V((width, slots), f32), V((width, slots), f32), V((slots, width), bf), *fulls,
     ]
-    for size in sizes[:3]:
+    for size in sizes:
         scratch += [
-            V((2, count, 2, rows, size), bf),
-            V((count, 2, rows // 2, size), bf), V((2, count, rows // 2, size), bf),
-            V((count, rows // 2, size), bf), V((count, rows // 2, size), bf),
-            V((count - 1, rows, size), bf),
+            V((2, count, 2, rows, size), bf), V((2, count, rows, size), bf),
+            V((2, count - 1, rows, size), bf), V((rows, size), bf),
         ]
     scratch += [
-        V((2, count, 2, rows, 3 * quarter), bf), V((2, count, rows, 3 * quarter), bf),
-        V((2, count - 1, rows, 3 * quarter), bf), V((rows, 3 * quarter), bf),
         V((count + 2, 16, width), f32), V((16, width), f32),
-        pltpu.SemaphoreType.DMA((8,)), pltpu.SemaphoreType.DMA((sems,)), pltpu.SemaphoreType.DMA((sems,)),
+        pltpu.SemaphoreType.DMA((20,)), pltpu.SemaphoreType.DMA((sems,)), pltpu.SemaphoreType.DMA((sems,)),
     ]
     return pl.pallas_call(
         whole_kernel,
         out_shape=out_shape,
         in_specs=[any_space] * 2 + [FULL] * 2 + [any_space] * 4 + [FULL] * 5,
-        out_specs=[FULL] * 7,
+        out_specs=[any_space] * 2 + [FULL] * 5 + [any_space],
         scratch_shapes=scratch,
         compiler_params=pltpu.CompilerParams(
             vmem_limit_bytes=67043328, collective_id=0, has_side_effects=True
@@ -851,6 +856,7 @@
 
 
 def finish(parts, qv_shape, up_shape, pair_shape):
+    parts = parts[:7]
     out, grad_x = parts[0], parts[1]
     block = pl.BlockSpec((1, 512, out.shape[2]), lambda step: (step // 2, step % 2, 0))
     fixed = lambda shape: pl.BlockSpec(shape, lambda step: (0,) * len(shape))

time: 140 us -> 134 us (0.957)
  Pallas kernels: 139 us -> 133 us
    pallas_call x1, Pallas kernels: 133 us -> 127 us  [whole(): pl.pallas_call(whole_kernel, out_shape=out_shape, in_specs=[any_space] *...]
where the time goes in v5:
time: 134 us
  Pallas kernels  133 us (99%)
    pallas_call x1, Pallas kernels, whole(): pl.pallas_call(whole_kernel, out_shape=out_shape, in_specs=[any_space] *...  127 us
    pallas_call x1, Pallas kernels, finish(): pl.pallas_call(finish_kernel, grid=(2 * out.shape[1] // 512,), out_shape=...  6.48 us

profile of v5, /device:TPU:0, one launch (start us, length us, event | category | flops | bytes accessed | tf_op | source)
XLA Modules:
  0.0 134.2 jit_solution(14045455240232869132)
XLA Ops:
  0.6 126.9 %shard_map.212 = (bf16[2,1024,512]{2,1,0:T(8,128)(2,1)}, bf16[2,1024,512]{2,1,0:T(8,128)(2,1)}, f32[32,1024]{1,0:T(8,128)}, f32[32,1024]{1,0:T(8,128)}, f32[32,2...) custom-call(bf16[2,1024,512]{2,1,0:T(8,128)(2,1)} %acts.1, ...), custom_call_target="tpu_custom_call" | custom-call | tf_op jit(solution)/shard_map/pallas_call | solution.py:833
  127.6 6.5 %shard_map.213 = (f32[2,1024,512]{2,1,0:T(8,128)}, f32[2,1024,512]{2,1,0:T(8,128)}, f32[3,32,256]{2,1,0:T(8,128)}, f32[32,256]{1,0:T(8,128)}, f32[32,1024]{1,0:T...) custom-call(bf16[2,1024,512]{2,1,0:T(8,128)(2,1)} %get-tuple-element, ...), custom_call_target="tpu_custom_call" | custom-call | tf_op jit(solution)/shard_map/pallas_call | solution.py:866
